TPU v7x, 32 devices: a whole 2x2x4 slice. The times are simulated.
32 devices in a mesh: loc: 16 (over z, x, core), yr: 2 (over y).
Axes of the slice: x: 2, y: 2, z: 4, core: 2. Of those that a mesh axis runs over, the one named last changes fastest.
Arguments:
- noise: bfloat16 [2, 111, 512, 1024], P(None, None, ('yr', 'loc')), parts along dimension 2, may hold values from -6 to 6
- loc_factor: bfloat16 [1024, 1024], P('loc'), as said below
- age_factor: bfloat16 [111, 111], replicated, as said below
- mean_rate: float32 [4, 111, 1024], P('yr'), parts along dimension 0, may hold values from -7 to -2
- population: float32 [4, 111, 1024], P('yr'), parts along dimension 0, may hold values from 0.1 to 10
- region_of: int32 [1024, 1], replicated, may hold values from 0 to 63
Outputs:
- log_rates: bfloat16 [2, 111, 1024, 512], P(None, None, 'loc', 'yr'), parts along dimension 3
- loc_survival: float32 [2, 1024, 512], P(None, 'loc', 'yr'), parts along dimension 2
- region_survival: float32 [2, 64, 512], P(None, 'loc', 'yr'), parts along dimension 2
There are 2 independent parts, one for each index of `yr`. A program takes and returns all parts, laid end to end along the dimension named above; an argument that names none is the same for every part. Nothing has to cross between parts.
Inputs may be any that keep to these rules, and one draw needn't show every extreme that they name: `region_of`: every region holds at least one location. `loc_factor`: lower triangular with a positive diagonal. `age_factor`: lower triangular with a positive diagonal.
All inputs are finite; a program needn't handle non-finite values.
Results may differ from a plain program's by a relative error of at most 0.006.
Values may be sent and summed in bfloat16 or wider, within the bound.
No kernel may reach another device: no remote copies, remote signals or barrier semaphores. Data moves between devices by JAX's collectives and lax.ppermute only.
A program may use at most 128 MiB of HBM per device.

v0:
```python
import jax
import jax.numpy as jnp
from jax import lax
from jax.sharding import PartitionSpec as P

REGIONS = 64


def survival(rates):
    hazard = jnp.cumsum(rates, axis=1)
    after = jnp.exp(-hazard)
    total = 0.5 + jnp.sum(after, axis=1) - 0.5 * after[:, -1]
    return total / rates.shape[1]


def shards(noise, loc_factor, age_factor, mean_rate, population, region_of):
    highest = lax.Precision.HIGHEST
    regions_all = REGIONS
    spread = jnp.einsum(
        "sark,lk->sarl",
        noise,
        lax.all_gather(loc_factor, "loc", axis=0, tiled=True),
        preferred_element_type=jnp.float32,
    ).astype(jnp.bfloat16)
    mixed = jnp.einsum("ab,sbrl->sarl", age_factor, spread, preferred_element_type=jnp.float32)
    log_section = (mean_rate[:, :, None, :] + mixed).astype(jnp.bfloat16)
    rates = jnp.exp(log_section.astype(jnp.float32))
    onehot = (region_of == jnp.arange(regions_all, dtype=jnp.int32)[None, :]).astype(jnp.float32)
    totals = jnp.einsum("sal,lg->sag", population, onehot, precision=highest)
    weighted = jnp.einsum(
        "sarl,lg->sarg", population[:, :, None, :] * rates, onehot, precision=highest
    )
    region_section = survival(weighted / totals[:, :, None, :])
    region_moved = lax.all_to_all(region_section, "loc", split_axis=2, concat_axis=1, tiled=True)
    region_survival = jnp.transpose(region_moved, (0, 2, 1))
    turned = jnp.transpose(
        lax.all_to_all(log_section, "loc", split_axis=3, concat_axis=2, tiled=True), (0, 1, 3, 2)
    )
    loc_survival = survival(jnp.exp(turned.astype(jnp.float32)))
    return (turned, loc_survival, region_survival)


def solution(mesh):
    placed = (
        P(None, None, ("yr", "loc"), None),
        P("loc", None),
        P(),
        P("yr", None, None),
        P("yr", None, None),
        P(),
    )
    return jax.shard_map(
        shards,
        mesh=mesh,
        in_specs=placed,
        out_specs=(P(None, None, "loc", "yr"), P(None, "loc", "yr"), P(None, "loc", "yr")),
        check_vma=False,
    )
```

profile of v0, /device:TPU:17, one launch (start us, length us, event | category | flops | bytes accessed | tf_op | source)
XLA Modules:
  0.0 370.0 jit_solution(1363313943726732951)
XLA Ops:
  7.2 0.0 copy-start
  7.2 0.0 all-gather.2.cloned.1.call-start
  7.2 0.7 all-gather.2.cloned.1.call-update
  7.9 1.5 copy.50
  9.4 1.5 copy.56
  10.9 2.0 convolution_bitcast_fusion
  12.9 0.0 copy-start.2
  12.9 38.4 %all-gather.2.cloned.1.call-done = bf16[1024,1024]{1,0:T(8,128)(2,1)} async-done(((bf16[64,1024]{1,0:T(8,128)(2,1)}), bf16[1024,1024]{1,0:T(8,128)(2,1)}) %all-gather.2.cloned.1.call-update) | async-done | bytes 2097168 | tf_op jit(solution)/shard_map/all_gather | solution.py:22
  51.4 0.0 copy-done
  51.4 21.3 %fusion = bf16[2,111,16,1024]{3,1,2,0:T(8,128)(2,1)} fusion(f32[2,111,1024]{2,1,0:T(8,128)S(1)} %copy.50, bf16[2,111,16,1024]{3,2,1,0:T(8,128)(2,1)} %param.6, bf16[1024,1024]{1,0:T(8,128)(2,1)} %all-gather.2.cloned.1.call-done, bf16[111,111]{1,0:T(8,128)(2,1)S(1)} %copy-done), kind=kOutput, calls=%fused_computation.1 | convolution fusion | flops 8267464704 | bytes 17580098 | tf_op jit(solution)/shard_map/ab,sbrl->sarl/dot_general | solution.py:25
  72.7 0.0 copy-done.2
  72.7 12.1 %fusion.25 = f32[2,111,16,64]{1,3,2,0:T(8,128)S(1)} fusion(bf16[2,111,16,1024]{3,1,2,0:T(8,128)(2,1)} %fusion, f32[2,111,1024]{2,1,0:T(8,128)S(1)} %copy.56, f32[2,111,64]{1,2,0:T(8,128)S(1)} %convolution_bitcast_fusion, s32[1024]{0:T(1024)S(1)} %bitcast.62), kind=kOutput, calls=%fused_computation.18 | convolution fusion | flops 2800973824 | bytes 9154048 | tf_op jit(solution)/shard_map/sarl,lg->sarg/dot_general | solution.py:30
  84.7 0.9 copy.58
  85.6 36.4 %fusion.44 = f32[2,111,16,64]{3,2,1,0:T(8,128)S(1)} fusion(f32[2,111,16,64]{3,2,1,0:T(8,128)S(1)} %copy.58), kind=kOutput, calls=%fused_computation.36 | output fusion | flops 25006080 | bytes 1818624 | tf_op jit(solution)/shard_map/jit(cumsum)/reduce_window_sum | solution.py:10
  122.0 0.2 fusion.42
  122.3 0.1 copy.59
  122.4 0.7 reshape.17
  123.1 5.5 %all-to-all-start.1 = ((f32[16,1,128]{2,1,0:T(1,128)}), f32[16,1,128]{2,1,0:T(1,128)S(1)}, u32[]{:S(2)}, u32[]{:S(2)}) async-start(f32[16,1,128]{2,1,0:T(1,128)} %reshape.17), calls=%async_computation.1 | async-start | bytes 16384 | tf_op jit(solution)/shard_map/all_to_all | solution.py:34
  128.6 12.3 %copy.52 = bf16[2,111,16,1024]{1,2,0,3:T(8,128)(2,1)} copy(bf16[2,111,16,1024]{3,1,2,0:T(8,128)(2,1)} %fusion) | data formatting | bytes 14548992 | tf_op jit(solution)/shard_map/convert_element_type | solution.py:26
  141.0 0.0 all-to-all-done.1
  141.0 6.0 %all-to-all-start = ((bf16[2,111,16,1024]{1,2,0,3:T(8,128)(2,1)}), bf16[2,111,16,1024]{1,2,0,3:T(8,128)(2,1)}, u32[]{:S(2)}, u32[]{:S(2)}) async-start(bf16[2,111,16,1024]{1,2,0,3:T(8,128)(2,1)} %copy.52), calls=%async_computation | async-start | bytes 16777216 | tf_op jit(solution)/shard_map/all_to_all | solution.py:37
  147.0 0.5 broadcast.27
  147.5 0.7 reduce
  148.2 0.1 reshape.18
  148.3 0.7 all_to_all.33
  149.0 180.0 %all-to-all-done = bf16[2,111,16,1024]{1,2,0,3:T(8,128)(2,1)} async-done(((bf16[2,111,16,1024]{1,2,0,3:T(8,128)(2,1)}), bf16[2,111,16,1024]{1,2,0,3:T(8,128)(2,1)}, u32[]{:S(2)}, u32[]{:S(2)}) %all-to-all-start) | async-done | bytes 7274528 | tf_op jit(solution)/shard_map/all_to_all | solution.py:37
  329.1 9.8 %copy.54 = bf16[2,111,16,16,64]{1,4,3,2,0:T(8,128)(2,1)} copy(bf16[2,111,16,16,64]{1,3,0,4,2:T(8,128)(2,1)} %bitcast.7) | data formatting | bytes 14548992 | tf_op jit(solution)/shard_map/all_to_all | solution.py:37
  338.9 13.5 %copy.55 = bf16[2,111,256,64]{2,3,1,0:T(8,128)(2,1)} copy(bf16[2,111,256,64]{1,3,2,0:T(8,128)(2,1)} %bitcast.54) | data formatting | bytes 14548992 | tf_op jit(solution)/shard_map/all_to_all | solution.py:37
  352.4 0.0 copy-start.1
  352.4 9.1 %fusion.43 = (f32[2,64,256]{2,1,0:T(8,128)S(1)}, f32[2,111,64,256]{3,2,1,0:T(8,128)}) fusion(bf16[2,111,64,256]{3,2,1,0:T(8,128)(2,1)} %bitcast.55), kind=kOutput, calls=%fused_computation.35 | output fusion | flops 410976256 | bytes 21954560 | tf_op jit(solution)/shard_map/jit(cumsum)/reduce_window_sum | solution.py:10
  361.6 1.6 fusion.34
  363.1 0.0 copy-done.1
  (3 shorter events, 0.0 us)
Async XLA Ops:
  7.2 44.2 %copy-start = (bf16[111,111]{1,0:T(8,128)(2,1)S(1)}, bf16[111,111]{1,0:T(8,128)(2,1)}, u32[]{:S(2)}) copy-start(bf16[111,111]{1,0:T(8,128)(2,1)} %param.8) | copy-start | bytes 73930
  7.2 44.2 %all-gather.2.cloned.1.call-start = ((), (), s32[]{:S(2)}) async-start(), calls=%async_computation.2 | async-start | bytes 2228224 | tf_op jit(solution)/shard_map/all_gather | solution.py:22
  12.9 59.8 %copy-start.2 = (s32[1024,1]{0,1:T(1,128)S(1)}, s32[1024,1]{0,1:T(1,128)}, u32[]{:S(2)}) copy-start(s32[1024,1]{0,1:T(1,128)} %param.11) | copy-start | bytes 12292
  123.1 17.9 %all-to-all-start.1 = ((f32[16,1,128]{2,1,0:T(1,128)}), f32[16,1,128]{2,1,0:T(1,128)S(1)}, u32[]{:S(2)}, u32[]{:S(2)}) async-start(f32[16,1,128]{2,1,0:T(1,128)} %reshape.17), calls=%async_computation.1 | async-start | bytes 16384 | tf_op jit(solution)/shard_map/all_to_all | solution.py:34
  141.0 188.1 %all-to-all-start = ((bf16[2,111,16,1024]{1,2,0,3:T(8,128)(2,1)}), bf16[2,111,16,1024]{1,2,0,3:T(8,128)(2,1)}, u32[]{:S(2)}, u32[]{:S(2)}) async-start(bf16[2,111,16,1024]{1,2,0,3:T(8,128)(2,1)} %copy.52), calls=%async_computation | async-start | bytes 16777216 | tf_op jit(solution)/shard_map/all_to_all | solution.py:37
  352.4 10.7 %copy-start.1 = (bf16[111,111]{1,0:T(8,128)(2,1)S(1)}, bf16[111,111]{1,0:T(8,128)(2,1)}, u32[]{:S(2)}) copy-start(bf16[111,111]{1,0:T(8,128)(2,1)} %param.8) | copy-start | bytes 73930
Sparse Core Ops, SparseCore 0:
  10.2 41.1 all-gather.1
where the time goes:
time: 371 us; the launch traced here: 370 us
  waiting for transfers between devices  219 us (59%)
  other arithmetic  48 us (13%)
  local copies, waits for them, and re-layouts  41.7 us (11%)
  matrix products  35.4 us (10%)
  between operations  14.1 us (4%)
  starting transfers between devices  11.6 us (3%)
    all_to_all x1, waiting for transfers between devices, shards(): lax.all_to_all(log_section, 'loc', split_axis=3, concat_axis=2, tiled=True)  180 us
    another operation x2, other arithmetic, survival(): hazard = jnp.cumsum(rates, axis=1)  45.5 us
    all_gather x1, waiting for transfers between devices, shards(): lax.all_gather(loc_factor, 'loc', axis=0, tiled=True)  38.4 us
    all_to_all x2, local copies, waits for them, and re-layouts, shards(): lax.all_to_all(log_section, 'loc', split_axis=3, concat_axis=2, tiled=True)  23.4 us
    dot_general x1, matrix products, shards(): jnp.einsum('ab,sbrl->sarl', age_factor, spread, preferred_element_type=jn...  21.3 us
    convert_element_type x1, local copies, waits for them, and re-layouts, shards(): log_section = (mean_rate[:, :, None, :] + mixed).astype(jnp.bfloat16)  12.3 us
    dot_general x1, matrix products, shards(): jnp.einsum('sarl,lg->sarg', population[:, :, None, :] * rates, onehot, pr...  12.1 us
  transfers between devices with their start and end apart: 3, of which 2 were waited for; matrix products, arithmetic and copies ran while one was open for 5% of the time, Pallas kernels for 0%

commit v1 on v0

--- a/solution.py
+++ b/solution.py
@@ -1,9 +1,17 @@
+import functools
+
 import jax
 import jax.numpy as jnp
 from jax import lax
+from jax.experimental import pallas as pl
+from jax.experimental.pallas import tpu as pltpu
 from jax.sharding import PartitionSpec as P
 
 REGIONS = 64
+LANES = 128
+HALF = 64
+NT = (((1,), (1,)), ((), ()))
+CHUNKS = ((8, 12, 4, 0), (10, 14, 6, 2), (9, 13, 5, 1), (11, 15, 7, 3))
 
 
 def survival(rates):
@@ -13,9 +21,8 @@
     return total / rates.shape[1]
 
 
-def shards(noise, loc_factor, age_factor, mean_rate, population, region_of):
+def shards_any(noise, loc_factor, age_factor, mean_rate, population, region_of):
     highest = lax.Precision.HIGHEST
-    regions_all = REGIONS
     spread = jnp.einsum(
         "sark,lk->sarl",
         noise,
@@ -25,7 +32,7 @@
     mixed = jnp.einsum("ab,sbrl->sarl", age_factor, spread, preferred_element_type=jnp.float32)
     log_section = (mean_rate[:, :, None, :] + mixed).astype(jnp.bfloat16)
     rates = jnp.exp(log_section.astype(jnp.float32))
-    onehot = (region_of == jnp.arange(regions_all, dtype=jnp.int32)[None, :]).astype(jnp.float32)
+    onehot = (region_of == jnp.arange(REGIONS, dtype=jnp.int32)[None, :]).astype(jnp.float32)
     totals = jnp.einsum("sal,lg->sag", population, onehot, precision=highest)
     weighted = jnp.einsum(
         "sarl,lg->sarg", population[:, :, None, :] * rates, onehot, precision=highest
@@ -38,6 +45,381 @@
     )
     loc_survival = survival(jnp.exp(turned.astype(jnp.float32)))
     return (turned, loc_survival, region_survival)
+
+
+def split_bf16(x):
+    hi = x.astype(jnp.bfloat16)
+    return hi, (x - hi.astype(jnp.float32)).astype(jnp.bfloat16)
+
+
+def age_mix_kernel(age_ref, x_ref, o_ref, wide_ref):
+    ages = age_ref.shape[0]
+    rows = x_ref.shape[1]
+    step = 256
+
+    @pl.when(jnp.logical_and(pl.program_id(0) == 0, pl.program_id(1) == 0))
+    def _():
+        pick = lax.broadcasted_iota(jnp.int32, (rows, ages), 0) >> 4
+        pick = (pick == lax.broadcasted_iota(jnp.int32, (rows, ages), 1)).astype(jnp.bfloat16)
+        tall = jnp.dot(pick, age_ref[...], preferred_element_type=jnp.float32).astype(jnp.bfloat16)
+        spread = lax.broadcasted_iota(jnp.int32, (ages, rows), 1) >> 4
+        spread = (spread == lax.broadcasted_iota(jnp.int32, (ages, rows), 0)).astype(jnp.bfloat16)
+        for lo in range(0, rows, step):
+            hi = min(lo + step, rows)
+            both = jnp.dot(tall[lo:hi], spread[:, :hi], preferred_element_type=jnp.float32)
+            same = (lax.broadcasted_iota(jnp.int32, both.shape, 0) & 15) == (
+                lax.broadcasted_iota(jnp.int32, both.shape, 1) & 15
+            )
+            wide_ref[lo:hi, :hi] = jnp.where(same, both, 0.0).astype(jnp.bfloat16)
+
+    for lo in range(0, rows, step):
+        hi = min(lo + step, rows)
+        o_ref[0, lo:hi, :] = jnp.dot(
+            wide_ref[lo:hi, :hi], x_ref[0, :hi, :], preferred_element_type=jnp.float32
+        ).astype(jnp.bfloat16)
+
+
+def age_mix(age_factor, noise):
+    sexes, rows, cols = noise.shape
+    ages = age_factor.shape[0]
+    width = 256
+    return pl.pallas_call(
+        age_mix_kernel,
+        out_shape=jax.ShapeDtypeStruct(noise.shape, jnp.bfloat16),
+        grid=(sexes, cols // width),
+        in_specs=[
+            pl.BlockSpec((ages, ages), lambda s, k: (0, 0)),
+            pl.BlockSpec((1, rows, width), lambda s, k: (s, 0, k)),
+        ],
+        out_specs=pl.BlockSpec((1, rows, width), lambda s, k: (s, 0, k)),
+        scratch_shapes=[pltpu.VMEM((rows, rows), jnp.bfloat16)],
+        compiler_params=pltpu.CompilerParams(vmem_limit_bytes=40 << 20),
+        cost_estimate=pl.CostEstimate(
+            flops=rows * rows * cols * sexes, bytes_accessed=4 * sexes * rows * cols, transcendentals=0
+        ),
+        name="age_mix",
+    )(age_factor, noise)
+
+
+def merge_pair(pair, odd_device, swapped):
+    axis = pair.ndim - 1
+    turned = pltpu.roll(pair, HALF, axis)
+    first = jnp.where(odd_device, turned, pair)
+    second = jnp.where(odd_device, pair, turned)
+    low = lax.broadcasted_iota(jnp.int32, pair.shape[:-2] + (1, LANES), axis) < HALF
+    s = 1 if swapped else 0
+    return jnp.where(low, first[..., s : s + 1, :], second[..., 1 - s : 2 - s, :])
+
+
+def loc_mix_kernel(e_ref, x_ref, *refs):
+    factors, means, outs = refs[:4], refs[4:8], refs[8:]
+    l0, l1, l2, l3 = [f[...] for f in factors]
+    r0 = lax.dot_general(
+        x_ref[0], jnp.concatenate([l0, l1, l2, l3], 0), NT, preferred_element_type=jnp.float32
+    )
+    r1 = lax.dot_general(
+        x_ref[1], jnp.concatenate([l1, l0, l3, l2], 0), NT, preferred_element_type=jnp.float32
+    )
+    ages, rows, _ = outs[0].shape
+    low = lax.broadcasted_iota(jnp.int32, (1, LANES), 1) < HALF
+    for q in range(4):
+        g = (q // 2) * LANES
+        a, b = r0[:, g : g + LANES], r1[:, g : g + LANES]
+        v = jnp.where(low, a, b) if q % 2 == 0 else jnp.where(low, b, a)
+        m = merge_pair(means[q][...], (e_ref[q] & 1) == 1, q % 2 == 1)
+        outs[q][...] = (v.reshape(ages, rows, LANES) + m).astype(jnp.bfloat16)
+
+
+def loc_mix(dests, mixed, factors, mean_t):
+    sexes, rows, cols = mixed.shape
+    ages = mean_t.shape[0]
+    steps = 3
+    block = ages // steps
+    per_age = rows // ages
+    msg = jax.ShapeDtypeStruct((ages, per_age, LANES), jnp.bfloat16)
+
+    def mean_spec(q):
+        return pl.BlockSpec((block, sexes, LANES), lambda i, e: (i, 0, e[q] // 2))
+
+    return pl.pallas_call(
+        loc_mix_kernel,
+        out_shape=[msg] * 4,
+        grid_spec=pltpu.PrefetchScalarGridSpec(
+            num_scalar_prefetch=1,
+            grid=(steps,),
+            in_specs=[pl.BlockSpec((sexes, block * per_age, cols), lambda i, e: (0, i, 0))]
+            + [pl.BlockSpec((HALF, cols), lambda i, e: (0, 0))] * 4
+            + [mean_spec(q) for q in range(4)],
+            out_specs=[pl.BlockSpec((block, per_age, LANES), lambda i, e: (i, 0, 0))] * 4,
+        ),
+        compiler_params=pltpu.CompilerParams(vmem_limit_bytes=40 << 20),
+        cost_estimate=pl.CostEstimate(
+            flops=2 * sexes * rows * cols * 256,
+            bytes_accessed=2 * sexes * rows * cols + 8 * rows * LANES,
+            transcendentals=0,
+        ),
+        name="loc_mix",
+    )(dests, mixed, *factors, *([mean_t] * 4))
+
+
+def survive_kernel(first, last, e_ref, *refs):
+    xs, pops, regs = refs[:4], refs[4:8], refs[8:12]
+    pos = 12
+    if not first:
+        wsum_in, psum_in = refs[pos : pos + 2]
+        pos += 2
+    locs = refs[pos : pos + 4]
+    pos += 4
+    if last:
+        region_ref = refs[pos]
+        pos += 1
+    wsum_ref, psum_ref = refs[pos : pos + 2]
+    hi_ref, lo_ref, pop_ref = refs[pos + 2 : pos + 5]
+    ages, rows, _ = xs[0].shape
+    odd = [(e_ref[q] & 1) == 1 for q in range(4)]
+    zero = jnp.zeros((rows, LANES), jnp.float32)
+
+    def age_step(a, carry):
+        hazards, totals = carry
+        new_h, new_t = [], []
+        at = pl.ds(pl.multiple_of(a * rows, rows), rows)
+        for q in range(4):
+            lanes = slice(q * LANES, (q + 1) * LANES)
+            rate = jnp.exp(xs[q][a].astype(jnp.float32))
+            h = hazards[q] + rate
+            new_h.append(h)
+            new_t.append(totals[q] + jnp.exp(-h))
+            pop = merge_pair(pops[q][a], odd[q], q % 2 == 1)
+            pop_ref[q, pl.ds(a, 1), :] = pop
+            hi, lo = split_bf16(rate * pop)
+            hi_ref[at, lanes] = hi
+            lo_ref[at, lanes] = lo
+        return tuple(new_h), tuple(new_t)
+
+    hazards, totals = lax.fori_loop(0, ages, age_step, ((zero,) * 4, (zero,) * 4))
+    for q in range(4):
+        out = (totals[q] + (0.5 - 0.5 * jnp.exp(-hazards[q]))) * (1.0 / ages)
+        if q % 2 == 1:
+            out = pltpu.roll(out, HALF, 1)
+        locs[q][...] = out
+
+    lane = lax.broadcasted_iota(jnp.int32, (1, LANES), 1)
+    low = lane < HALF
+    onehots = []
+    for q in range(4):
+        pair = regs[q][...]
+        turned = pltpu.roll(pair, HALF, 1)
+        mine = jnp.where(low, jnp.where(odd[q], turned, pair), jnp.where(odd[q], pair, turned))
+        upper = low if q % 2 == 1 else jnp.logical_not(low)
+        target = mine + jnp.where(upper, REGIONS, 0)
+        region = lax.broadcasted_iota(jnp.int32, (LANES, LANES), 0)
+        onehots.append(jnp.where(region == target, 1.0, 0.0).astype(jnp.bfloat16))
+    onehot = jnp.concatenate(onehots, 1)
+
+    def regions(x):
+        return lax.dot_general(x, onehot, NT, preferred_element_type=jnp.float32)
+
+    pop_hi, pop_lo = split_bf16(jnp.concatenate([pop_ref[q] for q in range(4)], 1))
+    wsum = regions(hi_ref[...]) + regions(lo_ref[...])
+    psum = regions(pop_hi) + regions(pop_lo)
+    if not first:
+        wsum = wsum + wsum_in[...]
+        psum = psum + psum_in[...]
+    wsum_ref[...] = wsum
+    psum_ref[...] = psum
+    if last:
+
+        def region_step(a, carry):
+            h, t = carry
+            at = pl.ds(pl.multiple_of(a * rows, rows), rows)
+            h = h + wsum_ref[at, :] / psum_ref[pl.ds(a, 1), :]
+            return h, t + jnp.exp(-h)
+
+        h, t = lax.fori_loop(0, ages, region_step, (zero, zero))
+        region_ref[...] = (t + (0.5 - 0.5 * jnp.exp(-h))) * (1.0 / ages)
+
+
+def survive(dests, messages, pop_t, region_row, sums, last):
+    ages, rows, _ = messages[0].shape
+    sexes = pop_t.shape[1]
+    first = sums is None
+    f32 = jnp.float32
+    loc = jax.ShapeDtypeStruct((rows, LANES), f32)
+    wsum = jax.ShapeDtypeStruct((ages * rows, LANES), f32)
+    psum = jax.ShapeDtypeStruct((ages, LANES), f32)
+    whole = lambda *shape: pl.BlockSpec(shape, lambda i, e: (0,) * len(shape))
+
+    def pop_spec(q):
+        return pl.BlockSpec((ages, sexes, LANES), lambda i, e: (0, 0, e[q] // 2))
+
+    def region_spec(q):
+        return pl.BlockSpec((1, LANES), lambda i, e: (0, e[q] // 2))
+
+    in_specs = [whole(ages, rows, LANES)] * 4
+    in_specs += [pop_spec(q) for q in range(4)] + [region_spec(q) for q in range(4)]
+    args = list(messages) + [pop_t] * 4 + [region_row] * 4
+    sum_specs = [whole(ages * rows, LANES), whole(ages, LANES)]
+    outs, out_specs = [loc] * 4, [whole(rows, LANES)] * 4
+    if not first:
+        in_specs += sum_specs
+        args += list(sums)
+    if last:
+        outs.append(loc)
+        out_specs.append(whole(rows, LANES))
+    scratch = [
+        pltpu.VMEM((ages * rows, 4 * LANES), jnp.bfloat16),
+        pltpu.VMEM((ages * rows, 4 * LANES), jnp.bfloat16),
+        pltpu.VMEM((4, ages, LANES), f32),
+    ]
+    if last:
+        scratch = [pltpu.VMEM(wsum.shape, f32), pltpu.VMEM(psum.shape, f32)] + scratch
+    else:
+        outs += [wsum, psum]
+        out_specs += sum_specs
+    return pl.pallas_call(
+        functools.partial(survive_kernel, first, last),
+        out_shape=outs,
+        grid_spec=pltpu.PrefetchScalarGridSpec(
+            num_scalar_prefetch=1,
+            grid=(1,),
+            in_specs=in_specs,
+            out_specs=out_specs,
+            scratch_shapes=scratch,
+        ),
+        compiler_params=pltpu.CompilerParams(vmem_limit_bytes=40 << 20),
+        cost_estimate=pl.CostEstimate(
+            flops=60 * 4 * ages * rows * LANES,
+            bytes_accessed=16 * ages * rows * LANES,
+            transcendentals=8 * ages * rows * LANES,
+        ),
+        name="survive",
+    )(dests, *args)
+
+
+def turn_kernel(near, d_ref, *refs):
+    xs, out_ref, order_ref = refs[:8], refs[-2], refs[-1]
+    d = d_ref[0]
+    ages = xs[0].shape[0]
+    for m in range(8):
+        order_ref[(d & 7) ^ m] = xs[m][...]
+    eye = (
+        lax.broadcasted_iota(jnp.int32, (LANES, LANES), 0)
+        == lax.broadcasted_iota(jnp.int32, (LANES, LANES), 1)
+    ).astype(jnp.bfloat16)
+    upper = (lax.broadcasted_iota(jnp.int32, (HALF, LANES), 1) >= HALF).astype(jnp.int32)
+    swapped = (upper ^ ((d >> 2) & 1) ^ (1 if near else 0)) == 1
+    for a in range(ages):
+        tile = order_ref[:, a].reshape(LANES, LANES)
+        t = lax.dot_general(eye, tile, NT, preferred_element_type=jnp.float32)
+        top, bottom = t[:HALF], t[HALF:]
+        out_ref[0, a] = jnp.where(swapped, bottom, top).astype(jnp.bfloat16)
+        out_ref[1, a] = jnp.where(swapped, top, bottom).astype(jnp.bfloat16)
+
+
+def turn(device, messages, out_shape, previous):
+    near = previous is None
+    ages, rows, _ = messages[0].shape
+    steps = 3
+    block = ages // steps
+    in_specs = [pl.BlockSpec((block, rows, LANES), lambda i, d: (i, 0, 0))] * 8
+    args = list(messages)
+    flip = 0 if near else 1
+    aliases = {}
+    if not near:
+        in_specs.append(pl.BlockSpec(memory_space=pl.ANY))
+        args.append(previous)
+        aliases = {9: 0}
+    return pl.pallas_call(
+        functools.partial(turn_kernel, near),
+        out_shape=out_shape,
+        grid_spec=pltpu.PrefetchScalarGridSpec(
+            num_scalar_prefetch=1,
+            grid=(steps,),
+            in_specs=in_specs,
+            out_specs=pl.BlockSpec((2, block, HALF, LANES), lambda i, d: (0, i, 0, (d[0] // 8) ^ flip)),
+            scratch_shapes=[pltpu.VMEM((8, block, rows, LANES), jnp.bfloat16)],
+        ),
+        input_output_aliases=aliases,
+        compiler_params=pltpu.CompilerParams(vmem_limit_bytes=40 << 20),
+        cost_estimate=pl.CostEstimate(
+            flops=2 * ages * LANES**3, bytes_accessed=32 * ages * rows * LANES, transcendentals=0
+        ),
+        name="turn",
+    )(device, *args)
+
+
+def shards_sixteen(noise, loc_factor, age_factor, mean_rate, population, region_of):
+    sexes, ages, rows, locs = noise.shape
+    devices = lax.axis_size("loc")
+    here = lax.axis_index("loc")
+
+    def swap(x, bits):
+        return lax.ppermute(x, "loc", [(i, i ^ bits) for i in range(devices)])
+
+    mean_t = jnp.transpose(mean_rate, (1, 0, 2))
+    pop_t = jnp.transpose(population, (1, 0, 2))
+    region_row = region_of.reshape(1, locs)
+    dests = [here ^ jnp.array(c, jnp.int32) for c in CHUNKS]
+
+    factors = {0: loc_factor}
+    for bits in (8, 12, 4):
+        factors[bits] = swap(loc_factor, bits)
+    mixed = age_mix(age_factor, noise.reshape(sexes, ages * rows, locs))
+
+    lane0 = jnp.concatenate([factors[b] for b in CHUNKS[0]], 0)
+    lane2 = swap(lane0, 2)
+    lane1 = swap(lane0, 1)
+    lane3 = swap(lane2, 1)
+    local = loc_factor.shape[0]
+    lanes = [[factors[b] for b in CHUNKS[0]]]
+    for whole in (lane2, lane1, lane3):
+        lanes.append([whole[i * local : (i + 1) * local] for i in range(4)])
+
+    sent, got = {}, {}
+    for c, bits in enumerate(CHUNKS):
+        messages = loc_mix(dests[c], mixed, lanes[c], mean_t)
+        for b, m in zip(bits, messages):
+            sent[b] = m
+            got[b] = m if b == 0 else swap(m, b)
+
+    loc_parts, sums = {}, None
+    for c, bits in enumerate(CHUNKS):
+        last = c == len(CHUNKS) - 1
+        out = survive(dests[c], [sent[b] for b in bits], pop_t, region_row, sums, last)
+        for b, o in zip(bits, out[:4]):
+            loc_parts[b] = o
+        if last:
+            region_part = out[4]
+        else:
+            sums = out[4:]
+
+    by_bits = jnp.stack([loc_parts[b] for b in range(devices)])
+    by_device = jnp.take(by_bits, here ^ jnp.arange(devices, dtype=jnp.int32), axis=0)
+    mine = REGIONS // devices
+    region_out = region_part.reshape(rows, sexes, devices, mine)
+    region_out = jnp.transpose(region_out, (2, 1, 3, 0)).reshape(devices, 1, sexes * mine * rows)
+    small = lax.all_to_all(
+        jnp.concatenate([by_device, region_out], axis=1), "loc", split_axis=0, concat_axis=0, tiled=True
+    )
+    loc_survival = jnp.transpose(small[:, :rows].reshape(devices * rows, LANES), (1, 0)).reshape(
+        sexes, local, devices * rows
+    )
+    region_survival = jnp.transpose(
+        small[:, rows].reshape(devices, sexes, mine, rows), (1, 2, 0, 3)
+    ).reshape(sexes, mine, devices * rows)
+
+    shape = jax.ShapeDtypeStruct((sexes, ages, local, devices * rows), jnp.bfloat16)
+    device = here[None]
+    half = turn(device, [got[b] for b in range(8)], shape, None)
+    log_rates = turn(device, [got[b] for b in range(8, 16)], shape, half)
+    return (log_rates, loc_survival, region_survival)
+
+
+def shards(noise, loc_factor, *rest):
+    sixteen = lax.axis_size("loc") == 16 and noise.shape[2] == 16 and noise.shape[1] % 3 == 0
+    if sixteen and noise.shape[0] == 2 and loc_factor.shape == (HALF, 1024):
+        return shards_sixteen(noise, loc_factor, *rest)
+    return shards_any(noise, loc_factor, *rest)
 
 
 def solution(mesh):

time: 371 us -> 240 us (0.65)
  waiting for transfers between devices: 219 us -> 23.4 us
  blocking collectives: 0 us -> 78.7 us
  Pallas kernels: 0 us -> 77 us
  matrix products: 35.4 us -> 0 us
  local copies, waits for them, and re-layouts: 41.7 us -> 6.43 us
  other arithmetic: 48 us -> 15.5 us
  starting transfers between devices: 11.6 us -> 36.4 us
  between operations: 14.1 us -> 1.13 us
    all_to_all x2 -> x0, waiting for transfers between devices: 180 us -> none  [the longest x1 180 us: shards(): lax.all_to_all(log_section, 'loc', split_axis=3, concat_axis=2, tiled=True)]
    all_to_all x0 -> x1, blocking collectives: none -> 78.7 us  [shards_sixteen(): lax.all_to_all(jnp.concatenate([by_device, region_out], axis=1), 'loc', s...]
    pallas_call x0 -> x10, Pallas kernels: none -> 77 us  [the longest x3 35.2 us: survive(): pl.pallas_call(functools.partial(survive_kernel, first, last), out_shape=...]
    another operation x2 -> x0, other arithmetic: 45.5 us -> none  [survival(): hazard = jnp.cumsum(rates, axis=1)]
    all_gather x1 -> x0, waiting for transfers between devices: 38.4 us -> none  [shards(): lax.all_gather(loc_factor, 'loc', axis=0, tiled=True)]
    ppermute x0 -> x21, starting transfers between devices: none -> 36.4 us  [swap(): return lax.ppermute(x, 'loc', [(i, i ^ bits) for i in range(devices)])]
    dot_general x3 -> x0, matrix products: 35.4 us -> none  [the longest x1 21.3 us: shards(): jnp.einsum('ab,sbrl->sarl', age_factor, spread, preferred_element_type=jn...]
    all_to_all x6 -> x0, local copies, waits for them, and re-layouts: 24.6 us -> none  [the longest x2 23.4 us: shards(): lax.all_to_all(log_section, 'loc', split_axis=3, concat_axis=2, tiled=True)]
  transfers between devices with their start and end apart: 3 -> 21, of which waited for: 2 -> 3; matrix products, arithmetic and copies ran while one was open for 5% -> 8% of each run, Pallas kernels for 0% -> 30%
where the time goes in v1:
time: 240 us; the launch traced here: 239 us
  blocking collectives  78.7 us (33%)
  Pallas kernels  77 us (32%)
  starting transfers between devices  36.4 us (15%)
  waiting for transfers between devices  23.4 us (10%)
  other arithmetic  15.5 us (6%)
  local copies, waits for them, and re-layouts  6.43 us (3%)
    all_to_all x1, blocking collectives, shards_sixteen(): lax.all_to_all(jnp.concatenate([by_device, region_out], axis=1), 'loc', s...  78.7 us
    ppermute x21, starting transfers between devices, swap(): return lax.ppermute(x, 'loc', [(i, i ^ bits) for i in range(devices)])  36.4 us
    pallas_call x3, Pallas kernels, survive(): pl.pallas_call(functools.partial(survive_kernel, first, last), out_shape=...  35.2 us
    ppermute x21, waiting for transfers between devices, swap(): return lax.ppermute(x, 'loc', [(i, i ^ bits) for i in range(devices)])  23.4 us
    pallas_call x4, Pallas kernels, loc_mix(): pl.pallas_call(loc_mix_kernel, out_shape=[msg] * 4, grid_spec=pltpu.Prefe...  17.4 us
    pallas_call x1, other arithmetic, survive(): pl.pallas_call(functools.partial(survive_kernel, first, last), out_shape=...  13.4 us
    pallas_call x2, Pallas kernels, turn(): pl.pallas_call(functools.partial(turn_kernel, near), out_shape=out_shape,...  12.3 us
    pallas_call x1, Pallas kernels, age_mix(): pl.pallas_call(age_mix_kernel, out_shape=jax.ShapeDtypeStruct(noise.shape...  12.2 us
  transfers between devices with their start and end apart: 21, of which 3 were waited for; matrix products, arithmetic and copies ran while one was open for 8% of the time, Pallas kernels for 30%

profile of v1, /device:TPU:17, one launch (start us, length us, event | category | flops | bytes accessed | tf_op | source)
XLA Modules:
  0.0 238.6 jit_solution(12071306831561867589)
XLA Ops:
  0.7 2.5 %collective-permute-start.1 = (bf16[64,1024]{1,0:T(8,128)(2,1)}, bf16[64,1024]{1,0:T(8,128)(2,1)S(1)}, u32[]{:S(2)}, u32[]{:S(2)}) collective-permute-start(bf16[64,1024]{1,0:T(8,128)(2,1)} %refs_3_.1), channel_id=1, source_target_pairs={{0,24},{2,26},{4,28},{6,30},{8,16},{10,18},{12,20},{14,22},{16,8},... | collective-permute-start | bytes 393224 | tf_op jit(solution)/shard_map/ppermute | solution.py:357
  3.2 1.1 collective-permute-start.2
  6.2 3.1 %copy-done.9 = bf16[2,111,16,1024]{3,2,1,0:T(8,128)(2,1)S(1)} copy-done((bf16[2,111,16,1024]{3,2,1,0:T(8,128)(2,1)S(1)}, bf16[2,111,16,1024]{3,2,1,0:T(8,128)(2,1)}, u32[]{:S(2)}) %copy-start.9) | copy-done | bytes 7274520
  9.3 0.7 copy-done.10
  10.0 12.2 %age_mix.1.x_ref = bf16[2,1776,1024]{2,1,0:T(8,128)(2,1)S(1)} custom-call(bf16[111,111]{1,0:T(8,128)(2,1)S(1)} %copy-done.10, bf16[2,1776,1024]{2,1,0:T(8,128)(2,1)S(1)} %bitcast.91), custom_call_target="tpu_custom_call" | custom-call | flops 6459752448 | bytes 14548992 | tf_op jit(solution)/shard_map/age_mix/pallas_call | solution.py:86
  22.5 1.3 collective-permute-start.6
  23.8 1.9 collective-permute-start.4
  25.6 4.8 %loc_mix.4 = (bf16[111,16,128]{2,1,0:T(8,128)(2,1)}, bf16[111,16,128]{2,1,0:T(8,128)(2,1)}, bf16[111,16,128]{2,1,0:T(8,128)(2,1)}, bf16[111,16,128]{2,1,0:T(8,128)(2,1)S(1)}) custom-call(s32[4]{0:T(128)S(1)} %broadcast_xor_fusion.3.e_ref, bf16[2,1776,1024]{2,1,0:T(8,128)(2,1)S(1)} %age_mix.1.x_ref, bf16[64,1024]{1,0:T(8,128)(2,1)S(1)} %collective-permute-done.refs_0_, ...), custom_call_target="tpu_custom_call" | custom-call | flops 1862270976 | bytes 9093120 | tf_op jit(solution)/shard_map/loc_mix/pallas_call | solution.py:144
  30.8 3.2 %collective-permute-start.3 = (bf16[111,16,128]{2,1,0:T(8,128)(2,1)}, bf16[111,16,128]{2,1,0:T(8,128)(2,1)}, u32[]{:S(2)}, u32[]{:S(2)}) collective-permute-start(bf16[111,16,128]{2,1,0:T(8,128)(2,1)} %get-tuple-element.42.refs_0_), channel_id=1, source_target_pairs={{0,16},{2,18},{4,20},{6,22},{8,24},{10,26},{12,28},{14,30},{16,0},... | collective-permute-start | bytes 1363976 | tf_op jit(solution)/shard_map/ppermute | solution.py:357
  33.9 12.2 %survive.4 = (f32[16,128]{1,0:T(8,128)S(1)}, f32[16,128]{1,0:T(8,128)S(1)}, f32[16,128]{1,0:T(8,128)S(1)}, f32[16,128]{1,0:T(8,128)S(1)}, f32[1776,128]{1,0:T(8,128)S(1)}, /*index=5*/f32[111,128]{1,0:T(8,128)S(1)}) custom-call(s32[4]{0:T(128)S(1)} %broadcast_xor_fusion.3.e_ref, bf16[111,16,128]{2,1,0:T(8,128)(2,1)} %get-tuple-element.42.refs_0_, ...), custom_call_target="tpu_custom_call" | custom-call | flops 54558720 | bytes 3637248 | tf_op jit(solution)/shard_map/survive/pallas_call | solution.py:279
  46.3 4.7 %loc_mix.6 = (bf16[111,16,128]{2,1,0:T(8,128)(2,1)S(1)}, bf16[111,16,128]{2,1,0:T(8,128)(2,1)S(1)}, bf16[111,16,128]{2,1,0:T(8,128)(2,1)}, bf16[111,16,128]{2,1,0:T(8,128)(2,1)S(1)}) custom-call(s32[4]{0:T(128)S(1)} %broadcast_xor_fusion.1.e_ref, bf16[2,1776,1024]{2,1,0:T(8,128)(2,1)S(1)} %age_mix.1.x_ref, bf16[64,1024]{1,0:T(8,128)(2,1)S(1)} %get-tuple-element.98.refs_0_, ...), custom_call_target="tpu_custom_call" | custom-call | flops 1862270976 | bytes 9093120 | tf_op jit(solution)/shard_map/loc_mix/pallas_call | solution.py:144
  51.2 1.1 collective-permute-start.8
  52.4 4.0 %loc_mix.5 = (bf16[111,16,128]{2,1,0:T(8,128)(2,1)S(1)}, bf16[111,16,128]{2,1,0:T(8,128)(2,1)S(1)}, bf16[111,16,128]{2,1,0:T(8,128)(2,1)S(1)}, bf16[111,16,128]{2,1,0:T(8,128)(2,1)S(1)}) custom-call(s32[4]{0:T(128)S(1)} %broadcast_xor_fusion.2.e_ref, bf16[2,1776,1024]{2,1,0:T(8,128)(2,1)S(1)} %age_mix.1.x_ref, ...), custom_call_target="tpu_custom_call" | custom-call | flops 1862270976 | bytes 9093120 | tf_op jit(solution)/shard_map/loc_mix/pallas_call | solution.py:144
  56.4 11.9 %survive.5 = (f32[16,128]{1,0:T(8,128)S(1)}, f32[16,128]{1,0:T(8,128)S(1)}, f32[16,128]{1,0:T(8,128)S(1)}, f32[16,128]{1,0:T(8,128)S(1)}, f32[1776,128]{1,0:T(8,128)S(1)}, /*index=5*/f32[111,128]{1,0:T(8,128)S(1)}) custom-call(s32[4]{0:T(128)S(1)} %broadcast_xor_fusion.1.e_ref, bf16[111,16,128]{2,1,0:T(8,128)(2,1)S(1)} %get-tuple-element.44.refs_0_, ...), custom_call_target="tpu_custom_call" | custom-call | flops 54558720 | bytes 3637248 | tf_op jit(solution)/shard_map/survive/pallas_call | solution.py:279
  68.2 11.0 %survive.6 = (f32[16,128]{1,0:T(8,128)S(1)}, f32[16,128]{1,0:T(8,128)S(1)}, f32[16,128]{1,0:T(8,128)S(1)}, f32[16,128]{1,0:T(8,128)S(1)}, f32[1776,128]{1,0:T(8,128)S(1)}, /*index=5*/f32[111,128]{1,0:T(8,128)S(1)}) custom-call(s32[4]{0:T(128)S(1)} %broadcast_xor_fusion.2.e_ref, bf16[111,16,128]{2,1,0:T(8,128)(2,1)S(1)} %get-tuple-element.43.refs_0_, ...), custom_call_target="tpu_custom_call" | custom-call | flops 54558720 | bytes 3637248 | tf_op jit(solution)/shard_map/survive/pallas_call | solution.py:279
  79.9 4.0 %loc_mix.7 = (bf16[111,16,128]{2,1,0:T(8,128)(2,1)S(1)}, bf16[111,16,128]{2,1,0:T(8,128)(2,1)S(1)}, bf16[111,16,128]{2,1,0:T(8,128)(2,1)S(1)}, bf16[111,16,128]{2,1,0:T(8,128)(2,1)S(1)}) custom-call(s32[4]{0:T(128)S(1)} %broadcast_xor_fusion.e_ref, bf16[2,1776,1024]{2,1,0:T(8,128)(2,1)S(1)} %age_mix.1.x_ref, bf16[64,1024]{1,0:T(8,128)(2,1)S(1)} %get-tuple-element.94.refs_0_, ...), custom_call_target="tpu_custom_call" | custom-call | flops 1862270976 | bytes 9093120 | tf_op jit(solution)/shard_map/loc_mix/pallas_call | solution.py:144
  83.9 13.4 %survive.7 = (f32[16,16,128]{2,1,0:T(8,128)S(1)}, f32[16,128]{1,0:T(8,128)S(1)}, f32[16,128]{1,0:T(8,128)S(1)}, f32[16,128]{1,0:T(8,128)S(1)}, f32[16,128]{1,0:T(8,128)S(1)}) fusion(f32[16,16,128]{2,1,0:T(8,128)S(1)} %constant_dynamic-update-slice_fusion.17, s32[4]{0:T(128)S(1)} %broadcast_xor_fusion.e_ref, ...), kind=kCustom, calls=%fused_computation.19 | custom fusion | flops 54558720 | bytes 3740160 | tf_op jit(solution)/shard_map/survive/pallas_call | solution.py:279
  98.1 2.1 collective-permute-start.18
  100.3 1.7 collective-permute-start.16
  102.0 0.7 collective-permute-start.20
  103.4 2.5 %collective-permute-start.7 = (bf16[111,16,128]{2,1,0:T(8,128)(2,1)S(1)}, bf16[111,16,128]{2,1,0:T(8,128)(2,1)S(1)}, u32[]{:S(2)}, u32[]{:S(2)}) collective-permute-start(bf16[111,16,128]{2,1,0:T(8,128)(2,1)S(1)} %get-tuple-element.44.refs_0_), channel_id=1, source_target_pairs={{0,20},{2,22},{4,16},{6,18},{8,28},{10,30},{12,24},{14,26},{16,4},... | collective-permute-start | bytes 1363976 | tf_op jit(solution)/shard_map/ppermute | solution.py:357
  105.9 5.5 %collective-permute-done.18.refs_5_ = bf16[111,16,128]{2,1,0:T(8,128)(2,1)} collective-permute-done((bf16[111,16,128]{2,1,0:T(8,128)(2,1)S(1)}, bf16[111,16,128]{2,1,0:T(8,128)(2,1)}, u32[]{:S(2)}, u32[]{:S(2)}) %collective-permute-start.18) | collective-permute-done | bytes 454688 | tf_op jit(solution)/shard_map/ppermute | solution.py:357
  111.5 12.4 %collective-permute-done.12.refs_6_ = bf16[111,16,128]{2,1,0:T(8,128)(2,1)} collective-permute-done((bf16[111,16,128]{2,1,0:T(8,128)(2,1)S(1)}, bf16[111,16,128]{2,1,0:T(8,128)(2,1)}, u32[]{:S(2)}, u32[]{:S(2)}) %collective-permute-start.12) | collective-permute-done | bytes 454688 | tf_op jit(solution)/shard_map/ppermute | solution.py:357
  123.9 1.3 collective-permute-start.5
  125.2 8.3 %collective-permute-start.13 = (bf16[111,16,128]{2,1,0:T(8,128)(2,1)}, bf16[111,16,128]{2,1,0:T(8,128)(2,1)}, u32[]{:S(2)}, u32[]{:S(2)}) collective-permute-start(bf16[111,16,128]{2,1,0:T(8,128)(2,1)} %copy-done.6), channel_id=1, source_target_pairs={{0,30},{2,28},{4,26},{6,24},{8,22},{10,20},{12,18},{14,16},{16,14}... | collective-permute-start | bytes 1363976 | tf_op jit(solution)/shard_map/ppermute | solution.py:357
  133.5 5.3 %collective-permute-done.20.refs_7_ = bf16[111,16,128]{2,1,0:T(8,128)(2,1)} collective-permute-done((bf16[111,16,128]{2,1,0:T(8,128)(2,1)}, bf16[111,16,128]{2,1,0:T(8,128)(2,1)}, u32[]{:S(2)}, u32[]{:S(2)}) %collective-permute-start.20) | collective-permute-done | bytes 454688 | tf_op jit(solution)/shard_map/ppermute | solution.py:357
  138.9 7.1 %collective-permute-start.9 = (bf16[111,16,128]{2,1,0:T(8,128)(2,1)}, bf16[111,16,128]{2,1,0:T(8,128)(2,1)}, u32[]{:S(2)}, u32[]{:S(2)}) collective-permute-start(bf16[111,16,128]{2,1,0:T(8,128)(2,1)} %copy-done.5), channel_id=1, source_target_pairs={{0,22},{2,20},{4,18},{6,16},{8,30},{10,28},{12,26},{14,24},{16,6},... | collective-permute-start | bytes 1363976 | tf_op jit(solution)/shard_map/ppermute | solution.py:357
  146.0 78.7 %all_to_all.5 = f32[16,17,128]{2,1,0:T(8,128)S(1)} all-to-all(f32[16,17,128]{2,1,0:T(8,128)S(1)} %pad_maximum_fusion), channel_id=1, replica_groups=mesh['loc'=16,'yr'=2] {'loc'}, dimensions={0} | all-to-all | bytes 278528 | tf_op jit(solution)/shard_map/all_to_all | solution.py:401
  224.7 0.8 copy.19
  225.6 0.7 reshape.54
  226.3 6.2 %turn.2.refs_8_ = bf16[2,111,64,256]{3,2,1,0:T(8,128)(2,1)} custom-call(s32[1]{0:T(128)} %bitcast.d_ref, bf16[111,16,128]{2,1,0:T(8,128)(2,1)S(1)} %get-tuple-element.50.refs_0_.refs_3_, bf16[111,16,128]{2,1,0:T(8,128)(2,1)} %collective-permute-done.14.refs_1_, bf16[111,16,128]{2,1,0:T(8,128)(2,1)} %collective-permute-done.15.refs_2_, ...), custom_call_target="tpu_custom_call" | custom-call | flops 465567744 | bytes 7274496 | tf_op jit(solution)/shard_map/turn/pallas_call | solution.py:332
  232.5 6.1 %turn.3 = bf16[2,111,64,256]{3,2,1,0:T(8,128)(2,1)} custom-call(s32[1]{0:T(128)} %bitcast.d_ref, bf16[111,16,128]{2,1,0:T(8,128)(2,1)} %collective-permute-done.3.refs_0_, bf16[111,16,128]{2,1,0:T(8,128)(2,1)} %collective-permute-done.5.refs_1_, bf16[111,16,128]{2,1,0:T(8,128)(2,1)S(1)} %collective-permute-done.7.refs_2_, ...), custom_call_target="tpu_custom_call", output_to_operand_aliasing={{}: (9, {})} | custom-call | flops 465567744 | bytes 7274496 | tf_op jit(solution)/shard_map/turn/pallas_call | solution.py:332
  (87 shorter events, 5.1 us)
Async XLA Ops:
  0.6 21.7 %collective-permute-start = (bf16[64,1024]{1,0:T(8,128)(2,1)}, bf16[64,1024]{1,0:T(8,128)(2,1)S(1)}, u32[]{:S(2)}, u32[]{:S(2)}) collective-permute-start(bf16[64,1024]{1,0:T(8,128)(2,1)} %refs_3_.1), channel_id=1, source_target_pairs={{0,16},{2,18},{4,20},{6,22},{8,24},{10,26},{12,28},{14,30},{16,0},... | collective-permute-start | bytes 393224 | tf_op jit(solution)/shard_map/ppermute | solution.py:357
  0.7 21.7 %collective-permute-start.1 = (bf16[64,1024]{1,0:T(8,128)(2,1)}, bf16[64,1024]{1,0:T(8,128)(2,1)S(1)}, u32[]{:S(2)}, u32[]{:S(2)}) collective-permute-start(bf16[64,1024]{1,0:T(8,128)(2,1)} %refs_3_.1), channel_id=1, source_target_pairs={{0,24},{2,26},{4,28},{6,30},{8,16},{10,18},{12,20},{14,22},{16,8},... | collective-permute-start | bytes 393224 | tf_op jit(solution)/shard_map/ppermute | solution.py:357
  3.2 19.2 %collective-permute-start.2 = (bf16[64,1024]{1,0:T(8,128)(2,1)}, bf16[64,1024]{1,0:T(8,128)(2,1)S(1)}, u32[]{:S(2)}, u32[]{:S(2)}) collective-permute-start(bf16[64,1024]{1,0:T(8,128)(2,1)} %refs_3_.1), channel_id=1, source_target_pairs={{0,8},{2,10},{4,12},{6,14},{8,0},{10,2},{12,4},{14,6},{16,24},{18,... | collective-permute-start | bytes 393224 | tf_op jit(solution)/shard_map/ppermute | solution.py:357
  6.2 3.1 %copy-start.9 = (bf16[2,111,16,1024]{3,2,1,0:T(8,128)(2,1)S(1)}, bf16[2,111,16,1024]{3,2,1,0:T(8,128)(2,1)}, u32[]{:S(2)}) copy-start(bf16[2,111,16,1024]{3,2,1,0:T(8,128)(2,1)} %param.10) | copy-start | bytes 21823492
  10.0 12.3 %copy-start.11 = (s32[4]{0:T(128)S(1)}, s32[4]{0:T(128)}, u32[]{:S(2)}) copy-start(s32[4]{0:T(128)} %constant.33.clone) | copy-start | bytes 52
  10.0 12.4 %copy-start.3 = (bf16[64,1024]{1,0:T(8,128)(2,1)S(1)}, bf16[64,1024]{1,0:T(8,128)(2,1)}, u32[]{:S(2)}) copy-start(bf16[64,1024]{1,0:T(8,128)(2,1)} %refs_3_.1) | copy-start | bytes 393220
  10.0 15.6 %copy-start = (f32[2,111,1024]{2,0,1:T(2,128)S(1)}, f32[2,111,1024]{2,0,1:T(2,128)}, u32[]{:S(2)}) copy-start(f32[2,111,1024]{2,0,1:T(2,128)} %param.13) | copy-start | bytes 2727940
  22.3 11.6 %copy-start.1 = (f32[2,111,1024]{2,0,1:T(2,128)S(1)}, f32[2,111,1024]{2,0,1:T(2,128)}, u32[]{:S(2)}) copy-start(f32[2,111,1024]{2,0,1:T(2,128)} %param.14) | copy-start | bytes 2727940
  22.3 11.6 %copy-start.2 = (s32[1024,1]{0,1:T(1,128)S(1)}, s32[1024,1]{0,1:T(1,128)}, u32[]{:S(2)}) copy-start(s32[1024,1]{0,1:T(1,128)} %param.15) | copy-start | bytes 12292
  22.5 23.7 %collective-permute-start.6 = (bf16[256,1024]{1,0:T(8,128)(2,1)S(1)}, bf16[256,1024]{1,0:T(8,128)(2,1)S(1)}, u32[]{:S(2)}, u32[]{:S(2)}) collective-permute-start(bf16[256,1024]{1,0:T(8,128)(2,1)S(1)} %constant_dynamic-update-slice_fusion), channel_id=1, source_target_pairs={{0,4},{2,6},{4,0},{6,2},{8,12},{10,14},{12,8},{14,10},{16,20},{18,... | collective-permute-start | bytes 1572872 | tf_op jit(solution)/shard_map/ppermute | solution.py:357
  23.8 27.4 %collective-permute-start.4 = (bf16[256,1024]{1,0:T(8,128)(2,1)S(1)}, bf16[256,1024]{1,0:T(8,128)(2,1)S(1)}, u32[]{:S(2)}, u32[]{:S(2)}) collective-permute-start(bf16[256,1024]{1,0:T(8,128)(2,1)S(1)} %constant_dynamic-update-slice_fusion), channel_id=1, source_target_pairs={{0,2},{2,0},{4,6},{6,4},{8,10},{10,8},{12,14},{14,12},{16,18},{18,... | collective-permute-start | bytes 1572872 | tf_op jit(solution)/shard_map/ppermute | solution.py:357
  30.4 67.3 %collective-permute-start.17 = (bf16[111,16,128]{2,1,0:T(8,128)(2,1)}, bf16[111,16,128]{2,1,0:T(8,128)(2,1)}, u32[]{:S(2)}, u32[]{:S(2)}) collective-permute-start(bf16[111,16,128]{2,1,0:T(8,128)(2,1)} %get-tuple-element.54.refs_2_), channel_id=1, source_target_pairs={{0,8},{2,10},{4,12},{6,14},{8,0},{10,2},{12,4},{14,6},{16,24},{18,... | collective-permute-start | bytes 1363976 | tf_op jit(solution)/shard_map/ppermute | solution.py:357
  30.8 67.3 %collective-permute-start.10 = (bf16[111,16,128]{2,1,0:T(8,128)(2,1)}, bf16[111,16,128]{2,1,0:T(8,128)(2,1)}, u32[]{:S(2)}, u32[]{:S(2)}) collective-permute-start(bf16[111,16,128]{2,1,0:T(8,128)(2,1)} %get-tuple-element.46.refs_1_), channel_id=1, source_target_pairs={{0,24},{2,26},{4,28},{6,30},{8,16},{10,18},{12,20},{14,22},{16,8},... | collective-permute-start | bytes 1363976 | tf_op jit(solution)/shard_map/ppermute | solution.py:357
  30.8 69.4 %collective-permute-start.3 = (bf16[111,16,128]{2,1,0:T(8,128)(2,1)}, bf16[111,16,128]{2,1,0:T(8,128)(2,1)}, u32[]{:S(2)}, u32[]{:S(2)}) collective-permute-start(bf16[111,16,128]{2,1,0:T(8,128)(2,1)} %get-tuple-element.42.refs_0_), channel_id=1, source_target_pairs={{0,16},{2,18},{4,20},{6,22},{8,24},{10,26},{12,28},{14,30},{16,0},... | collective-permute-start | bytes 1363976 | tf_op jit(solution)/shard_map/ppermute | solution.py:357
  50.9 49.4 %collective-permute-start.15 = (bf16[111,16,128]{2,1,0:T(8,128)(2,1)S(1)}, bf16[111,16,128]{2,1,0:T(8,128)(2,1)}, u32[]{:S(2)}, u32[]{:S(2)}) collective-permute-start(bf16[111,16,128]{2,1,0:T(8,128)(2,1)S(1)} %get-tuple-element.52.refs_3_), channel_id=1, source_target_pairs={{0,4},{2,6},{4,0},{6,2},{8,12},{10,14},{12,8},{14,10},{16,20},{18,... | collective-permute-start | bytes 1363976 | tf_op jit(solution)/shard_map/ppermute | solution.py:357
  51.2 28.1 %collective-permute-start.8 = (bf16[256,1024]{1,0:T(8,128)(2,1)S(1)}, bf16[256,1024]{1,0:T(8,128)(2,1)S(1)}, u32[]{:S(2)}, u32[]{:S(2)}) collective-permute-start(bf16[256,1024]{1,0:T(8,128)(2,1)S(1)} %collective-permute-done.6), channel_id=1, source_target_pairs={{0,2},{2,0},{4,6},{6,4},{8,10},{10,8},{12,14},{14,12},{16,18},{18,... | collective-permute-start | bytes 1572872 | tf_op jit(solution)/shard_map/ppermute | solution.py:357
  56.3 23.0 %copy-start.4 = (bf16[111,16,128]{2,1,0:T(8,128)(2,1)}, bf16[111,16,128]{2,1,0:T(8,128)(2,1)S(1)}, u32[]{:S(2)}) copy-start(bf16[111,16,128]{2,1,0:T(8,128)(2,1)S(1)} %get-tuple-element.51.refs_3_) | copy-start | bytes 1363972
  79.3 22.6 %collective-permute-start.19 = (bf16[111,16,128]{2,1,0:T(8,128)(2,1)}, bf16[111,16,128]{2,1,0:T(8,128)(2,1)}, u32[]{:S(2)}, u32[]{:S(2)}) collective-permute-start(bf16[111,16,128]{2,1,0:T(8,128)(2,1)} %get-tuple-element.56.refs_2_), channel_id=1, source_target_pairs={{0,12},{2,14},{4,8},{6,10},{8,4},{10,6},{12,0},{14,2},{16,28},{18,... | collective-permute-start | bytes 1363976 | tf_op jit(solution)/shard_map/ppermute | solution.py:357
  83.8 13.5 %copy-start.5 = (bf16[111,16,128]{2,1,0:T(8,128)(2,1)}, bf16[111,16,128]{2,1,0:T(8,128)(2,1)S(1)}, u32[]{:S(2)}) copy-start(bf16[111,16,128]{2,1,0:T(8,128)(2,1)S(1)} %get-tuple-element.45) | copy-start | bytes 1363972
  83.8 13.5 %copy-start.6 = (bf16[111,16,128]{2,1,0:T(8,128)(2,1)}, bf16[111,16,128]{2,1,0:T(8,128)(2,1)S(1)}, u32[]{:S(2)}) copy-start(bf16[111,16,128]{2,1,0:T(8,128)(2,1)S(1)} %get-tuple-element.49) | copy-start | bytes 1363972
  83.9 13.5 %copy-start.7 = (bf16[111,16,128]{2,1,0:T(8,128)(2,1)}, bf16[111,16,128]{2,1,0:T(8,128)(2,1)S(1)}, u32[]{:S(2)}) copy-start(bf16[111,16,128]{2,1,0:T(8,128)(2,1)S(1)} %get-tuple-element.57) | copy-start | bytes 1363972
  83.9 13.5 %copy-start.8 = (bf16[111,16,128]{2,1,0:T(8,128)(2,1)}, bf16[111,16,128]{2,1,0:T(8,128)(2,1)S(1)}, u32[]{:S(2)}) copy-start(bf16[111,16,128]{2,1,0:T(8,128)(2,1)S(1)} %get-tuple-element.53) | copy-start | bytes 1363972
  97.7 5.7 %collective-permute-start.14 = (bf16[111,16,128]{2,1,0:T(8,128)(2,1)}, bf16[111,16,128]{2,1,0:T(8,128)(2,1)}, u32[]{:S(2)}, u32[]{:S(2)}) collective-permute-start(bf16[111,16,128]{2,1,0:T(8,128)(2,1)} %copy-done.4), channel_id=1, source_target_pairs={{0,2},{2,0},{4,6},{6,4},{8,10},{10,8},{12,14},{14,12},{16,18},{18,... | collective-permute-start | bytes 1363976 | tf_op jit(solution)/shard_map/ppermute | solution.py:357
  98.1 13.4 %collective-permute-start.18 = (bf16[111,16,128]{2,1,0:T(8,128)(2,1)S(1)}, bf16[111,16,128]{2,1,0:T(8,128)(2,1)}, u32[]{:S(2)}, u32[]{:S(2)}) collective-permute-start(bf16[111,16,128]{2,1,0:T(8,128)(2,1)S(1)} %get-tuple-element.55.refs_2_), channel_id=1, source_target_pairs={{0,10},{2,8},{4,14},{6,12},{8,2},{10,0},{12,6},{14,4},{16,26},{18,... | collective-permute-start | bytes 1363976 | tf_op jit(solution)/shard_map/ppermute | solution.py:357
  100.2 23.7 %collective-permute-start.12 = (bf16[111,16,128]{2,1,0:T(8,128)(2,1)S(1)}, bf16[111,16,128]{2,1,0:T(8,128)(2,1)}, u32[]{:S(2)}, u32[]{:S(2)}) collective-permute-start(bf16[111,16,128]{2,1,0:T(8,128)(2,1)S(1)} %get-tuple-element.48.refs_1_), channel_id=1, source_target_pairs={{0,28},{2,30},{4,24},{6,26},{8,20},{10,22},{12,16},{14,18},{16,12}... | collective-permute-start | bytes 1363976 | tf_op jit(solution)/shard_map/ppermute | solution.py:357
  100.3 24.9 %collective-permute-start.16 = (bf16[111,16,128]{2,1,0:T(8,128)(2,1)}, bf16[111,16,128]{2,1,0:T(8,128)(2,1)}, u32[]{:S(2)}, u32[]{:S(2)}) collective-permute-start(bf16[111,16,128]{2,1,0:T(8,128)(2,1)} %copy-done.8), channel_id=1, source_target_pairs={{0,6},{2,4},{4,2},{6,0},{8,14},{10,12},{12,10},{14,8},{16,22},{18,... | collective-permute-start | bytes 1363976 | tf_op jit(solution)/shard_map/ppermute | solution.py:357
  102.0 36.9 %collective-permute-start.20 = (bf16[111,16,128]{2,1,0:T(8,128)(2,1)}, bf16[111,16,128]{2,1,0:T(8,128)(2,1)}, u32[]{:S(2)}, u32[]{:S(2)}) collective-permute-start(bf16[111,16,128]{2,1,0:T(8,128)(2,1)} %copy-done.7), channel_id=1, source_target_pairs={{0,14},{2,12},{4,10},{6,8},{8,6},{10,4},{12,2},{14,0},{16,30},{18,... | collective-permute-start | bytes 1363976 | tf_op jit(solution)/shard_map/ppermute | solution.py:357
  103.4 129.1 %collective-permute-start.7 = (bf16[111,16,128]{2,1,0:T(8,128)(2,1)S(1)}, bf16[111,16,128]{2,1,0:T(8,128)(2,1)S(1)}, u32[]{:S(2)}, u32[]{:S(2)}) collective-permute-start(bf16[111,16,128]{2,1,0:T(8,128)(2,1)S(1)} %get-tuple-element.44.refs_0_), channel_id=1, source_target_pairs={{0,20},{2,22},{4,16},{6,18},{8,28},{10,30},{12,24},{14,26},{16,4},... | collective-permute-start | bytes 1363976 | tf_op jit(solution)/shard_map/ppermute | solution.py:357
  111.4 121.0 %collective-permute-start.11 = (bf16[111,16,128]{2,1,0:T(8,128)(2,1)S(1)}, bf16[111,16,128]{2,1,0:T(8,128)(2,1)S(1)}, u32[]{:S(2)}, u32[]{:S(2)}) collective-permute-start(bf16[111,16,128]{2,1,0:T(8,128)(2,1)S(1)} %get-tuple-element.47.refs_1_), channel_id=1, source_target_pairs={{0,26},{2,24},{4,30},{6,28},{8,18},{10,16},{12,22},{14,20},{16,10}... | collective-permute-start | bytes 1363976 | tf_op jit(solution)/shard_map/ppermute | solution.py:357
  123.9 108.6 %collective-permute-start.5 = (bf16[111,16,128]{2,1,0:T(8,128)(2,1)S(1)}, bf16[111,16,128]{2,1,0:T(8,128)(2,1)}, u32[]{:S(2)}, u32[]{:S(2)}) collective-permute-start(bf16[111,16,128]{2,1,0:T(8,128)(2,1)S(1)} %get-tuple-element.43.refs_0_), channel_id=1, source_target_pairs={{0,18},{2,16},{4,22},{6,20},{8,26},{10,24},{12,30},{14,28},{16,2},... | collective-permute-start | bytes 1363976 | tf_op jit(solution)/shard_map/ppermute | solution.py:357
  125.2 107.3 %collective-permute-start.13 = (bf16[111,16,128]{2,1,0:T(8,128)(2,1)}, bf16[111,16,128]{2,1,0:T(8,128)(2,1)}, u32[]{:S(2)}, u32[]{:S(2)}) collective-permute-start(bf16[111,16,128]{2,1,0:T(8,128)(2,1)} %copy-done.6), channel_id=1, source_target_pairs={{0,30},{2,28},{4,26},{6,24},{8,22},{10,20},{12,18},{14,16},{16,14}... | collective-permute-start | bytes 1363976 | tf_op jit(solution)/shard_map/ppermute | solution.py:357
  138.9 93.7 %collective-permute-start.9 = (bf16[111,16,128]{2,1,0:T(8,128)(2,1)}, bf16[111,16,128]{2,1,0:T(8,128)(2,1)}, u32[]{:S(2)}, u32[]{:S(2)}) collective-permute-start(bf16[111,16,128]{2,1,0:T(8,128)(2,1)} %copy-done.5), channel_id=1, source_target_pairs={{0,22},{2,20},{4,18},{6,16},{8,30},{10,28},{12,26},{14,24},{16,6},... | collective-permute-start | bytes 1363976 | tf_op jit(solution)/shard_map/ppermute | solution.py:357
  (1 other events, 0.7 us)

commit v2 on v1

--- a/solution.py
+++ b/solution.py
@@ -11,7 +11,9 @@
 LANES = 128
 HALF = 64
 NT = (((1,), (1,)), ((), ()))
-CHUNKS = ((8, 12, 4, 0), (10, 14, 6, 2), (9, 13, 5, 1), (11, 15, 7, 3))
+CHUNKS = ((8, 12, 4, 0), (9, 13, 5, 1), (10, 14, 6, 2), (11, 15, 7, 3))
+FAR = (8, 12, 9, 13, 10, 14, 11, 15)
+NEAR = (4, 5, 1, 6, 2, 7, 3)
 
 
 def survival(rates):
@@ -47,6 +49,10 @@
     return (turned, loc_survival, region_survival)
 
 
+def after(x, *others):
+    return lax.optimization_barrier((x,) + others)[0]
+
+
 def split_bf16(x):
     hi = x.astype(jnp.bfloat16)
     return hi, (x - hi.astype(jnp.float32)).astype(jnp.bfloat16)
@@ -82,7 +88,7 @@
 def age_mix(age_factor, noise):
     sexes, rows, cols = noise.shape
     ages = age_factor.shape[0]
-    width = 256
+    width = 512
     return pl.pallas_call(
         age_mix_kernel,
         out_shape=jax.ShapeDtypeStruct(noise.shape, jnp.bfloat16),
@@ -93,7 +99,7 @@
         ],
         out_specs=pl.BlockSpec((1, rows, width), lambda s, k: (s, 0, k)),
         scratch_shapes=[pltpu.VMEM((rows, rows), jnp.bfloat16)],
-        compiler_params=pltpu.CompilerParams(vmem_limit_bytes=40 << 20),
+        compiler_params=pltpu.CompilerParams(vmem_limit_bytes=60 << 20),
         cost_estimate=pl.CostEstimate(
             flops=rows * rows * cols * sexes, bytes_accessed=4 * sexes * rows * cols, transcendentals=0
         ),
@@ -111,7 +117,7 @@
     return jnp.where(low, first[..., s : s + 1, :], second[..., 1 - s : 2 - s, :])
 
 
-def loc_mix_kernel(e_ref, x_ref, *refs):
+def loc_mix_kernel(bits, d_ref, x_ref, *refs):
     factors, means, outs = refs[:4], refs[4:8], refs[8:]
     l0, l1, l2, l3 = [f[...] for f in factors]
     r0 = lax.dot_general(
@@ -126,11 +132,11 @@
         g = (q // 2) * LANES
         a, b = r0[:, g : g + LANES], r1[:, g : g + LANES]
         v = jnp.where(low, a, b) if q % 2 == 0 else jnp.where(low, b, a)
-        m = merge_pair(means[q][...], (e_ref[q] & 1) == 1, q % 2 == 1)
+        m = merge_pair(means[q][...], ((d_ref[0] ^ bits[q]) & 1) == 1, q % 2 == 1)
         outs[q][...] = (v.reshape(ages, rows, LANES) + m).astype(jnp.bfloat16)
 
 
-def loc_mix(dests, mixed, factors, mean_t):
+def loc_mix(device, bits, mixed, factors, mean_t):
     sexes, rows, cols = mixed.shape
     ages = mean_t.shape[0]
     steps = 3
@@ -139,10 +145,10 @@
     msg = jax.ShapeDtypeStruct((ages, per_age, LANES), jnp.bfloat16)
 
     def mean_spec(q):
-        return pl.BlockSpec((block, sexes, LANES), lambda i, e: (i, 0, e[q] // 2))
+        return pl.BlockSpec((block, sexes, LANES), lambda i, d: (i, 0, (d[0] ^ bits[q]) // 2))
 
     return pl.pallas_call(
-        loc_mix_kernel,
+        functools.partial(loc_mix_kernel, bits),
         out_shape=[msg] * 4,
         grid_spec=pltpu.PrefetchScalarGridSpec(
             num_scalar_prefetch=1,
@@ -159,24 +165,27 @@
             transcendentals=0,
         ),
         name="loc_mix",
-    )(dests, mixed, *factors, *([mean_t] * 4))
-
-
-def survive_kernel(first, last, e_ref, *refs):
+    )(device, mixed, *factors, *([mean_t] * 4))
+
+
+def survive_kernel(bits, first, last, d_ref, *refs):
     xs, pops, regs = refs[:4], refs[4:8], refs[8:12]
     pos = 12
     if not first:
-        wsum_in, psum_in = refs[pos : pos + 2]
-        pos += 2
-    locs = refs[pos : pos + 4]
-    pos += 4
+        locs_in, wsum_in, psum_in = refs[pos : pos + 3]
+        pos += 3
+    locs = refs[pos]
+    pos += 1
+    if not first:
+        locs[...] = locs_in[...]
     if last:
         region_ref = refs[pos]
         pos += 1
     wsum_ref, psum_ref = refs[pos : pos + 2]
     hi_ref, lo_ref, pop_ref = refs[pos + 2 : pos + 5]
     ages, rows, _ = xs[0].shape
-    odd = [(e_ref[q] & 1) == 1 for q in range(4)]
+    dests = [d_ref[0] ^ b for b in bits]
+    odd = [(e & 1) == 1 for e in dests]
     zero = jnp.zeros((rows, LANES), jnp.float32)
 
     def age_step(a, carry):
@@ -196,12 +205,12 @@
             lo_ref[at, lanes] = lo
         return tuple(new_h), tuple(new_t)
 
-    hazards, totals = lax.fori_loop(0, ages, age_step, ((zero,) * 4, (zero,) * 4))
+    hazards, totals = lax.fori_loop(0, ages, age_step, ((zero,) * 4, (zero,) * 4), unroll=3)
     for q in range(4):
         out = (totals[q] + (0.5 - 0.5 * jnp.exp(-hazards[q]))) * (1.0 / ages)
         if q % 2 == 1:
             out = pltpu.roll(out, HALF, 1)
-        locs[q][...] = out
+        locs[dests[q]] = out
 
     lane = lax.broadcasted_iota(jnp.int32, (1, LANES), 1)
     low = lane < HALF
@@ -235,36 +244,36 @@
             h = h + wsum_ref[at, :] / psum_ref[pl.ds(a, 1), :]
             return h, t + jnp.exp(-h)
 
-        h, t = lax.fori_loop(0, ages, region_step, (zero, zero))
+        h, t = lax.fori_loop(0, ages, region_step, (zero, zero), unroll=3)
         region_ref[...] = (t + (0.5 - 0.5 * jnp.exp(-h))) * (1.0 / ages)
 
 
-def survive(dests, messages, pop_t, region_row, sums, last):
+def survive(device, bits, messages, pop_t, region_row, sums, last):
     ages, rows, _ = messages[0].shape
-    sexes = pop_t.shape[1]
+    sexes, locs = pop_t.shape[1], pop_t.shape[2] // HALF
     first = sums is None
     f32 = jnp.float32
-    loc = jax.ShapeDtypeStruct((rows, LANES), f32)
+    loc = jax.ShapeDtypeStruct((locs, rows, LANES), f32)
     wsum = jax.ShapeDtypeStruct((ages * rows, LANES), f32)
     psum = jax.ShapeDtypeStruct((ages, LANES), f32)
     whole = lambda *shape: pl.BlockSpec(shape, lambda i, e: (0,) * len(shape))
 
     def pop_spec(q):
-        return pl.BlockSpec((ages, sexes, LANES), lambda i, e: (0, 0, e[q] // 2))
+        return pl.BlockSpec((ages, sexes, LANES), lambda i, d: (0, 0, (d[0] ^ bits[q]) // 2))
 
     def region_spec(q):
-        return pl.BlockSpec((1, LANES), lambda i, e: (0, e[q] // 2))
+        return pl.BlockSpec((1, LANES), lambda i, d: (0, (d[0] ^ bits[q]) // 2))
 
     in_specs = [whole(ages, rows, LANES)] * 4
     in_specs += [pop_spec(q) for q in range(4)] + [region_spec(q) for q in range(4)]
     args = list(messages) + [pop_t] * 4 + [region_row] * 4
     sum_specs = [whole(ages * rows, LANES), whole(ages, LANES)]
-    outs, out_specs = [loc] * 4, [whole(rows, LANES)] * 4
+    outs, out_specs = [loc], [whole(locs, rows, LANES)]
     if not first:
-        in_specs += sum_specs
+        in_specs += out_specs + sum_specs
         args += list(sums)
     if last:
-        outs.append(loc)
+        outs.append(jax.ShapeDtypeStruct((rows, LANES), f32))
         out_specs.append(whole(rows, LANES))
     scratch = [
         pltpu.VMEM((ages * rows, 4 * LANES), jnp.bfloat16),
@@ -277,7 +286,7 @@
         outs += [wsum, psum]
         out_specs += sum_specs
     return pl.pallas_call(
-        functools.partial(survive_kernel, first, last),
+        functools.partial(survive_kernel, bits, first, last),
         out_shape=outs,
         grid_spec=pltpu.PrefetchScalarGridSpec(
             num_scalar_prefetch=1,
@@ -293,7 +302,7 @@
             transcendentals=8 * ages * rows * LANES,
         ),
         name="survive",
-    )(dests, *args)
+    )(device, *args)
 
 
 def turn_kernel(near, d_ref, *refs):
@@ -302,15 +311,11 @@
     ages = xs[0].shape[0]
     for m in range(8):
         order_ref[(d & 7) ^ m] = xs[m][...]
-    eye = (
-        lax.broadcasted_iota(jnp.int32, (LANES, LANES), 0)
-        == lax.broadcasted_iota(jnp.int32, (LANES, LANES), 1)
-    ).astype(jnp.bfloat16)
     upper = (lax.broadcasted_iota(jnp.int32, (HALF, LANES), 1) >= HALF).astype(jnp.int32)
     swapped = (upper ^ ((d >> 2) & 1) ^ (1 if near else 0)) == 1
     for a in range(ages):
         tile = order_ref[:, a].reshape(LANES, LANES)
-        t = lax.dot_general(eye, tile, NT, preferred_element_type=jnp.float32)
+        t = tile.T.astype(jnp.float32)
         top, bottom = t[:HALF], t[HALF:]
         out_ref[0, a] = jnp.where(swapped, bottom, top).astype(jnp.bfloat16)
         out_ref[1, a] = jnp.where(swapped, top, bottom).astype(jnp.bfloat16)
@@ -359,48 +364,47 @@
     mean_t = jnp.transpose(mean_rate, (1, 0, 2))
     pop_t = jnp.transpose(population, (1, 0, 2))
     region_row = region_of.reshape(1, locs)
-    dests = [here ^ jnp.array(c, jnp.int32) for c in CHUNKS]
+    device = here[None]
+    local = loc_factor.shape[0]
 
     factors = {0: loc_factor}
     for bits in (8, 12, 4):
         factors[bits] = swap(loc_factor, bits)
     mixed = age_mix(age_factor, noise.reshape(sexes, ages * rows, locs))
 
-    lane0 = jnp.concatenate([factors[b] for b in CHUNKS[0]], 0)
-    lane2 = swap(lane0, 2)
-    lane1 = swap(lane0, 1)
+    def pieces(whole):
+        return [whole[i * local : (i + 1) * local] for i in range(4)]
+
+    lane0 = [factors[b] for b in CHUNKS[0]]
+    joined = jnp.concatenate(lane0, 0)
+    lane1 = swap(joined, 1)
+    lane2 = swap(joined, 2)
     lane3 = swap(lane2, 1)
-    local = loc_factor.shape[0]
-    lanes = [[factors[b] for b in CHUNKS[0]]]
-    for whole in (lane2, lane1, lane3):
-        lanes.append([whole[i * local : (i + 1) * local] for i in range(4)])
-
-    sent, got = {}, {}
+    sent = {}
+    for bits, lane in zip(CHUNKS, (lane0, pieces(lane1), pieces(lane2), pieces(lane3))):
+        sent.update(zip(bits, loc_mix(device, bits, mixed, lane, mean_t)))
+
+    got = {0: sent[0]}
+    for order, window in ((FAR, 3), (NEAR, 2)):
+        for i, b in enumerate(order):
+            message = sent[b] if i < window else after(sent[b], got[order[i - window]])
+            got[b] = swap(message, b)
+
+    sums = None
     for c, bits in enumerate(CHUNKS):
-        messages = loc_mix(dests[c], mixed, lanes[c], mean_t)
-        for b, m in zip(bits, messages):
-            sent[b] = m
-            got[b] = m if b == 0 else swap(m, b)
-
-    loc_parts, sums = {}, None
-    for c, bits in enumerate(CHUNKS):
-        last = c == len(CHUNKS) - 1
-        out = survive(dests[c], [sent[b] for b in bits], pop_t, region_row, sums, last)
-        for b, o in zip(bits, out[:4]):
-            loc_parts[b] = o
-        if last:
-            region_part = out[4]
+        messages = [sent[b] for b in bits]
+        if c == 0:
+            messages[0] = after(messages[0], sent[CHUNKS[3][3]])
         else:
-            sums = out[4:]
-
-    by_bits = jnp.stack([loc_parts[b] for b in range(devices)])
-    by_device = jnp.take(by_bits, here ^ jnp.arange(devices, dtype=jnp.int32), axis=0)
+            messages[0] = after(messages[0], got[FAR[c - 1]])
+        sums = survive(device, bits, messages, pop_t, region_row, sums, c == len(CHUNKS) - 1)
+    by_device, region_part = sums
+
     mine = REGIONS // devices
     region_out = region_part.reshape(rows, sexes, devices, mine)
     region_out = jnp.transpose(region_out, (2, 1, 3, 0)).reshape(devices, 1, sexes * mine * rows)
-    small = lax.all_to_all(
-        jnp.concatenate([by_device, region_out], axis=1), "loc", split_axis=0, concat_axis=0, tiled=True
-    )
+    packed = jnp.concatenate([by_device, region_out], axis=1)
+    small = lax.all_to_all(packed, "loc", split_axis=0, concat_axis=0, tiled=True)
     loc_survival = jnp.transpose(small[:, :rows].reshape(devices * rows, LANES), (1, 0)).reshape(
         sexes, local, devices * rows
     )
@@ -409,8 +413,9 @@
     ).reshape(sexes, mine, devices * rows)
 
     shape = jax.ShapeDtypeStruct((sexes, ages, local, devices * rows), jnp.bfloat16)
-    device = here[None]
-    half = turn(device, [got[b] for b in range(8)], shape, None)
+    close = [got[b] for b in range(8)]
+    close[0] = after(close[0], packed)
+    half = turn(device, close, shape, None)
     log_rates = turn(device, [got[b] for b in range(8, 16)], shape, half)
     return (log_rates, loc_survival, region_survival)
 

time: 240 us -> 232 us (0.967)
  waiting for transfers between devices: 23.4 us -> 112 us
  blocking collectives: 78.7 us -> 0 us
  Pallas kernels: 77 us -> 60.5 us
  other arithmetic: 15.5 us -> 0 us
  starting transfers between devices: 36.4 us -> 45.8 us
  local copies, waits for them, and re-layouts: 6.43 us -> 12.9 us
    all_to_all x1 -> x0, blocking collectives: 78.7 us -> none  [shards_sixteen(): lax.all_to_all(jnp.concatenate([by_device, region_out], axis=1), 'loc', s...]
    ppermute x21, waiting for transfers between devices: 23.4 us -> 88.9 us  [swap(): return lax.ppermute(x, 'loc', [(i, i ^ bits) for i in range(devices)])]
    all_to_all x0 -> x1, waiting for transfers between devices: none -> 22.8 us  [shards_sixteen(): lax.all_to_all(packed, 'loc', split_axis=0, concat_axis=0, tiled=True)]
    pallas_call x7 -> x8, Pallas kernels: 52.5 us -> 38.9 us  [the longest x4 23.7 us: survive(): pl.pallas_call(functools.partial(survive_kernel, bits, first, last), out_...]
    pallas_call x1 -> x0, other arithmetic: 13.4 us -> none  [survive(): pl.pallas_call(functools.partial(survive_kernel, first, last), out_shape=...]
    all_to_all x0 -> x1, starting transfers between devices: none -> 4.94 us  [shards_sixteen(): lax.all_to_all(packed, 'loc', split_axis=0, concat_axis=0, tiled=True)]
    ppermute x21, starting transfers between devices: 36.4 us -> 40.9 us  [swap(): return lax.ppermute(x, 'loc', [(i, i ^ bits) for i in range(devices)])]
    unnamed x41 -> x30, local copies, waits for them, and re-layouts: 3.93 us -> 7.46 us
  transfers between devices with their start and end apart: 21 -> 22, of which waited for: 3 -> 9; matrix products, arithmetic and copies ran while one was open for 8% -> 2% of each run, Pallas kernels for 30% -> 24%
where the time goes in v2:
time: 232 us
  waiting for transfers between devices  112 us (48%)
  Pallas kernels  60.5 us (26%)
  starting transfers between devices  45.8 us (20%)
  local copies, waits for them, and re-layouts  12.9 us (6%)
    ppermute x21, waiting for transfers between devices, swap(): return lax.ppermute(x, 'loc', [(i, i ^ bits) for i in range(devices)])  88.9 us
    ppermute x21, starting transfers between devices, swap(): return lax.ppermute(x, 'loc', [(i, i ^ bits) for i in range(devices)])  40.9 us
    pallas_call x4, Pallas kernels, survive(): pl.pallas_call(functools.partial(survive_kernel, bits, first, last), out_...  23.7 us
    all_to_all x1, waiting for transfers between devices, shards_sixteen(): lax.all_to_all(packed, 'loc', split_axis=0, concat_axis=0, tiled=True)  22.8 us
    pallas_call x4, Pallas kernels, loc_mix(): pl.pallas_call(functools.partial(loc_mix_kernel, bits), out_shape=[msg] *...  15.3 us
    pallas_call x1, Pallas kernels, age_mix(): pl.pallas_call(age_mix_kernel, out_shape=jax.ShapeDtypeStruct(noise.shape...  12.6 us
    pallas_call x2, Pallas kernels, turn(): pl.pallas_call(functools.partial(turn_kernel, near), out_shape=out_shape,...  8.97 us
    unnamed x30, local copies, waits for them, and re-layouts  7.46 us
  transfers between devices with their start and end apart: 22, of which 9 were waited for; matrix products, arithmetic and copies ran while one was open for 2% of the time, Pallas kernels for 24%

profile of v2, /device:TPU:17, one launch (start us, length us, event | category | flops | bytes accessed | tf_op | source)
XLA Modules:
  0.0 231.7 jit_solution(14572552961036101092)
XLA Ops:
  0.7 2.5 %collective-permute-start.1 = (bf16[64,1024]{1,0:T(8,128)(2,1)}, bf16[64,1024]{1,0:T(8,128)(2,1)S(1)}, u32[]{:S(2)}, u32[]{:S(2)}) collective-permute-start(bf16[64,1024]{1,0:T(8,128)(2,1)} %refs_3_.1), channel_id=1, source_target_pairs={{0,24},{2,26},{4,28},{6,30},{8,16},{10,18},{12,20},{14,22},{16,8},... | collective-permute-start | bytes 393224 | tf_op jit(solution)/shard_map/ppermute | solution.py:362
  4.2 4.5 %collective-permute-done.refs_0_ = bf16[64,1024]{1,0:T(8,128)(2,1)S(1)} collective-permute-done((bf16[64,1024]{1,0:T(8,128)(2,1)}, bf16[64,1024]{1,0:T(8,128)(2,1)S(1)}, u32[]{:S(2)}, u32[]{:S(2)}) %collective-permute-start) | collective-permute-done | bytes 131104 | tf_op jit(solution)/shard_map/ppermute | solution.py:362
  8.8 6.9 %collective-permute-done.1.refs_1_ = bf16[64,1024]{1,0:T(8,128)(2,1)S(1)} collective-permute-done((bf16[64,1024]{1,0:T(8,128)(2,1)}, bf16[64,1024]{1,0:T(8,128)(2,1)S(1)}, u32[]{:S(2)}, u32[]{:S(2)}) %collective-permute-start.1) | collective-permute-done | bytes 131104 | tf_op jit(solution)/shard_map/ppermute | solution.py:362
  16.7 1.3 collective-permute-start.6
  18.7 12.6 %age_mix.1.x_ref = bf16[2,1776,1024]{2,1,0:T(8,128)(2,1)} custom-call(bf16[111,111]{1,0:T(8,128)(2,1)} %age_ref.1, bf16[2,1776,1024]{2,1,0:T(8,128)(2,1)} %bitcast.67), custom_call_target="tpu_custom_call" | custom-call | flops 6459752448 | bytes 14548992 | tf_op jit(solution)/shard_map/age_mix/pallas_call | solution.py:92
  31.3 3.1 %copy-done.2 = bf16[2,1776,1024]{2,1,0:T(8,128)(2,1)S(1)} copy-done((bf16[2,1776,1024]{2,1,0:T(8,128)(2,1)S(1)}, bf16[2,1776,1024]{2,1,0:T(8,128)(2,1)}, u32[]{:S(2)}) %copy-start.2) | copy-done | bytes 7274520
  34.4 3.4 %loc_mix.4 = (bf16[111,16,128]{2,1,0:T(8,128)(2,1)S(1)}, bf16[111,16,128]{2,1,0:T(8,128)(2,1)S(1)}, bf16[111,16,128]{2,1,0:T(8,128)(2,1)S(1)}, bf16[111,16,128]{2,1,0:T(8,128)(2,1)S(1)}) custom-call(s32[1]{0:T(128)} %bitcast.d_ref, bf16[2,1776,1024]{2,1,0:T(8,128)(2,1)S(1)} %copy-done.2, bf16[64,1024]{1,0:T(8,128)(2,1)S(1)} %collective-permute-done.refs_0_, ...), custom_call_target="tpu_custom_call" | custom-call | flops 1862270976 | bytes 9093120 | tf_op jit(solution)/shard_map/loc_mix/pallas_call | solution.py:150
  38.4 2.1 collective-permute-start.7
  41.4 3.5 %loc_mix.5 = (bf16[111,16,128]{2,1,0:T(8,128)(2,1)S(1)}, bf16[111,16,128]{2,1,0:T(8,128)(2,1)S(1)}, bf16[111,16,128]{2,1,0:T(8,128)(2,1)S(1)}, bf16[111,16,128]{2,1,0:T(8,128)(2,1)S(1)}) custom-call(s32[1]{0:T(128)} %bitcast.d_ref, bf16[2,1776,1024]{2,1,0:T(8,128)(2,1)S(1)} %copy-done.2, bf16[64,1024]{1,0:T(8,128)(2,1)S(1)} %get-tuple-element.96.refs_0_, ...), custom_call_target="tpu_custom_call" | custom-call | flops 1862270976 | bytes 9093120 | tf_op jit(solution)/shard_map/loc_mix/pallas_call | solution.py:150
  45.5 10.1 %collective-permute-done.14.refs_4_ = bf16[111,16,128]{2,1,0:T(8,128)(2,1)S(1)} collective-permute-done((bf16[111,16,128]{2,1,0:T(8,128)(2,1)S(1)}, bf16[111,16,128]{2,1,0:T(8,128)(2,1)S(1)}, u32[]{:S(2)}, u32[]{:S(2)}) %collective-permute-start.14) | collective-permute-done | bytes 454688 | tf_op jit(solution)/shard_map/ppermute | solution.py:362
  56.4 2.4 %collective-permute-done.3.refs_0_ = bf16[111,16,128]{2,1,0:T(8,128)(2,1)S(1)} collective-permute-done((bf16[111,16,128]{2,1,0:T(8,128)(2,1)S(1)}, bf16[111,16,128]{2,1,0:T(8,128)(2,1)S(1)}, u32[]{:S(2)}, u32[]{:S(2)}) %collective-permute-start.3) | collective-permute-done | bytes 454688 | tf_op jit(solution)/shard_map/ppermute | solution.py:362
  58.8 13.3 %collective-permute-start.5 = (bf16[111,16,128]{2,1,0:T(8,128)(2,1)S(1)}, bf16[111,16,128]{2,1,0:T(8,128)(2,1)S(1)}, u32[]{:S(2)}, u32[]{:S(2)}) collective-permute-start(bf16[111,16,128]{2,1,0:T(8,128)(2,1)S(1)} %get-tuple-element.63.refs_0_), channel_id=1, source_target_pairs={{0,18},{2,16},{4,22},{6,20},{8,26},{10,24},{12,30},{14,28},{16,2},... | collective-permute-start | bytes 1363976 | tf_op jit(solution)/shard_map/ppermute | solution.py:362
  73.1 4.1 %loc_mix.6 = (bf16[111,16,128]{2,1,0:T(8,128)(2,1)S(1)}, bf16[111,16,128]{2,1,0:T(8,128)(2,1)}, bf16[111,16,128]{2,1,0:T(8,128)(2,1)S(1)}, bf16[111,16,128]{2,1,0:T(8,128)(2,1)S(1)}) custom-call(s32[1]{0:T(128)} %bitcast.d_ref, bf16[2,1776,1024]{2,1,0:T(8,128)(2,1)S(1)} %copy-done.2, bf16[64,1024]{1,0:T(8,128)(2,1)S(1)} %get-tuple-element.92.refs_0_, ...), custom_call_target="tpu_custom_call" | custom-call | flops 1862270976 | bytes 9093120 | tf_op jit(solution)/shard_map/loc_mix/pallas_call | solution.py:150
  77.3 22.3 %collective-permute-done.7.refs_4_ = bf16[111,16,128]{2,1,0:T(8,128)(2,1)S(1)} collective-permute-done((bf16[111,16,128]{2,1,0:T(8,128)(2,1)S(1)}, bf16[111,16,128]{2,1,0:T(8,128)(2,1)S(1)}, u32[]{:S(2)}, u32[]{:S(2)}) %collective-permute-start.7) | collective-permute-done | bytes 454688 | tf_op jit(solution)/shard_map/ppermute | solution.py:362
  100.5 4.3 %collective-permute-start.19 = (bf16[111,16,128]{2,1,0:T(8,128)(2,1)S(1)}, bf16[111,16,128]{2,1,0:T(8,128)(2,1)S(1)}, u32[]{:S(2)}, u32[]{:S(2)}) collective-permute-start(bf16[111,16,128]{2,1,0:T(8,128)(2,1)S(1)} %get-tuple-element.83.refs_2_), channel_id=1, source_target_pairs={{0,12},{2,14},{4,8},{6,10},{8,4},{10,6},{12,0},{14,2},{16,28},{18,... | collective-permute-start | bytes 1363976 | tf_op jit(solution)/shard_map/ppermute | solution.py:362
  104.8 11.4 %collective-permute-done.5.refs_1_ = bf16[111,16,128]{2,1,0:T(8,128)(2,1)S(1)} collective-permute-done((bf16[111,16,128]{2,1,0:T(8,128)(2,1)S(1)}, bf16[111,16,128]{2,1,0:T(8,128)(2,1)S(1)}, u32[]{:S(2)}, u32[]{:S(2)}) %collective-permute-start.5) | collective-permute-done | bytes 454688 | tf_op jit(solution)/shard_map/ppermute | solution.py:362
  116.4 3.1 %collective-permute-start.12 = (bf16[111,16,128]{2,1,0:T(8,128)(2,1)}, bf16[111,16,128]{2,1,0:T(8,128)(2,1)}, u32[]{:S(2)}, u32[]{:S(2)}) collective-permute-start(bf16[111,16,128]{2,1,0:T(8,128)(2,1)} %get-tuple-element.54.refs_1_), channel_id=1, source_target_pairs={{0,28},{2,30},{4,24},{6,26},{8,20},{10,22},{12,16},{14,18},{16,12}... | collective-permute-start | bytes 1363976 | tf_op jit(solution)/shard_map/ppermute | solution.py:362
  119.6 4.3 %loc_mix.7 = (bf16[111,16,128]{2,1,0:T(8,128)(2,1)}, bf16[111,16,128]{2,1,0:T(8,128)(2,1)}, bf16[111,16,128]{2,1,0:T(8,128)(2,1)}, bf16[111,16,128]{2,1,0:T(8,128)(2,1)}) custom-call(s32[1]{0:T(128)} %bitcast.d_ref, bf16[2,1776,1024]{2,1,0:T(8,128)(2,1)S(1)} %copy-done.2, bf16[64,1024]{1,0:T(8,128)(2,1)S(1)} %get-tuple-element.88.refs_0_, ...), custom_call_target="tpu_custom_call" | custom-call | flops 1862270976 | bytes 9093120 | tf_op jit(solution)/shard_map/loc_mix/pallas_call | solution.py:150
  123.9 15.8 %collective-permute-done.10.refs_5_ = bf16[111,16,128]{2,1,0:T(8,128)(2,1)S(1)} collective-permute-done((bf16[111,16,128]{2,1,0:T(8,128)(2,1)S(1)}, bf16[111,16,128]{2,1,0:T(8,128)(2,1)S(1)}, u32[]{:S(2)}, u32[]{:S(2)}) %collective-permute-start.10) | collective-permute-done | bytes 454688 | tf_op jit(solution)/shard_map/ppermute | solution.py:362
  139.7 15.5 %collective-permute-done.8.refs_2_ = bf16[111,16,128]{2,1,0:T(8,128)(2,1)S(1)} collective-permute-done((bf16[111,16,128]{2,1,0:T(8,128)(2,1)S(1)}, bf16[111,16,128]{2,1,0:T(8,128)(2,1)S(1)}, u32[]{:S(2)}, u32[]{:S(2)}) %collective-permute-start.8) | collective-permute-done | bytes 454688 | tf_op jit(solution)/shard_map/ppermute | solution.py:362
  155.2 3.8 %collective-permute-start.13 = (bf16[111,16,128]{2,1,0:T(8,128)(2,1)}, bf16[111,16,128]{2,1,0:T(8,128)(2,1)}, u32[]{:S(2)}, u32[]{:S(2)}) collective-permute-start(bf16[111,16,128]{2,1,0:T(8,128)(2,1)} %get-tuple-element.56.refs_1_), channel_id=1, source_target_pairs={{0,30},{2,28},{4,26},{6,24},{8,22},{10,20},{12,18},{14,16},{16,14}... | collective-permute-start | bytes 1363976 | tf_op jit(solution)/shard_map/ppermute | solution.py:362
  159.0 5.1 %survive.4 = (f32[16,16,128]{2,1,0:T(8,128)S(1)}, f32[1776,128]{1,0:T(8,128)S(1)}, f32[111,128]{1,0:T(8,128)S(1)}) custom-call(s32[1]{0:T(128)} %bitcast.d_ref, bf16[111,16,128]{2,1,0:T(8,128)(2,1)S(1)} %get-tuple-element.66.refs_0_, bf16[111,16,128]{2,1,0:T(8,128)(2,1)S(1)} %get-tuple-element.47.refs_1_, ...), custom_call_target="tpu_custom_call" | custom-call | flops 54558720 | bytes 3637248 | tf_op jit(solution)/shard_map/survive/pallas_call | solution.py:288
  164.1 5.2 %survive.5 = (f32[16,16,128]{2,1,0:T(8,128)S(1)}, f32[1776,128]{1,0:T(8,128)S(1)}, f32[111,128]{1,0:T(8,128)S(1)}) custom-call(s32[1]{0:T(128)} %bitcast.d_ref, bf16[111,16,128]{2,1,0:T(8,128)(2,1)S(1)} %get-tuple-element.63.refs_0_, bf16[111,16,128]{2,1,0:T(8,128)(2,1)S(1)} %get-tuple-element.51.refs_1_, ...), custom_call_target="tpu_custom_call" | custom-call | flops 54558720 | bytes 3637248 | tf_op jit(solution)/shard_map/survive/pallas_call | solution.py:288
  169.3 6.1 %survive.6 = (f32[16,16,128]{2,1,0:T(8,128)S(1)}, f32[1776,128]{1,0:T(8,128)S(1)}, f32[111,128]{1,0:T(8,128)S(1)}) custom-call(s32[1]{0:T(128)} %bitcast.d_ref, bf16[111,16,128]{2,1,0:T(8,128)(2,1)S(1)} %get-tuple-element.48.refs_0_, bf16[111,16,128]{2,1,0:T(8,128)(2,1)} %get-tuple-element.54.refs_1_, bf16[111,16,128]{2,1,0:T(8,128)(2,1)S(1)} %get-tuple-element.83.refs_2_, ...), custom_call_target="tpu_custom_call" | custom-call | flops 54558720 | bytes 3637248 | tf_op jit(solution)/shard_map/survive/pallas_call | solution.py:288
  175.5 7.2 %survive.7 = (f32[16,16,128]{2,1,0:T(8,128)S(1)}, f32[16,128]{1,0:T(8,128)S(1)}) custom-call(s32[1]{0:T(128)} %bitcast.d_ref, bf16[111,16,128]{2,1,0:T(8,128)(2,1)} %get-tuple-element.58.refs_0_, bf16[111,16,128]{2,1,0:T(8,128)(2,1)} %get-tuple-element.56.refs_1_, bf16[111,16,128]{2,1,0:T(8,128)(2,1)} %get-tuple-element.84.refs_2_, ...), custom_call_target="tpu_custom_call" | custom-call | flops 54558720 | bytes 3637248 | tf_op jit(solution)/shard_map/survive/pallas_call | solution.py:288
  183.5 2.9 %collective-permute-start.20 = (bf16[111,16,128]{2,1,0:T(8,128)(2,1)}, bf16[111,16,128]{2,1,0:T(8,128)(2,1)}, u32[]{:S(2)}, u32[]{:S(2)}) collective-permute-start(bf16[111,16,128]{2,1,0:T(8,128)(2,1)} %get-tuple-element.84.refs_2_), channel_id=1, source_target_pairs={{0,14},{2,12},{4,10},{6,8},{8,6},{10,4},{12,2},{14,0},{16,30},{18,... | collective-permute-start | bytes 1363976 | tf_op jit(solution)/shard_map/ppermute | solution.py:362
  187.2 1.6 collective-permute-start.17
  189.7 1.5 dynamic-update-slice.1
  191.2 4.9 %all-to-all-start = ((f32[16,17,128]{2,1,0:T(8,128)}), f32[16,17,128]{2,1,0:T(8,128)S(1)}, u32[]{:S(2)}, u32[]{:S(2)}) async-start(f32[16,17,128]{2,1,0:T(8,128)} %dynamic-update-slice.1), calls=%async_computation | async-start | bytes 393216 | tf_op jit(solution)/shard_map/all_to_all | solution.py:407
  196.2 22.8 %all-to-all-done = f32[16,17,128]{2,1,0:T(8,128)S(1)} async-done(((f32[16,17,128]{2,1,0:T(8,128)}), f32[16,17,128]{2,1,0:T(8,128)S(1)}, u32[]{:S(2)}, u32[]{:S(2)}) %all-to-all-start) | async-done | bytes 139296 | tf_op jit(solution)/shard_map/all_to_all | solution.py:407
  222.7 4.3 %turn.2.refs_8_ = bf16[2,111,64,256]{3,2,1,0:T(8,128)(2,1)} custom-call(s32[1]{0:T(128)} %bitcast.d_ref, bf16[111,16,128]{2,1,0:T(8,128)(2,1)S(1)} %get-tuple-element.79.refs_3_.refs_0_, bf16[111,16,128]{2,1,0:T(8,128)(2,1)S(1)} %collective-permute-done.15.refs_1_, bf16[111,16,128]{2,1,0:T(8,128)(2,1)S(1)} %copy-done.12, ...), custom_call_target="tpu_custom_call" | custom-call | flops 465567744 | bytes 7274496 | tf_op jit(solution)/shard_map/turn/pallas_call | solution.py:337
  227.1 4.7 %turn.3 = bf16[2,111,64,256]{3,2,1,0:T(8,128)(2,1)} custom-call(s32[1]{0:T(128)} %bitcast.d_ref, bf16[111,16,128]{2,1,0:T(8,128)(2,1)S(1)} %collective-permute-done.3.refs_0_, bf16[111,16,128]{2,1,0:T(8,128)(2,1)S(1)} %collective-permute-done.5.refs_1_, bf16[111,16,128]{2,1,0:T(8,128)(2,1)S(1)} %copy-done.8, ...), custom_call_target="tpu_custom_call", output_to_operand_aliasing={{}: (9, {})} | custom-call | flops 465567744 | bytes 7274496 | tf_op jit(solution)/shard_map/turn/pallas_call | solution.py:337
  (67 shorter events, 14.4 us)
Async XLA Ops:
  0.6 8.1 %collective-permute-start = (bf16[64,1024]{1,0:T(8,128)(2,1)}, bf16[64,1024]{1,0:T(8,128)(2,1)S(1)}, u32[]{:S(2)}, u32[]{:S(2)}) collective-permute-start(bf16[64,1024]{1,0:T(8,128)(2,1)} %refs_3_.1), channel_id=1, source_target_pairs={{0,16},{2,18},{4,20},{6,22},{8,24},{10,26},{12,28},{14,30},{16,0},... | collective-permute-start | bytes 393224 | tf_op jit(solution)/shard_map/ppermute | solution.py:362
  0.7 15.0 %collective-permute-start.1 = (bf16[64,1024]{1,0:T(8,128)(2,1)}, bf16[64,1024]{1,0:T(8,128)(2,1)S(1)}, u32[]{:S(2)}, u32[]{:S(2)}) collective-permute-start(bf16[64,1024]{1,0:T(8,128)(2,1)} %refs_3_.1), channel_id=1, source_target_pairs={{0,24},{2,26},{4,28},{6,30},{8,16},{10,18},{12,20},{14,22},{16,8},... | collective-permute-start | bytes 393224 | tf_op jit(solution)/shard_map/ppermute | solution.py:362
  3.2 12.5 %collective-permute-start.2 = (bf16[64,1024]{1,0:T(8,128)(2,1)}, bf16[64,1024]{1,0:T(8,128)(2,1)S(1)}, u32[]{:S(2)}, u32[]{:S(2)}) collective-permute-start(bf16[64,1024]{1,0:T(8,128)(2,1)} %refs_3_.1), channel_id=1, source_target_pairs={{0,8},{2,10},{4,12},{6,14},{8,0},{10,2},{12,4},{14,6},{16,24},{18,... | collective-permute-start | bytes 393224 | tf_op jit(solution)/shard_map/ppermute | solution.py:362
  16.7 23.8 %collective-permute-start.6 = (bf16[256,1024]{1,0:T(8,128)(2,1)S(1)}, bf16[256,1024]{1,0:T(8,128)(2,1)}, u32[]{:S(2)}, u32[]{:S(2)}) collective-permute-start(bf16[256,1024]{1,0:T(8,128)(2,1)S(1)} %constant_dynamic-update-slice_fusion), channel_id=1, source_target_pairs={{0,4},{2,6},{4,0},{6,2},{8,12},{10,14},{12,8},{14,10},{16,20},{18,... | collective-permute-start | bytes 1572872 | tf_op jit(solution)/shard_map/ppermute | solution.py:362
  17.9 23.4 %collective-permute-start.4 = (bf16[256,1024]{1,0:T(8,128)(2,1)S(1)}, bf16[256,1024]{1,0:T(8,128)(2,1)S(1)}, u32[]{:S(2)}, u32[]{:S(2)}) collective-permute-start(bf16[256,1024]{1,0:T(8,128)(2,1)S(1)} %constant_dynamic-update-slice_fusion), channel_id=1, source_target_pairs={{0,2},{2,0},{4,6},{6,4},{8,10},{10,8},{12,14},{14,12},{16,18},{18,... | collective-permute-start | bytes 1572872 | tf_op jit(solution)/shard_map/ppermute | solution.py:362
  18.7 12.6 %copy-start = (f32[2,111,1024]{2,0,1:T(2,128)S(1)}, f32[2,111,1024]{2,0,1:T(2,128)}, u32[]{:S(2)}) copy-start(f32[2,111,1024]{2,0,1:T(2,128)} %param.9) | copy-start | bytes 2727940
  18.7 12.6 %copy-start.4 = (bf16[64,1024]{1,0:T(8,128)(2,1)S(1)}, bf16[64,1024]{1,0:T(8,128)(2,1)}, u32[]{:S(2)}) copy-start(bf16[64,1024]{1,0:T(8,128)(2,1)} %refs_3_.1) | copy-start | bytes 393220
  31.3 3.1 %copy-start.2 = (bf16[2,1776,1024]{2,1,0:T(8,128)(2,1)S(1)}, bf16[2,1776,1024]{2,1,0:T(8,128)(2,1)}, u32[]{:S(2)}) copy-start(bf16[2,1776,1024]{2,1,0:T(8,128)(2,1)} %age_mix.1.x_ref) | copy-start | bytes 21823492
  37.8 17.8 %collective-permute-start.14 = (bf16[111,16,128]{2,1,0:T(8,128)(2,1)S(1)}, bf16[111,16,128]{2,1,0:T(8,128)(2,1)S(1)}, u32[]{:S(2)}, u32[]{:S(2)}) collective-permute-start(bf16[111,16,128]{2,1,0:T(8,128)(2,1)S(1)} %get-tuple-element.67.refs_2_), channel_id=1, source_target_pairs={{0,8},{2,10},{4,12},{6,14},{8,0},{10,2},{12,4},{14,6},{16,24},{18,... | collective-permute-start | bytes 1363976 | tf_op jit(solution)/shard_map/ppermute | solution.py:362
  37.8 20.9 %collective-permute-start.3 = (bf16[111,16,128]{2,1,0:T(8,128)(2,1)S(1)}, bf16[111,16,128]{2,1,0:T(8,128)(2,1)S(1)}, u32[]{:S(2)}, u32[]{:S(2)}) collective-permute-start(bf16[111,16,128]{2,1,0:T(8,128)(2,1)S(1)} %get-tuple-element.66.refs_0_), channel_id=1, source_target_pairs={{0,16},{2,18},{4,20},{6,22},{8,24},{10,26},{12,28},{14,30},{16,0},... | collective-permute-start | bytes 1363976 | tf_op jit(solution)/shard_map/ppermute | solution.py:362
  38.4 61.2 %collective-permute-start.7 = (bf16[111,16,128]{2,1,0:T(8,128)(2,1)S(1)}, bf16[111,16,128]{2,1,0:T(8,128)(2,1)S(1)}, u32[]{:S(2)}, u32[]{:S(2)}) collective-permute-start(bf16[111,16,128]{2,1,0:T(8,128)(2,1)S(1)} %get-tuple-element.47.refs_1_), channel_id=1, source_target_pairs={{0,24},{2,26},{4,28},{6,30},{8,16},{10,18},{12,20},{14,22},{16,8},... | collective-permute-start | bytes 1363976 | tf_op jit(solution)/shard_map/ppermute | solution.py:362
  40.5 76.0 %collective-permute-start.9 = (bf16[256,1024]{1,0:T(8,128)(2,1)}, bf16[256,1024]{1,0:T(8,128)(2,1)S(1)}, u32[]{:S(2)}, u32[]{:S(2)}) collective-permute-start(bf16[256,1024]{1,0:T(8,128)(2,1)} %collective-permute-done.6), channel_id=1, source_target_pairs={{0,2},{2,0},{4,6},{6,4},{8,10},{10,8},{12,14},{14,12},{16,18},{18,... | collective-permute-start | bytes 1572872 | tf_op jit(solution)/shard_map/ppermute | solution.py:362
  44.8 55.7 %collective-permute-start.18 = (bf16[111,16,128]{2,1,0:T(8,128)(2,1)S(1)}, bf16[111,16,128]{2,1,0:T(8,128)(2,1)S(1)}, u32[]{:S(2)}, u32[]{:S(2)}) collective-permute-start(bf16[111,16,128]{2,1,0:T(8,128)(2,1)S(1)} %get-tuple-element.64.refs_2_), channel_id=1, source_target_pairs={{0,10},{2,8},{4,14},{6,12},{8,2},{10,0},{12,6},{14,4},{16,26},{18,... | collective-permute-start | bytes 1363976 | tf_op jit(solution)/shard_map/ppermute | solution.py:362
  55.6 45.0 %collective-permute-start.15 = (bf16[111,16,128]{2,1,0:T(8,128)(2,1)S(1)}, bf16[111,16,128]{2,1,0:T(8,128)(2,1)S(1)}, u32[]{:S(2)}, u32[]{:S(2)}) collective-permute-start(bf16[111,16,128]{2,1,0:T(8,128)(2,1)S(1)} %get-tuple-element.80.refs_3_), channel_id=1, source_target_pairs={{0,2},{2,0},{4,6},{6,4},{8,10},{10,8},{12,14},{14,12},{16,18},{18,... | collective-permute-start | bytes 1363976 | tf_op jit(solution)/shard_map/ppermute | solution.py:362
  58.8 57.4 %collective-permute-start.5 = (bf16[111,16,128]{2,1,0:T(8,128)(2,1)S(1)}, bf16[111,16,128]{2,1,0:T(8,128)(2,1)S(1)}, u32[]{:S(2)}, u32[]{:S(2)}) collective-permute-start(bf16[111,16,128]{2,1,0:T(8,128)(2,1)S(1)} %get-tuple-element.63.refs_0_), channel_id=1, source_target_pairs={{0,18},{2,16},{4,22},{6,20},{8,26},{10,24},{12,30},{14,28},{16,2},... | collective-permute-start | bytes 1363976 | tf_op jit(solution)/shard_map/ppermute | solution.py:362
  77.3 81.7 %copy-start.1 = (f32[2,111,1024]{2,0,1:T(2,128)S(1)}, f32[2,111,1024]{2,0,1:T(2,128)}, u32[]{:S(2)}) copy-start(f32[2,111,1024]{2,0,1:T(2,128)} %param.10) | copy-start | bytes 2727940
  77.3 81.7 %copy-start.3 = (s32[1024,1]{0,1:T(1,128)S(1)}, s32[1024,1]{0,1:T(1,128)}, u32[]{:S(2)}) copy-start(s32[1024,1]{0,1:T(1,128)} %param.11) | copy-start | bytes 12292
  99.5 40.2 %collective-permute-start.10 = (bf16[111,16,128]{2,1,0:T(8,128)(2,1)S(1)}, bf16[111,16,128]{2,1,0:T(8,128)(2,1)S(1)}, u32[]{:S(2)}, u32[]{:S(2)}) collective-permute-start(bf16[111,16,128]{2,1,0:T(8,128)(2,1)S(1)} %get-tuple-element.51.refs_1_), channel_id=1, source_target_pairs={{0,26},{2,24},{4,30},{6,28},{8,18},{10,16},{12,22},{14,20},{16,10}... | collective-permute-start | bytes 1363976 | tf_op jit(solution)/shard_map/ppermute | solution.py:362
  100.5 54.6 %collective-permute-start.8 = (bf16[111,16,128]{2,1,0:T(8,128)(2,1)S(1)}, bf16[111,16,128]{2,1,0:T(8,128)(2,1)S(1)}, u32[]{:S(2)}, u32[]{:S(2)}) collective-permute-start(bf16[111,16,128]{2,1,0:T(8,128)(2,1)S(1)} %get-tuple-element.48.refs_0_), channel_id=1, source_target_pairs={{0,20},{2,22},{4,16},{6,18},{8,28},{10,30},{12,24},{14,26},{16,4},... | collective-permute-start | bytes 1363976 | tf_op jit(solution)/shard_map/ppermute | solution.py:362
  100.5 82.2 %collective-permute-start.19 = (bf16[111,16,128]{2,1,0:T(8,128)(2,1)S(1)}, bf16[111,16,128]{2,1,0:T(8,128)(2,1)S(1)}, u32[]{:S(2)}, u32[]{:S(2)}) collective-permute-start(bf16[111,16,128]{2,1,0:T(8,128)(2,1)S(1)} %get-tuple-element.83.refs_2_), channel_id=1, source_target_pairs={{0,12},{2,14},{4,8},{6,10},{8,4},{10,6},{12,0},{14,2},{16,28},{18,... | collective-permute-start | bytes 1363976 | tf_op jit(solution)/shard_map/ppermute | solution.py:362
  116.2 70.2 %collective-permute-start.16 = (bf16[111,16,128]{2,1,0:T(8,128)(2,1)S(1)}, bf16[111,16,128]{2,1,0:T(8,128)(2,1)S(1)}, u32[]{:S(2)}, u32[]{:S(2)}) collective-permute-start(bf16[111,16,128]{2,1,0:T(8,128)(2,1)S(1)} %get-tuple-element.81.refs_3_), channel_id=1, source_target_pairs={{0,4},{2,6},{4,0},{6,2},{8,12},{10,14},{12,8},{14,10},{16,20},{18,... | collective-permute-start | bytes 1363976 | tf_op jit(solution)/shard_map/ppermute | solution.py:362
  116.4 110.6 %collective-permute-start.12 = (bf16[111,16,128]{2,1,0:T(8,128)(2,1)}, bf16[111,16,128]{2,1,0:T(8,128)(2,1)}, u32[]{:S(2)}, u32[]{:S(2)}) collective-permute-start(bf16[111,16,128]{2,1,0:T(8,128)(2,1)} %get-tuple-element.54.refs_1_), channel_id=1, source_target_pairs={{0,28},{2,30},{4,24},{6,26},{8,20},{10,22},{12,16},{14,18},{16,12}... | collective-permute-start | bytes 1363976 | tf_op jit(solution)/shard_map/ppermute | solution.py:362
  139.7 35.8 %copy-start.5 = (bf16[111,16,128]{2,1,0:T(8,128)(2,1)}, bf16[111,16,128]{2,1,0:T(8,128)(2,1)S(1)}, u32[]{:S(2)}) copy-start(bf16[111,16,128]{2,1,0:T(8,128)(2,1)S(1)} %collective-permute-done.10.refs_5_) | copy-start | bytes 1363972
  139.7 87.3 %collective-permute-start.11 = (bf16[111,16,128]{2,1,0:T(8,128)(2,1)}, bf16[111,16,128]{2,1,0:T(8,128)(2,1)}, u32[]{:S(2)}, u32[]{:S(2)}) collective-permute-start(bf16[111,16,128]{2,1,0:T(8,128)(2,1)} %get-tuple-element.58.refs_0_), channel_id=1, source_target_pairs={{0,22},{2,20},{4,18},{6,16},{8,30},{10,28},{12,26},{14,24},{16,6},... | collective-permute-start | bytes 1363976 | tf_op jit(solution)/shard_map/ppermute | solution.py:362
  155.2 20.3 %copy-start.7 = (bf16[111,16,128]{2,1,0:T(8,128)(2,1)}, bf16[111,16,128]{2,1,0:T(8,128)(2,1)S(1)}, u32[]{:S(2)}) copy-start(bf16[111,16,128]{2,1,0:T(8,128)(2,1)S(1)} %collective-permute-done.8.refs_2_) | copy-start | bytes 1363972
  155.2 71.8 %collective-permute-start.13 = (bf16[111,16,128]{2,1,0:T(8,128)(2,1)}, bf16[111,16,128]{2,1,0:T(8,128)(2,1)}, u32[]{:S(2)}, u32[]{:S(2)}) collective-permute-start(bf16[111,16,128]{2,1,0:T(8,128)(2,1)} %get-tuple-element.56.refs_1_), channel_id=1, source_target_pairs={{0,30},{2,28},{4,26},{6,24},{8,22},{10,20},{12,18},{14,16},{16,14}... | collective-permute-start | bytes 1363976 | tf_op jit(solution)/shard_map/ppermute | solution.py:362
  183.5 37.1 %collective-permute-start.20 = (bf16[111,16,128]{2,1,0:T(8,128)(2,1)}, bf16[111,16,128]{2,1,0:T(8,128)(2,1)}, u32[]{:S(2)}, u32[]{:S(2)}) collective-permute-start(bf16[111,16,128]{2,1,0:T(8,128)(2,1)} %get-tuple-element.84.refs_2_), channel_id=1, source_target_pairs={{0,14},{2,12},{4,10},{6,8},{8,6},{10,4},{12,2},{14,0},{16,30},{18,... | collective-permute-start | bytes 1363976 | tf_op jit(solution)/shard_map/ppermute | solution.py:362
  187.2 33.4 %collective-permute-start.17 = (bf16[111,16,128]{2,1,0:T(8,128)(2,1)}, bf16[111,16,128]{2,1,0:T(8,128)(2,1)}, u32[]{:S(2)}, u32[]{:S(2)}) collective-permute-start(bf16[111,16,128]{2,1,0:T(8,128)(2,1)} %get-tuple-element.82.refs_3_), channel_id=1, source_target_pairs={{0,6},{2,4},{4,2},{6,0},{8,14},{10,12},{12,10},{14,8},{16,22},{18,... | collective-permute-start | bytes 1363976 | tf_op jit(solution)/shard_map/ppermute | solution.py:362
  191.2 27.7 %all-to-all-start = ((f32[16,17,128]{2,1,0:T(8,128)}), f32[16,17,128]{2,1,0:T(8,128)S(1)}, u32[]{:S(2)}, u32[]{:S(2)}) async-start(f32[16,17,128]{2,1,0:T(8,128)} %dynamic-update-slice.1), calls=%async_computation | async-start | bytes 393216 | tf_op jit(solution)/shard_map/all_to_all | solution.py:407
  220.6 6.5 %copy-start.6 = (bf16[111,16,128]{2,1,0:T(8,128)(2,1)S(1)}, bf16[111,16,128]{2,1,0:T(8,128)(2,1)}, u32[]{:S(2)}) copy-start(bf16[111,16,128]{2,1,0:T(8,128)(2,1)} %copy-done.5) | copy-start | bytes 1363972
  220.6 6.5 %copy-start.8 = (bf16[111,16,128]{2,1,0:T(8,128)(2,1)S(1)}, bf16[111,16,128]{2,1,0:T(8,128)(2,1)}, u32[]{:S(2)}) copy-start(bf16[111,16,128]{2,1,0:T(8,128)(2,1)} %copy-done.7) | copy-start | bytes 1363972
  220.6 1.1 copy-start.10
  (3 other events, 2.6 us)

commit v3 on v2

--- a/solution.py
+++ b/solution.py
@@ -49,8 +49,8 @@
     return (turned, loc_survival, region_survival)
 
 
-def after(x, *others):
-    return lax.optimization_barrier((x,) + others)[0]
+def tie(x, other):
+    return lax.optimization_barrier((x, other))
 
 
 def split_bf16(x):
@@ -58,7 +58,7 @@
     return hi, (x - hi.astype(jnp.float32)).astype(jnp.bfloat16)
 
 
-def age_mix_kernel(age_ref, x_ref, o_ref, wide_ref):
+def age_mix_kernel(age_ref, x_ref, o_ref, done_ref, wide_ref):
     ages = age_ref.shape[0]
     rows = x_ref.shape[1]
     step = 256
@@ -78,6 +78,7 @@
             )
             wide_ref[lo:hi, :hi] = jnp.where(same, both, 0.0).astype(jnp.bfloat16)
 
+    done_ref[...] = jnp.zeros_like(done_ref)
     for lo in range(0, rows, step):
         hi = min(lo + step, rows)
         o_ref[0, lo:hi, :] = jnp.dot(
@@ -91,13 +92,13 @@
     width = 512
     return pl.pallas_call(
         age_mix_kernel,
-        out_shape=jax.ShapeDtypeStruct(noise.shape, jnp.bfloat16),
+        out_shape=(jax.ShapeDtypeStruct(noise.shape, jnp.bfloat16), jax.ShapeDtypeStruct((8, LANES), jnp.float32)),
         grid=(sexes, cols // width),
         in_specs=[
             pl.BlockSpec((ages, ages), lambda s, k: (0, 0)),
             pl.BlockSpec((1, rows, width), lambda s, k: (s, 0, k)),
         ],
-        out_specs=pl.BlockSpec((1, rows, width), lambda s, k: (s, 0, k)),
+        out_specs=(pl.BlockSpec((1, rows, width), lambda s, k: (s, 0, k)), pl.BlockSpec((8, LANES), lambda s, k: (0, 0))),
         scratch_shapes=[pltpu.VMEM((rows, rows), jnp.bfloat16)],
         compiler_params=pltpu.CompilerParams(vmem_limit_bytes=60 << 20),
         cost_estimate=pl.CostEstimate(
@@ -117,16 +118,34 @@
     return jnp.where(low, first[..., s : s + 1, :], second[..., 1 - s : 2 - s, :])
 
 
-def loc_mix_kernel(bits, d_ref, x_ref, *refs):
-    factors, means, outs = refs[:4], refs[4:8], refs[8:]
-    l0, l1, l2, l3 = [f[...] for f in factors]
-    r0 = lax.dot_general(
-        x_ref[0], jnp.concatenate([l0, l1, l2, l3], 0), NT, preferred_element_type=jnp.float32
+def join_kernel(*refs):
+    size = refs[0].shape[0]
+    for i, ref in enumerate(refs[:-1]):
+        refs[-1][i * size : (i + 1) * size, :] = ref[...]
+
+
+def join(parts):
+    rows, cols = parts[0].shape
+    return pl.pallas_call(
+        join_kernel,
+        out_shape=jax.ShapeDtypeStruct((rows * len(parts), cols), parts[0].dtype),
+        compiler_params=pltpu.CompilerParams(vmem_limit_bytes=60 << 20),
+        cost_estimate=pl.CostEstimate(
+            flops=0, bytes_accessed=4 * len(parts) * rows * cols, transcendentals=0
+        ),
+        name="join",
+    )(*parts)
+
+
+def loc_mix_kernel(bits, d_ref, x_ref, l_ref, m0, m1, m2, m3, done_ref, *outs):
+    factor = l_ref[...]
+    crossed = jnp.concatenate(
+        [l_ref[at * HALF : (at + 1) * HALF, :] for at in (1, 0, 3, 2)], 0
     )
-    r1 = lax.dot_general(
-        x_ref[1], jnp.concatenate([l1, l0, l3, l2], 0), NT, preferred_element_type=jnp.float32
-    )
+    means = (m0, m1, m2, m3)
     ages, rows, _ = outs[0].shape
+    r0 = lax.dot_general(x_ref[0], factor, NT, preferred_element_type=jnp.float32)
+    r1 = lax.dot_general(x_ref[1], crossed, NT, preferred_element_type=jnp.float32)
     low = lax.broadcasted_iota(jnp.int32, (1, LANES), 1) < HALF
     for q in range(4):
         g = (q // 2) * LANES
@@ -136,7 +155,7 @@
         outs[q][...] = (v.reshape(ages, rows, LANES) + m).astype(jnp.bfloat16)
 
 
-def loc_mix(device, bits, mixed, factors, mean_t):
+def loc_mix(device, bits, mixed, factor, mean_t, done):
     sexes, rows, cols = mixed.shape
     ages = mean_t.shape[0]
     steps = 3
@@ -153,19 +172,20 @@
         grid_spec=pltpu.PrefetchScalarGridSpec(
             num_scalar_prefetch=1,
             grid=(steps,),
-            in_specs=[pl.BlockSpec((sexes, block * per_age, cols), lambda i, e: (0, i, 0))]
-            + [pl.BlockSpec((HALF, cols), lambda i, e: (0, 0))] * 4
-            + [mean_spec(q) for q in range(4)],
-            out_specs=[pl.BlockSpec((block, per_age, LANES), lambda i, e: (i, 0, 0))] * 4,
-        ),
-        compiler_params=pltpu.CompilerParams(vmem_limit_bytes=40 << 20),
+            in_specs=[pl.BlockSpec((sexes, block * per_age, cols), lambda i, d: (0, i, 0))]
+            + [pl.BlockSpec(factor.shape, lambda i, d: (0, 0))]
+            + [mean_spec(q) for q in range(4)]
+            + [pl.BlockSpec(done.shape, lambda i, d: (0, 0))],
+            out_specs=[pl.BlockSpec((block, per_age, LANES), lambda i, d: (i, 0, 0))] * 4,
+        ),
+        compiler_params=pltpu.CompilerParams(vmem_limit_bytes=60 << 20),
         cost_estimate=pl.CostEstimate(
             flops=2 * sexes * rows * cols * 256,
             bytes_accessed=2 * sexes * rows * cols + 8 * rows * LANES,
             transcendentals=0,
         ),
         name="loc_mix",
-    )(device, mixed, *factors, *([mean_t] * 4))
+    )(device, mixed, factor, *([mean_t] * 4), done)
 
 
 def survive_kernel(bits, first, last, d_ref, *refs):
@@ -256,7 +276,7 @@
     loc = jax.ShapeDtypeStruct((locs, rows, LANES), f32)
     wsum = jax.ShapeDtypeStruct((ages * rows, LANES), f32)
     psum = jax.ShapeDtypeStruct((ages, LANES), f32)
-    whole = lambda *shape: pl.BlockSpec(shape, lambda i, e: (0,) * len(shape))
+    whole = lambda *shape: pl.BlockSpec(shape, lambda i, d: (0,) * len(shape))
 
     def pop_spec(q):
         return pl.BlockSpec((ages, sexes, LANES), lambda i, d: (0, 0, (d[0] ^ bits[q]) // 2))
@@ -295,7 +315,7 @@
             out_specs=out_specs,
             scratch_shapes=scratch,
         ),
-        compiler_params=pltpu.CompilerParams(vmem_limit_bytes=40 << 20),
+        compiler_params=pltpu.CompilerParams(vmem_limit_bytes=60 << 20),
         cost_estimate=pl.CostEstimate(
             flops=60 * 4 * ages * rows * LANES,
             bytes_accessed=16 * ages * rows * LANES,
@@ -321,7 +341,7 @@
         out_ref[1, a] = jnp.where(swapped, top, bottom).astype(jnp.bfloat16)
 
 
-def turn(device, messages, out_shape, previous):
+def turn(device, messages, out_shape, previous, ready=()):
     near = previous is None
     ages, rows, _ = messages[0].shape
     steps = 3
@@ -331,8 +351,8 @@
     flip = 0 if near else 1
     aliases = {}
     if not near:
-        in_specs.append(pl.BlockSpec(memory_space=pl.ANY))
-        args.append(previous)
+        in_specs += [pl.BlockSpec(memory_space=pl.ANY)] * (1 + len(ready))
+        args += [previous, *ready]
         aliases = {9: 0}
     return pl.pallas_call(
         functools.partial(turn_kernel, near),
@@ -345,7 +365,7 @@
             scratch_shapes=[pltpu.VMEM((8, block, rows, LANES), jnp.bfloat16)],
         ),
         input_output_aliases=aliases,
-        compiler_params=pltpu.CompilerParams(vmem_limit_bytes=40 << 20),
+        compiler_params=pltpu.CompilerParams(vmem_limit_bytes=60 << 20),
         cost_estimate=pl.CostEstimate(
             flops=2 * ages * LANES**3, bytes_accessed=32 * ages * rows * LANES, transcendentals=0
         ),
@@ -353,70 +373,75 @@
     )(device, *args)
 
 
-def shards_sixteen(noise, loc_factor, age_factor, mean_rate, population, region_of):
-    sexes, ages, rows, locs = noise.shape
-    devices = lax.axis_size("loc")
-    here = lax.axis_index("loc")
-
-    def swap(x, bits):
-        return lax.ppermute(x, "loc", [(i, i ^ bits) for i in range(devices)])
-
-    mean_t = jnp.transpose(mean_rate, (1, 0, 2))
-    pop_t = jnp.transpose(population, (1, 0, 2))
-    region_row = region_of.reshape(1, locs)
-    device = here[None]
-    local = loc_factor.shape[0]
-
-    factors = {0: loc_factor}
-    for bits in (8, 12, 4):
-        factors[bits] = swap(loc_factor, bits)
-    mixed = age_mix(age_factor, noise.reshape(sexes, ages * rows, locs))
-
-    def pieces(whole):
-        return [whole[i * local : (i + 1) * local] for i in range(4)]
-
-    lane0 = [factors[b] for b in CHUNKS[0]]
-    joined = jnp.concatenate(lane0, 0)
-    lane1 = swap(joined, 1)
-    lane2 = swap(joined, 2)
-    lane3 = swap(lane2, 1)
-    sent = {}
-    for bits, lane in zip(CHUNKS, (lane0, pieces(lane1), pieces(lane2), pieces(lane3))):
-        sent.update(zip(bits, loc_mix(device, bits, mixed, lane, mean_t)))
-
-    got = {0: sent[0]}
-    for order, window in ((FAR, 3), (NEAR, 2)):
-        for i, b in enumerate(order):
-            message = sent[b] if i < window else after(sent[b], got[order[i - window]])
-            got[b] = swap(message, b)
-
-    sums = None
-    for c, bits in enumerate(CHUNKS):
-        messages = [sent[b] for b in bits]
-        if c == 0:
-            messages[0] = after(messages[0], sent[CHUNKS[3][3]])
-        else:
-            messages[0] = after(messages[0], got[FAR[c - 1]])
-        sums = survive(device, bits, messages, pop_t, region_row, sums, c == len(CHUNKS) - 1)
-    by_device, region_part = sums
-
+def exchange(by_device, region_part, sexes):
+    devices, rows, _ = by_device.shape
     mine = REGIONS // devices
     region_out = region_part.reshape(rows, sexes, devices, mine)
     region_out = jnp.transpose(region_out, (2, 1, 3, 0)).reshape(devices, 1, sexes * mine * rows)
     packed = jnp.concatenate([by_device, region_out], axis=1)
     small = lax.all_to_all(packed, "loc", split_axis=0, concat_axis=0, tiled=True)
-    loc_survival = jnp.transpose(small[:, :rows].reshape(devices * rows, LANES), (1, 0)).reshape(
-        sexes, local, devices * rows
-    )
+    loc_survival = jnp.transpose(small[:, :rows].reshape(devices * rows, LANES), (1, 0))
     region_survival = jnp.transpose(
         small[:, rows].reshape(devices, sexes, mine, rows), (1, 2, 0, 3)
     ).reshape(sexes, mine, devices * rows)
-
-    shape = jax.ShapeDtypeStruct((sexes, ages, local, devices * rows), jnp.bfloat16)
+    return loc_survival.reshape(sexes, HALF, devices * rows), region_survival
+
+
+def shards_sixteen(noise, loc_factor, age_factor, mean_rate, population, region_of):
+    sexes, ages, rows, locs = noise.shape
+    devices = lax.axis_size("loc")
+    here = lax.axis_index("loc")
+
+    def swap(x, bits):
+        return lax.ppermute(x, "loc", [(i, i ^ bits) for i in range(devices)])
+
+    mean_t = jnp.transpose(mean_rate, (1, 0, 2))
+    pop_t = jnp.transpose(population, (1, 0, 2))
+    region_row = region_of.reshape(1, locs)
+    device = here[None]
+
+    factors = {0: loc_factor}
+    for bits in (8, 12, 4):
+        factors[bits] = swap(loc_factor, bits)
+    mixed, done = age_mix(age_factor, noise.reshape(sexes, ages * rows, locs))
+    factors, done = tie(factors, done)
+
+    lane0 = join([factors[b] for b in CHUNKS[0]])
+    lane1 = swap(lane0, 1)
+    lane2 = swap(lane0, 2)
+    lane3 = swap(lane2, 1)
+    sent = {}
+    for bits, lane in zip(CHUNKS, (lane0, lane1, lane2, lane3)):
+        sent.update(zip(bits, loc_mix(device, bits, mixed, lane, mean_t, done)))
+
+    got = {0: sent[0]}
+    first, sent[CHUNKS[3][3]] = tie(sent[CHUNKS[0][0]], sent[CHUNKS[3][3]])
+    sums = None
+    for i, b in enumerate(FAR):
+        message = sent[b]
+        if i >= 3:
+            message, got[FAR[i - 3]] = tie(message, got[FAR[i - 3]])
+        if 3 <= i < 7:
+            bits = CHUNKS[i - 3]
+            messages = [first if b == CHUNKS[0][0] else sent[b] for b in bits]
+            sums = survive(device, bits, messages, pop_t, region_row, sums, i == 6)
+            message, sums = tie(message, sums)
+        if i == 7:
+            small = exchange(*sums, sexes)
+            message, small = tie(message, small)
+        got[b] = swap(message, b)
+    for i, b in enumerate(NEAR):
+        message = sent[b]
+        if i >= 2:
+            message, got[NEAR[i - 2]] = tie(message, got[NEAR[i - 2]])
+        got[b] = swap(message, b)
+
+    shape = jax.ShapeDtypeStruct((sexes, ages, HALF, devices * rows), jnp.bfloat16)
     close = [got[b] for b in range(8)]
-    close[0] = after(close[0], packed)
     half = turn(device, close, shape, None)
-    log_rates = turn(device, [got[b] for b in range(8, 16)], shape, half)
+    loc_survival, region_survival = small
+    ready = (loc_survival, region_survival)
+    log_rates = turn(device, [got[b] for b in range(8, 16)], shape, half, ready)
     return (log_rates, loc_survival, region_survival)
 
 

time: 232 us -> 221 us (0.953)
  Pallas kernels: 60.5 us -> 82.6 us
  waiting for transfers between devices: 112 us -> 95.8 us
  starting transfers between devices: 45.8 us -> 33.4 us
  local copies, waits for them, and re-layouts: 12.9 us -> 5.67 us
    ppermute x21, starting transfers between devices: 40.9 us -> 28.2 us  [swap(): return lax.ppermute(x, 'loc', [(i, i ^ bits) for i in range(devices)])]
    all_to_all x1, waiting for transfers between devices: 22.8 us -> 11.2 us  [exchange(): lax.all_to_all(packed, 'loc', split_axis=0, concat_axis=0, tiled=True)]
    pallas_call x4, Pallas kernels: 15.3 us -> 25.3 us  [loc_mix(): pl.pallas_call(functools.partial(loc_mix_kernel, bits), out_shape=[msg] *...]
    pallas_call x4, Pallas kernels: 23.7 us -> 31.8 us  [survive(): pl.pallas_call(functools.partial(survive_kernel, bits, first, last), out_...]
    unnamed x30 -> x38, local copies, waits for them, and re-layouts: 7.46 us -> 3.16 us
    ppermute x21, waiting for transfers between devices: 88.9 us -> 84.6 us  [swap(): return lax.ppermute(x, 'loc', [(i, i ^ bits) for i in range(devices)])]
    concatenate x2 -> x0, local copies, waits for them, and re-layouts: 2.42 us -> none  [the longest x1 1.51 us: shards_sixteen(): packed = jnp.concatenate([by_device, region_out], axis=1)]
    pallas_call x1 -> x2, Pallas kernels: 12.6 us -> 14.4 us  [the longest x1 12.5 us: age_mix(): pl.pallas_call(age_mix_kernel, out_shape=(jax.ShapeDtypeStruct(noise.shap...]
  transfers between devices with their start and end apart: 22 -> 22, of which waited for: 9 -> 10; matrix products, arithmetic and copies ran while one was open for 2% -> 2% of each run, Pallas kernels for 24% -> 34%
where the time goes in v3:
time: 221 us; the launch traced here: 220 us
  waiting for transfers between devices  95.8 us (43%)
  Pallas kernels  82.6 us (37%)
  starting transfers between devices  33.4 us (15%)
  local copies, waits for them, and re-layouts  5.67 us (3%)
    ppermute x21, waiting for transfers between devices, swap(): return lax.ppermute(x, 'loc', [(i, i ^ bits) for i in range(devices)])  84.6 us
    pallas_call x4, Pallas kernels, survive(): pl.pallas_call(functools.partial(survive_kernel, bits, first, last), out_...  31.8 us
    ppermute x21, starting transfers between devices, swap(): return lax.ppermute(x, 'loc', [(i, i ^ bits) for i in range(devices)])  28.2 us
    pallas_call x4, Pallas kernels, loc_mix(): pl.pallas_call(functools.partial(loc_mix_kernel, bits), out_shape=[msg] *...  25.3 us
    pallas_call x1, Pallas kernels, age_mix(): pl.pallas_call(age_mix_kernel, out_shape=(jax.ShapeDtypeStruct(noise.shap...  12.5 us
    all_to_all x1, waiting for transfers between devices, exchange(): lax.all_to_all(packed, 'loc', split_axis=0, concat_axis=0, tiled=True)  11.2 us
    pallas_call x2, Pallas kernels, turn(): pl.pallas_call(functools.partial(turn_kernel, near), out_shape=out_shape,...  11.1 us
    all_to_all x1, starting transfers between devices, exchange(): lax.all_to_all(packed, 'loc', split_axis=0, concat_axis=0, tiled=True)  5.18 us
  transfers between devices with their start and end apart: 22, of which 10 were waited for; matrix products, arithmetic and copies ran while one was open for 2% of the time, Pallas kernels for 34%

profile of v3, /device:TPU:17, one launch (start us, length us, event | category | flops | bytes accessed | tf_op | source)
XLA Modules:
  0.0 219.9 jit_solution(3751922195680386631)
XLA Ops:
  0.7 1.4 collective-permute-start
  3.3 12.5 %age_mix.1 = (bf16[2,1776,1024]{2,1,0:T(8,128)(2,1)}, f32[8,128]{1,0:T(8,128)}) custom-call(bf16[111,111]{1,0:T(8,128)(2,1)} %age_ref.1, bf16[2,1776,1024]{2,1,0:T(8,128)(2,1)} %bitcast.70), custom_call_target="tpu_custom_call" | custom-call | flops 6459752448 | bytes 14548992 | tf_op jit(solution)/shard_map/age_mix/pallas_call | solution.py:93
  16.6 1.9 join.1.l_ref
  19.7 1.8 collective-permute-start.3
  21.5 9.1 %collective-permute-done.5.l_ref = bf16[256,1024]{1,0:T(8,128)(2,1)S(1)} collective-permute-done((bf16[256,1024]{1,0:T(8,128)(2,1)}, bf16[256,1024]{1,0:T(8,128)(2,1)S(1)}, u32[]{:S(2)}, u32[]{:S(2)}) %collective-permute-start.5) | collective-permute-done | bytes 524320 | tf_op jit(solution)/shard_map/ppermute | solution.py:396
  30.6 2.4 %collective-permute-start.7 = (bf16[256,1024]{1,0:T(8,128)(2,1)S(1)}, bf16[256,1024]{1,0:T(8,128)(2,1)S(1)}, u32[]{:S(2)}, u32[]{:S(2)}) collective-permute-start(bf16[256,1024]{1,0:T(8,128)(2,1)S(1)} %collective-permute-done.5.l_ref), channel_id=1, source_target_pairs={{0,2},{2,0},{4,6},{6,4},{8,10},{10,8},{12,14},{14,12},{16,18},{18,... | collective-permute-start | bytes 1572872 | tf_op jit(solution)/shard_map/ppermute | solution.py:396
  33.1 6.3 %loc_mix.5 = (bf16[111,16,128]{2,1,0:T(8,128)(2,1)}, bf16[111,16,128]{2,1,0:T(8,128)(2,1)}, bf16[111,16,128]{2,1,0:T(8,128)(2,1)}, bf16[111,16,128]{2,1,0:T(8,128)(2,1)}) custom-call(s32[1]{0:T(128)} %bitcast.d_ref, bf16[2,1776,1024]{2,1,0:T(8,128)(2,1)} %get-tuple-element.77.x_ref, bf16[256,1024]{1,0:T(8,128)(2,1)} %join.1.l_ref, f32[111,2,1024]{2,1,0:T(2,128)} %bitcast.17, ...), custom_call_target="tpu_custom_call" | custom-call | flops 1862270976 | bytes 9093120 | tf_op jit(solution)/shard_map/loc_mix/pallas_call | solution.py:169
  43.6 6.3 %loc_mix.4 = (bf16[111,16,128]{2,1,0:T(8,128)(2,1)}, bf16[111,16,128]{2,1,0:T(8,128)(2,1)}, bf16[111,16,128]{2,1,0:T(8,128)(2,1)}, bf16[111,16,128]{2,1,0:T(8,128)(2,1)}) custom-call(s32[1]{0:T(128)} %bitcast.d_ref, bf16[2,1776,1024]{2,1,0:T(8,128)(2,1)} %get-tuple-element.77.x_ref, bf16[256,1024]{1,0:T(8,128)(2,1)} %copy-done.2, f32[111,2,1024]{2,1,0:T(2,128)} %bitcast.21, ...), custom_call_target="tpu_custom_call" | custom-call | flops 1862270976 | bytes 9093120 | tf_op jit(solution)/shard_map/loc_mix/pallas_call | solution.py:169
  49.9 2.2 collective-permute-start.6
  52.1 8.1 %collective-permute-done.4.refs_0_ = bf16[111,16,128]{2,1,0:T(8,128)(2,1)S(1)} collective-permute-done((bf16[111,16,128]{2,1,0:T(8,128)(2,1)}, bf16[111,16,128]{2,1,0:T(8,128)(2,1)S(1)}, u32[]{:S(2)}, u32[]{:S(2)}) %collective-permute-start.4) | collective-permute-done | bytes 454688 | tf_op jit(solution)/shard_map/ppermute | solution.py:396
  60.2 4.7 %collective-permute-start.18 = (bf16[111,16,128]{2,1,0:T(8,128)(2,1)}, bf16[111,16,128]{2,1,0:T(8,128)(2,1)S(1)}, u32[]{:S(2)}, u32[]{:S(2)}) collective-permute-start(bf16[111,16,128]{2,1,0:T(8,128)(2,1)} %get-tuple-element.94.refs_2_), channel_id=1, source_target_pairs={{0,10},{2,8},{4,14},{6,12},{8,2},{10,0},{12,6},{14,4},{16,26},{18,... | collective-permute-start | bytes 1363976 | tf_op jit(solution)/shard_map/ppermute | solution.py:396
  65.8 6.3 %loc_mix.7 = (bf16[111,16,128]{2,1,0:T(8,128)(2,1)}, bf16[111,16,128]{2,1,0:T(8,128)(2,1)}, bf16[111,16,128]{2,1,0:T(8,128)(2,1)}, bf16[111,16,128]{2,1,0:T(8,128)(2,1)}) custom-call(s32[1]{0:T(128)} %bitcast.d_ref, bf16[2,1776,1024]{2,1,0:T(8,128)(2,1)} %get-tuple-element.77.x_ref, bf16[256,1024]{1,0:T(8,128)(2,1)} %copy-done.1, f32[111,2,1024]{2,1,0:T(2,128)} %bitcast.25, ...), custom_call_target="tpu_custom_call" | custom-call | flops 1862270976 | bytes 9093120 | tf_op jit(solution)/shard_map/loc_mix/pallas_call | solution.py:169
  72.1 7.5 %survive.4 = (f32[16,16,128]{2,1,0:T(8,128)}, f32[1776,128]{1,0:T(8,128)}, f32[111,128]{1,0:T(8,128)}) custom-call(s32[1]{0:T(128)} %bitcast.d_ref, bf16[111,16,128]{2,1,0:T(8,128)(2,1)} %get-tuple-element.98.refs_0_, bf16[111,16,128]{2,1,0:T(8,128)(2,1)} %get-tuple-element.92.refs_1_, bf16[111,16,128]{2,1,0:T(8,128)(2,1)} %get-tuple-element.99.refs_2_, ...), custom_call_target="tpu_custom_call" | custom-call | flops 54558720 | bytes 3637248 | tf_op jit(solution)/shard_map/survive/pallas_call | solution.py:308
  80.0 6.3 %loc_mix.6 = (bf16[111,16,128]{2,1,0:T(8,128)(2,1)}, bf16[111,16,128]{2,1,0:T(8,128)(2,1)}, bf16[111,16,128]{2,1,0:T(8,128)(2,1)}, bf16[111,16,128]{2,1,0:T(8,128)(2,1)}) custom-call(s32[1]{0:T(128)} %bitcast.d_ref, bf16[2,1776,1024]{2,1,0:T(8,128)(2,1)} %get-tuple-element.77.x_ref, bf16[256,1024]{1,0:T(8,128)(2,1)} %copy-done, f32[111,2,1024]{2,1,0:T(2,128)} %bitcast.29, ...), custom_call_target="tpu_custom_call" | custom-call | flops 1862270976 | bytes 9093120 | tf_op jit(solution)/shard_map/loc_mix/pallas_call | solution.py:169
  86.3 6.1 %collective-permute-done.8.refs_4_ = bf16[111,16,128]{2,1,0:T(8,128)(2,1)S(1)} collective-permute-done((bf16[111,16,128]{2,1,0:T(8,128)(2,1)}, bf16[111,16,128]{2,1,0:T(8,128)(2,1)S(1)}, u32[]{:S(2)}, u32[]{:S(2)}) %collective-permute-start.8) | collective-permute-done | bytes 454688 | tf_op jit(solution)/shard_map/ppermute | solution.py:396
  93.8 7.8 %survive.5 = (f32[16,16,128]{2,1,0:T(8,128)}, f32[1776,128]{1,0:T(8,128)}, f32[111,128]{1,0:T(8,128)}) custom-call(s32[1]{0:T(128)} %bitcast.d_ref, bf16[111,16,128]{2,1,0:T(8,128)(2,1)} %get-tuple-element.88.refs_0_, bf16[111,16,128]{2,1,0:T(8,128)(2,1)} %get-tuple-element.113.refs_1_, bf16[111,16,128]{2,1,0:T(8,128)(2,1)} %get-tuple-element.94.refs_2_, ...), custom_call_target="tpu_custom_call" | custom-call | flops 54558720 | bytes 3637248 | tf_op jit(solution)/shard_map/survive/pallas_call | solution.py:308
  101.6 2.3 %collective-permute-start.9 = (bf16[111,16,128]{2,1,0:T(8,128)(2,1)}, bf16[111,16,128]{2,1,0:T(8,128)(2,1)S(1)}, u32[]{:S(2)}, u32[]{:S(2)}) collective-permute-start(bf16[111,16,128]{2,1,0:T(8,128)(2,1)} %get-tuple-element.110.refs_0_), channel_id=1, source_target_pairs={{0,20},{2,22},{4,16},{6,18},{8,28},{10,30},{12,24},{14,26},{16,4},... | collective-permute-start | bytes 1363976 | tf_op jit(solution)/shard_map/ppermute | solution.py:396
  103.9 5.0 %collective-permute-done.6.refs_1_ = bf16[111,16,128]{2,1,0:T(8,128)(2,1)S(1)} collective-permute-done((bf16[111,16,128]{2,1,0:T(8,128)(2,1)}, bf16[111,16,128]{2,1,0:T(8,128)(2,1)S(1)}, u32[]{:S(2)}, u32[]{:S(2)}) %collective-permute-start.6) | collective-permute-done | bytes 454688 | tf_op jit(solution)/shard_map/ppermute | solution.py:396
  108.9 8.0 %survive.6 = (f32[16,16,128]{2,1,0:T(8,128)}, f32[1776,128]{1,0:T(8,128)}, f32[111,128]{1,0:T(8,128)}) custom-call(s32[1]{0:T(128)} %bitcast.d_ref, bf16[111,16,128]{2,1,0:T(8,128)(2,1)} %get-tuple-element.110.refs_0_, bf16[111,16,128]{2,1,0:T(8,128)(2,1)} %get-tuple-element.134.refs_1_, bf16[111,16,128]{2,1,0:T(8,128)(2,1)} %get-tuple-element.146.refs_2_, ...), custom_call_target="tpu_custom_call" | custom-call | flops 54558720 | bytes 3637248 | tf_op jit(solution)/shard_map/survive/pallas_call | solution.py:308
  116.9 8.5 %survive.7 = (f32[16,16,128]{2,1,0:T(8,128)}, f32[16,128]{1,0:T(8,128)}) custom-call(s32[1]{0:T(128)} %bitcast.d_ref, bf16[111,16,128]{2,1,0:T(8,128)(2,1)} %get-tuple-element.131.refs_0_, bf16[111,16,128]{2,1,0:T(8,128)(2,1)} %get-tuple-element.138.refs_1_, bf16[111,16,128]{2,1,0:T(8,128)(2,1)} %get-tuple-element.148.refs_2_, ...), custom_call_target="tpu_custom_call" | custom-call | flops 54558720 | bytes 3637248 | tf_op jit(solution)/shard_map/survive/pallas_call | solution.py:308
  125.4 5.5 %collective-permute-done.10.refs_5_ = bf16[111,16,128]{2,1,0:T(8,128)(2,1)S(1)} collective-permute-done((bf16[111,16,128]{2,1,0:T(8,128)(2,1)}, bf16[111,16,128]{2,1,0:T(8,128)(2,1)S(1)}, u32[]{:S(2)}, u32[]{:S(2)}) %collective-permute-start.10) | collective-permute-done | bytes 454688 | tf_op jit(solution)/shard_map/ppermute | solution.py:396
  131.9 1.6 pad_maximum_fusion
  133.5 5.2 %all-to-all-start = ((f32[16,17,128]{2,1,0:T(8,128)}), f32[16,17,128]{2,1,0:T(8,128)S(1)}, u32[]{:S(2)}, u32[]{:S(2)}) async-start(f32[16,17,128]{2,1,0:T(8,128)} %pad_maximum_fusion), calls=%async_computation | async-start | bytes 393216 | tf_op jit(solution)/shard_map/all_to_all | solution.py:382
  141.2 1.3 collective-permute-start.17
  142.5 1.9 collective-permute-start.11
  144.5 11.2 %all-to-all-done = f32[16,17,128]{2,1,0:T(8,128)S(1)} async-done(((f32[16,17,128]{2,1,0:T(8,128)}), f32[16,17,128]{2,1,0:T(8,128)S(1)}, u32[]{:S(2)}, u32[]{:S(2)}) %all-to-all-start) | async-done | bytes 139296 | tf_op jit(solution)/shard_map/all_to_all | solution.py:382
  157.3 17.0 %collective-permute-done.20.refs_7_ = bf16[111,16,128]{2,1,0:T(8,128)(2,1)} collective-permute-done((bf16[111,16,128]{2,1,0:T(8,128)(2,1)}, bf16[111,16,128]{2,1,0:T(8,128)(2,1)}, u32[]{:S(2)}, u32[]{:S(2)}) %collective-permute-start.20) | collective-permute-done | bytes 454688 | tf_op jit(solution)/shard_map/ppermute | solution.py:396
  174.3 5.6 %turn.2.refs_8_ = bf16[2,111,64,256]{3,2,1,0:T(8,128)(2,1)} custom-call(s32[1]{0:T(128)} %bitcast.d_ref, bf16[111,16,128]{2,1,0:T(8,128)(2,1)} %get-tuple-element.100.refs_3_.refs_0_, bf16[111,16,128]{2,1,0:T(8,128)(2,1)} %collective-permute-done.15.refs_1_, bf16[111,16,128]{2,1,0:T(8,128)(2,1)} %collective-permute-done.16.refs_2_, ...), custom_call_target="tpu_custom_call" | custom-call | flops 465567744 | bytes 7274496 | tf_op jit(solution)/shard_map/turn/pallas_call | solution.py:357
  179.8 14.3 %collective-permute-done.12.refs_6_ = bf16[111,16,128]{2,1,0:T(8,128)(2,1)S(1)} collective-permute-done((bf16[111,16,128]{2,1,0:T(8,128)(2,1)}, bf16[111,16,128]{2,1,0:T(8,128)(2,1)S(1)}, u32[]{:S(2)}, u32[]{:S(2)}) %collective-permute-start.12) | collective-permute-done | bytes 454688 | tf_op jit(solution)/shard_map/ppermute | solution.py:396
  194.1 6.2 %collective-permute-done.11.refs_3_ = bf16[111,16,128]{2,1,0:T(8,128)(2,1)S(1)} collective-permute-done((bf16[111,16,128]{2,1,0:T(8,128)(2,1)S(1)}, bf16[111,16,128]{2,1,0:T(8,128)(2,1)S(1)}, u32[]{:S(2)}, u32[]{:S(2)}) %collective-permute-start.11) | collective-permute-done | bytes 454688 | tf_op jit(solution)/shard_map/ppermute | solution.py:396
  200.3 13.3 %collective-permute-done.13.refs_7_ = bf16[111,16,128]{2,1,0:T(8,128)(2,1)S(1)} collective-permute-done((bf16[111,16,128]{2,1,0:T(8,128)(2,1)S(1)}, bf16[111,16,128]{2,1,0:T(8,128)(2,1)S(1)}, u32[]{:S(2)}, u32[]{:S(2)}) %collective-permute-start.13) | collective-permute-done | bytes 454688 | tf_op jit(solution)/shard_map/ppermute | solution.py:396
  214.4 5.5 %turn.3 = bf16[2,111,64,256]{3,2,1,0:T(8,128)(2,1)} custom-call(s32[1]{0:T(128)} %bitcast.d_ref, bf16[111,16,128]{2,1,0:T(8,128)(2,1)} %copy-done.3, bf16[111,16,128]{2,1,0:T(8,128)(2,1)} %copy-done.5, bf16[111,16,128]{2,1,0:T(8,128)(2,1)} %copy-done.7, bf16[111,16,128]{2,1,0:T(8,128)(2,1)} %copy-done.9, ...), custom_call_target="tpu_custom_call", output_to_operand_aliasing={{}: (9, {})} | custom-call | flops 465567744 | bytes 7274496 | tf_op jit(solution)/shard_map/turn/pallas_call | solution.py:357
  (72 shorter events, 15.9 us)
Async XLA Ops:
  0.6 15.2 %collective-permute-start.1 = (bf16[64,1024]{1,0:T(8,128)(2,1)}, bf16[64,1024]{1,0:T(8,128)(2,1)S(1)}, u32[]{:S(2)}, u32[]{:S(2)}) collective-permute-start(bf16[64,1024]{1,0:T(8,128)(2,1)} %refs_3_), channel_id=1, source_target_pairs={{0,16},{2,18},{4,20},{6,22},{8,24},{10,26},{12,28},{14,30},{16,0},... | collective-permute-start | bytes 393224 | tf_op jit(solution)/shard_map/ppermute | solution.py:396
  0.7 15.1 %collective-permute-start = (bf16[64,1024]{1,0:T(8,128)(2,1)}, bf16[64,1024]{1,0:T(8,128)(2,1)S(1)}, u32[]{:S(2)}, u32[]{:S(2)}) collective-permute-start(bf16[64,1024]{1,0:T(8,128)(2,1)} %refs_3_), channel_id=1, source_target_pairs={{0,8},{2,10},{4,12},{6,14},{8,0},{10,2},{12,4},{14,6},{16,24},{18,... | collective-permute-start | bytes 393224 | tf_op jit(solution)/shard_map/ppermute | solution.py:396
  2.1 13.8 %collective-permute-start.2 = (bf16[64,1024]{1,0:T(8,128)(2,1)}, bf16[64,1024]{1,0:T(8,128)(2,1)S(1)}, u32[]{:S(2)}, u32[]{:S(2)}) collective-permute-start(bf16[64,1024]{1,0:T(8,128)(2,1)} %refs_3_), channel_id=1, source_target_pairs={{0,24},{2,26},{4,28},{6,30},{8,16},{10,18},{12,20},{14,22},{16,8},... | collective-permute-start | bytes 393224 | tf_op jit(solution)/shard_map/ppermute | solution.py:396
  18.5 12.1 %collective-permute-start.5 = (bf16[256,1024]{1,0:T(8,128)(2,1)}, bf16[256,1024]{1,0:T(8,128)(2,1)S(1)}, u32[]{:S(2)}, u32[]{:S(2)}) collective-permute-start(bf16[256,1024]{1,0:T(8,128)(2,1)} %join.1.l_ref), channel_id=1, source_target_pairs={{0,4},{2,6},{4,0},{6,2},{8,12},{10,14},{12,8},{14,10},{16,20},{18,... | collective-permute-start | bytes 1572872 | tf_op jit(solution)/shard_map/ppermute | solution.py:396
  19.7 23.1 %collective-permute-start.3 = (bf16[256,1024]{1,0:T(8,128)(2,1)}, bf16[256,1024]{1,0:T(8,128)(2,1)S(1)}, u32[]{:S(2)}, u32[]{:S(2)}) collective-permute-start(bf16[256,1024]{1,0:T(8,128)(2,1)} %join.1.l_ref), channel_id=1, source_target_pairs={{0,2},{2,0},{4,6},{6,4},{8,10},{10,8},{12,14},{14,12},{16,18},{18,... | collective-permute-start | bytes 1572872 | tf_op jit(solution)/shard_map/ppermute | solution.py:396
  30.6 19.3 %copy-start = (bf16[256,1024]{1,0:T(8,128)(2,1)}, bf16[256,1024]{1,0:T(8,128)(2,1)S(1)}, u32[]{:S(2)}) copy-start(bf16[256,1024]{1,0:T(8,128)(2,1)S(1)} %collective-permute-done.5.l_ref) | copy-start | bytes 1572868
  30.6 34.3 %collective-permute-start.7 = (bf16[256,1024]{1,0:T(8,128)(2,1)S(1)}, bf16[256,1024]{1,0:T(8,128)(2,1)S(1)}, u32[]{:S(2)}, u32[]{:S(2)}) collective-permute-start(bf16[256,1024]{1,0:T(8,128)(2,1)S(1)} %collective-permute-done.5.l_ref), channel_id=1, source_target_pairs={{0,2},{2,0},{4,6},{6,4},{8,10},{10,8},{12,14},{14,12},{16,18},{18,... | collective-permute-start | bytes 1572872 | tf_op jit(solution)/shard_map/ppermute | solution.py:396
  39.4 20.8 %collective-permute-start.4 = (bf16[111,16,128]{2,1,0:T(8,128)(2,1)}, bf16[111,16,128]{2,1,0:T(8,128)(2,1)S(1)}, u32[]{:S(2)}, u32[]{:S(2)}) collective-permute-start(bf16[111,16,128]{2,1,0:T(8,128)(2,1)} %get-tuple-element.98.refs_0_), channel_id=1, source_target_pairs={{0,16},{2,18},{4,20},{6,22},{8,24},{10,26},{12,28},{14,30},{16,0},... | collective-permute-start | bytes 1363976 | tf_op jit(solution)/shard_map/ppermute | solution.py:396
  40.4 24.5 %collective-permute-start.14 = (bf16[111,16,128]{2,1,0:T(8,128)(2,1)}, bf16[111,16,128]{2,1,0:T(8,128)(2,1)S(1)}, u32[]{:S(2)}, u32[]{:S(2)}) collective-permute-start(bf16[111,16,128]{2,1,0:T(8,128)(2,1)} %get-tuple-element.99.refs_2_), channel_id=1, source_target_pairs={{0,8},{2,10},{4,12},{6,14},{8,0},{10,2},{12,4},{14,6},{16,24},{18,... | collective-permute-start | bytes 1363976 | tf_op jit(solution)/shard_map/ppermute | solution.py:396
  41.7 50.7 %collective-permute-start.8 = (bf16[111,16,128]{2,1,0:T(8,128)(2,1)}, bf16[111,16,128]{2,1,0:T(8,128)(2,1)S(1)}, u32[]{:S(2)}, u32[]{:S(2)}) collective-permute-start(bf16[111,16,128]{2,1,0:T(8,128)(2,1)} %get-tuple-element.92.refs_1_), channel_id=1, source_target_pairs={{0,24},{2,26},{4,28},{6,30},{8,16},{10,18},{12,20},{14,22},{16,8},... | collective-permute-start | bytes 1363976 | tf_op jit(solution)/shard_map/ppermute | solution.py:396
  49.9 59.0 %collective-permute-start.6 = (bf16[111,16,128]{2,1,0:T(8,128)(2,1)}, bf16[111,16,128]{2,1,0:T(8,128)(2,1)S(1)}, u32[]{:S(2)}, u32[]{:S(2)}) collective-permute-start(bf16[111,16,128]{2,1,0:T(8,128)(2,1)} %get-tuple-element.88.refs_0_), channel_id=1, source_target_pairs={{0,18},{2,16},{4,22},{6,20},{8,26},{10,24},{12,30},{14,28},{16,2},... | collective-permute-start | bytes 1363976 | tf_op jit(solution)/shard_map/ppermute | solution.py:396
  60.2 65.2 %copy-start.3 = (bf16[111,16,128]{2,1,0:T(8,128)(2,1)}, bf16[111,16,128]{2,1,0:T(8,128)(2,1)S(1)}, u32[]{:S(2)}) copy-start(bf16[111,16,128]{2,1,0:T(8,128)(2,1)S(1)} %collective-permute-done.4.refs_0_) | copy-start | bytes 1363972
  60.2 32.3 %collective-permute-start.18 = (bf16[111,16,128]{2,1,0:T(8,128)(2,1)}, bf16[111,16,128]{2,1,0:T(8,128)(2,1)S(1)}, u32[]{:S(2)}, u32[]{:S(2)}) collective-permute-start(bf16[111,16,128]{2,1,0:T(8,128)(2,1)} %get-tuple-element.94.refs_2_), channel_id=1, source_target_pairs={{0,10},{2,8},{4,14},{6,12},{8,2},{10,0},{12,6},{14,4},{16,26},{18,... | collective-permute-start | bytes 1363976 | tf_op jit(solution)/shard_map/ppermute | solution.py:396
  64.9 60.5 %copy-start.11 = (bf16[111,16,128]{2,1,0:T(8,128)(2,1)}, bf16[111,16,128]{2,1,0:T(8,128)(2,1)S(1)}, u32[]{:S(2)}) copy-start(bf16[111,16,128]{2,1,0:T(8,128)(2,1)S(1)} %collective-permute-done.14.refs_4_) | copy-start | bytes 1363972
  64.9 27.6 %collective-permute-start.15 = (bf16[111,16,128]{2,1,0:T(8,128)(2,1)}, bf16[111,16,128]{2,1,0:T(8,128)(2,1)}, u32[]{:S(2)}, u32[]{:S(2)}) collective-permute-start(bf16[111,16,128]{2,1,0:T(8,128)(2,1)} %get-tuple-element.139.refs_3_), channel_id=1, source_target_pairs={{0,2},{2,0},{4,6},{6,4},{8,10},{10,8},{12,14},{14,12},{16,18},{18,... | collective-permute-start | bytes 1363976 | tf_op jit(solution)/shard_map/ppermute | solution.py:396
  79.6 51.4 %collective-permute-start.10 = (bf16[111,16,128]{2,1,0:T(8,128)(2,1)}, bf16[111,16,128]{2,1,0:T(8,128)(2,1)S(1)}, u32[]{:S(2)}, u32[]{:S(2)}) collective-permute-start(bf16[111,16,128]{2,1,0:T(8,128)(2,1)} %get-tuple-element.113.refs_1_), channel_id=1, source_target_pairs={{0,26},{2,24},{4,30},{6,28},{8,18},{10,16},{12,22},{14,20},{16,10}... | collective-permute-start | bytes 1363976 | tf_op jit(solution)/shard_map/ppermute | solution.py:396
  92.4 33.0 %copy-start.4 = (bf16[111,16,128]{2,1,0:T(8,128)(2,1)}, bf16[111,16,128]{2,1,0:T(8,128)(2,1)S(1)}, u32[]{:S(2)}) copy-start(bf16[111,16,128]{2,1,0:T(8,128)(2,1)S(1)} %collective-permute-done.8.refs_4_) | copy-start | bytes 1363972
  92.4 47.4 %collective-permute-start.19 = (bf16[111,16,128]{2,1,0:T(8,128)(2,1)}, bf16[111,16,128]{2,1,0:T(8,128)(2,1)S(1)}, u32[]{:S(2)}, u32[]{:S(2)}) collective-permute-start(bf16[111,16,128]{2,1,0:T(8,128)(2,1)} %get-tuple-element.146.refs_2_), channel_id=1, source_target_pairs={{0,12},{2,14},{4,8},{6,10},{8,4},{10,6},{12,0},{14,2},{16,28},{18,... | collective-permute-start | bytes 1363976 | tf_op jit(solution)/shard_map/ppermute | solution.py:396
  92.5 48.6 %collective-permute-start.16 = (bf16[111,16,128]{2,1,0:T(8,128)(2,1)}, bf16[111,16,128]{2,1,0:T(8,128)(2,1)}, u32[]{:S(2)}, u32[]{:S(2)}) collective-permute-start(bf16[111,16,128]{2,1,0:T(8,128)(2,1)} %get-tuple-element.141.refs_3_), channel_id=1, source_target_pairs={{0,4},{2,6},{4,0},{6,2},{8,12},{10,14},{12,8},{14,10},{16,20},{18,... | collective-permute-start | bytes 1363976 | tf_op jit(solution)/shard_map/ppermute | solution.py:396
  101.6 40.9 %copy-start.14 = (bf16[111,16,128]{2,1,0:T(8,128)(2,1)S(1)}, bf16[111,16,128]{2,1,0:T(8,128)(2,1)}, u32[]{:S(2)}) copy-start(bf16[111,16,128]{2,1,0:T(8,128)(2,1)} %get-tuple-element.131.refs_0_) | copy-start | bytes 1363972
  101.6 40.9 %collective-permute-start.9 = (bf16[111,16,128]{2,1,0:T(8,128)(2,1)}, bf16[111,16,128]{2,1,0:T(8,128)(2,1)S(1)}, u32[]{:S(2)}, u32[]{:S(2)}) collective-permute-start(bf16[111,16,128]{2,1,0:T(8,128)(2,1)} %get-tuple-element.110.refs_0_), channel_id=1, source_target_pairs={{0,20},{2,22},{4,16},{6,18},{8,28},{10,30},{12,24},{14,26},{16,4},... | collective-permute-start | bytes 1363976 | tf_op jit(solution)/shard_map/ppermute | solution.py:396
  108.9 47.6 %copy-start.5 = (bf16[111,16,128]{2,1,0:T(8,128)(2,1)}, bf16[111,16,128]{2,1,0:T(8,128)(2,1)S(1)}, u32[]{:S(2)}) copy-start(bf16[111,16,128]{2,1,0:T(8,128)(2,1)S(1)} %collective-permute-done.6.refs_1_) | copy-start | bytes 1363972
  108.9 48.4 %copy-start.13 = (bf16[111,16,128]{2,1,0:T(8,128)(2,1)S(1)}, bf16[111,16,128]{2,1,0:T(8,128)(2,1)}, u32[]{:S(2)}) copy-start(bf16[111,16,128]{2,1,0:T(8,128)(2,1)} %get-tuple-element.138.refs_1_) | copy-start | bytes 1363972
  131.0 82.6 %copy-start.6 = (bf16[111,16,128]{2,1,0:T(8,128)(2,1)}, bf16[111,16,128]{2,1,0:T(8,128)(2,1)S(1)}, u32[]{:S(2)}) copy-start(bf16[111,16,128]{2,1,0:T(8,128)(2,1)S(1)} %collective-permute-done.10.refs_5_) | copy-start | bytes 1363972
  133.5 22.2 %all-to-all-start = ((f32[16,17,128]{2,1,0:T(8,128)}), f32[16,17,128]{2,1,0:T(8,128)S(1)}, u32[]{:S(2)}, u32[]{:S(2)}) async-start(f32[16,17,128]{2,1,0:T(8,128)} %pad_maximum_fusion), calls=%async_computation | async-start | bytes 393216 | tf_op jit(solution)/shard_map/all_to_all | solution.py:382
  138.7 55.4 %collective-permute-start.12 = (bf16[111,16,128]{2,1,0:T(8,128)(2,1)}, bf16[111,16,128]{2,1,0:T(8,128)(2,1)S(1)}, u32[]{:S(2)}, u32[]{:S(2)}) collective-permute-start(bf16[111,16,128]{2,1,0:T(8,128)(2,1)} %get-tuple-element.134.refs_1_), channel_id=1, source_target_pairs={{0,28},{2,30},{4,24},{6,26},{8,20},{10,22},{12,16},{14,18},{16,12}... | collective-permute-start | bytes 1363976 | tf_op jit(solution)/shard_map/ppermute | solution.py:396
  139.8 34.4 %collective-permute-start.20 = (bf16[111,16,128]{2,1,0:T(8,128)(2,1)}, bf16[111,16,128]{2,1,0:T(8,128)(2,1)}, u32[]{:S(2)}, u32[]{:S(2)}) collective-permute-start(bf16[111,16,128]{2,1,0:T(8,128)(2,1)} %get-tuple-element.148.refs_2_), channel_id=1, source_target_pairs={{0,14},{2,12},{4,10},{6,8},{8,6},{10,4},{12,2},{14,0},{16,30},{18,... | collective-permute-start | bytes 1363976 | tf_op jit(solution)/shard_map/ppermute | solution.py:396
  141.2 33.1 %collective-permute-start.17 = (bf16[111,16,128]{2,1,0:T(8,128)(2,1)}, bf16[111,16,128]{2,1,0:T(8,128)(2,1)}, u32[]{:S(2)}, u32[]{:S(2)}) collective-permute-start(bf16[111,16,128]{2,1,0:T(8,128)(2,1)} %get-tuple-element.143.refs_3_), channel_id=1, source_target_pairs={{0,6},{2,4},{4,2},{6,0},{8,14},{10,12},{12,10},{14,8},{16,22},{18,... | collective-permute-start | bytes 1363976 | tf_op jit(solution)/shard_map/ppermute | solution.py:396
  142.5 71.1 %copy-start.7 = (bf16[111,16,128]{2,1,0:T(8,128)(2,1)}, bf16[111,16,128]{2,1,0:T(8,128)(2,1)S(1)}, u32[]{:S(2)}) copy-start(bf16[111,16,128]{2,1,0:T(8,128)(2,1)S(1)} %collective-permute-done.9.refs_2_) | copy-start | bytes 1363972
  142.5 57.8 %collective-permute-start.11 = (bf16[111,16,128]{2,1,0:T(8,128)(2,1)S(1)}, bf16[111,16,128]{2,1,0:T(8,128)(2,1)S(1)}, u32[]{:S(2)}, u32[]{:S(2)}) collective-permute-start(bf16[111,16,128]{2,1,0:T(8,128)(2,1)S(1)} %copy-done.14), channel_id=1, source_target_pairs={{0,22},{2,20},{4,18},{6,16},{8,30},{10,28},{12,26},{14,24},{16,6},... | collective-permute-start | bytes 1363976 | tf_op jit(solution)/shard_map/ppermute | solution.py:396
  157.3 56.3 %collective-permute-start.13 = (bf16[111,16,128]{2,1,0:T(8,128)(2,1)S(1)}, bf16[111,16,128]{2,1,0:T(8,128)(2,1)S(1)}, u32[]{:S(2)}, u32[]{:S(2)}) collective-permute-start(bf16[111,16,128]{2,1,0:T(8,128)(2,1)S(1)} %copy-done.13), channel_id=1, source_target_pairs={{0,30},{2,28},{4,26},{6,24},{8,22},{10,20},{12,18},{14,16},{16,14}... | collective-permute-start | bytes 1363976 | tf_op jit(solution)/shard_map/ppermute | solution.py:396
  194.1 19.5 %copy-start.8 = (bf16[111,16,128]{2,1,0:T(8,128)(2,1)}, bf16[111,16,128]{2,1,0:T(8,128)(2,1)S(1)}, u32[]{:S(2)}) copy-start(bf16[111,16,128]{2,1,0:T(8,128)(2,1)S(1)} %collective-permute-done.12.refs_6_) | copy-start | bytes 1363972
  (9 other events, 29.6 us)

commit v4 on v3

--- a/solution.py
+++ b/solution.py
@@ -100,7 +100,7 @@
         ],
         out_specs=(pl.BlockSpec((1, rows, width), lambda s, k: (s, 0, k)), pl.BlockSpec((8, LANES), lambda s, k: (0, 0))),
         scratch_shapes=[pltpu.VMEM((rows, rows), jnp.bfloat16)],
-        compiler_params=pltpu.CompilerParams(vmem_limit_bytes=60 << 20),
+        compiler_params=pltpu.CompilerParams(vmem_limit_bytes=57 << 20),
         cost_estimate=pl.CostEstimate(
             flops=rows * rows * cols * sexes, bytes_accessed=4 * sexes * rows * cols, transcendentals=0
         ),
@@ -118,74 +118,68 @@
     return jnp.where(low, first[..., s : s + 1, :], second[..., 1 - s : 2 - s, :])
 
 
-def join_kernel(*refs):
-    size = refs[0].shape[0]
-    for i, ref in enumerate(refs[:-1]):
-        refs[-1][i * size : (i + 1) * size, :] = ref[...]
-
-
-def join(parts):
-    rows, cols = parts[0].shape
-    return pl.pallas_call(
-        join_kernel,
-        out_shape=jax.ShapeDtypeStruct((rows * len(parts), cols), parts[0].dtype),
-        compiler_params=pltpu.CompilerParams(vmem_limit_bytes=60 << 20),
-        cost_estimate=pl.CostEstimate(
-            flops=0, bytes_accessed=4 * len(parts) * rows * cols, transcendentals=0
-        ),
-        name="join",
-    )(*parts)
-
-
-def loc_mix_kernel(bits, d_ref, x_ref, l_ref, m0, m1, m2, m3, done_ref, *outs):
-    factor = l_ref[...]
-    crossed = jnp.concatenate(
-        [l_ref[at * HALF : (at + 1) * HALF, :] for at in (1, 0, 3, 2)], 0
-    )
-    means = (m0, m1, m2, m3)
+def loc_mix_kernel(bits, blocks, d_ref, x_ref, *refs):
+    factors, refs = refs[:blocks], refs[blocks:]
+    means, outs, done_ref = refs[:4], refs[5:9], refs[9]
+    if blocks > 1:
+        for i, f in enumerate(factors):
+            refs[10][i * HALF : (i + 1) * HALF, :] = f[...]
+    done_ref[...] = jnp.zeros_like(done_ref)
+    if blocks == 1:
+        parts = [factors[0][i * HALF : (i + 1) * HALF, :] for i in range(4)]
+    else:
+        parts = [f[...] for f in factors]
     ages, rows, _ = outs[0].shape
-    r0 = lax.dot_general(x_ref[0], factor, NT, preferred_element_type=jnp.float32)
-    r1 = lax.dot_general(x_ref[1], crossed, NT, preferred_element_type=jnp.float32)
+    sums = []
+    for s, order in enumerate(((0, 1, 2, 3), (1, 0, 3, 2))):
+        factor = jnp.concatenate([parts[i] for i in order], 0)
+        sums.append(lax.dot_general(x_ref[s], factor, NT, preferred_element_type=jnp.float32))
     low = lax.broadcasted_iota(jnp.int32, (1, LANES), 1) < HALF
     for q in range(4):
         g = (q // 2) * LANES
-        a, b = r0[:, g : g + LANES], r1[:, g : g + LANES]
+        a, b = [x[:, g : g + LANES] for x in sums]
         v = jnp.where(low, a, b) if q % 2 == 0 else jnp.where(low, b, a)
         m = merge_pair(means[q][...], ((d_ref[0] ^ bits[q]) & 1) == 1, q % 2 == 1)
         outs[q][...] = (v.reshape(ages, rows, LANES) + m).astype(jnp.bfloat16)
 
 
-def loc_mix(device, bits, mixed, factor, mean_t, done):
+def loc_mix(device, bits, mixed, factors, mean_t, done):
     sexes, rows, cols = mixed.shape
     ages = mean_t.shape[0]
     steps = 3
     block = ages // steps
     per_age = rows // ages
     msg = jax.ShapeDtypeStruct((ages, per_age, LANES), jnp.bfloat16)
+    flag_spec = pl.BlockSpec(done.shape, lambda i, d: (0, 0))
 
     def mean_spec(q):
         return pl.BlockSpec((block, sexes, LANES), lambda i, d: (i, 0, (d[0] ^ bits[q]) // 2))
 
+    outs = [msg] * 4 + [jax.ShapeDtypeStruct(done.shape, done.dtype)]
+    out_specs = [pl.BlockSpec((block, per_age, LANES), lambda i, d: (i, 0, 0))] * 4 + [flag_spec]
+    if len(factors) > 1:
+        outs.append(jax.ShapeDtypeStruct((4 * HALF, cols), jnp.bfloat16))
+        out_specs.append(pl.BlockSpec((4 * HALF, cols), lambda i, d: (0, 0)))
     return pl.pallas_call(
-        functools.partial(loc_mix_kernel, bits),
-        out_shape=[msg] * 4,
+        functools.partial(loc_mix_kernel, bits, len(factors)),
+        out_shape=outs,
         grid_spec=pltpu.PrefetchScalarGridSpec(
             num_scalar_prefetch=1,
             grid=(steps,),
             in_specs=[pl.BlockSpec((sexes, block * per_age, cols), lambda i, d: (0, i, 0))]
-            + [pl.BlockSpec(factor.shape, lambda i, d: (0, 0))]
+            + [pl.BlockSpec(f.shape, lambda i, d: (0, 0)) for f in factors]
             + [mean_spec(q) for q in range(4)]
-            + [pl.BlockSpec(done.shape, lambda i, d: (0, 0))],
-            out_specs=[pl.BlockSpec((block, per_age, LANES), lambda i, d: (i, 0, 0))] * 4,
-        ),
-        compiler_params=pltpu.CompilerParams(vmem_limit_bytes=60 << 20),
+            + [flag_spec],
+            out_specs=out_specs,
+        ),
+        compiler_params=pltpu.CompilerParams(vmem_limit_bytes=57 << 20),
         cost_estimate=pl.CostEstimate(
             flops=2 * sexes * rows * cols * 256,
             bytes_accessed=2 * sexes * rows * cols + 8 * rows * LANES,
             transcendentals=0,
         ),
         name="loc_mix",
-    )(device, mixed, factor, *([mean_t] * 4), done)
+    )(device, mixed, *factors, *([mean_t] * 4), done)
 
 
 def survive_kernel(bits, first, last, d_ref, *refs):
@@ -315,7 +309,7 @@
             out_specs=out_specs,
             scratch_shapes=scratch,
         ),
-        compiler_params=pltpu.CompilerParams(vmem_limit_bytes=60 << 20),
+        compiler_params=pltpu.CompilerParams(vmem_limit_bytes=57 << 20),
         cost_estimate=pl.CostEstimate(
             flops=60 * 4 * ages * rows * LANES,
             bytes_accessed=16 * ages * rows * LANES,
@@ -365,7 +359,7 @@
             scratch_shapes=[pltpu.VMEM((8, block, rows, LANES), jnp.bfloat16)],
         ),
         input_output_aliases=aliases,
-        compiler_params=pltpu.CompilerParams(vmem_limit_bytes=60 << 20),
+        compiler_params=pltpu.CompilerParams(vmem_limit_bytes=24 << 20),
         cost_estimate=pl.CostEstimate(
             flops=2 * ages * LANES**3, bytes_accessed=32 * ages * rows * LANES, transcendentals=0
         ),
@@ -406,13 +400,20 @@
     mixed, done = age_mix(age_factor, noise.reshape(sexes, ages * rows, locs))
     factors, done = tie(factors, done)
 
-    lane0 = join([factors[b] for b in CHUNKS[0]])
-    lane1 = swap(lane0, 1)
-    lane2 = swap(lane0, 2)
-    lane3 = swap(lane2, 1)
     sent = {}
-    for bits, lane in zip(CHUNKS, (lane0, lane1, lane2, lane3)):
-        sent.update(zip(bits, loc_mix(device, bits, mixed, lane, mean_t, done)))
+
+    def mix(c, lane, done):
+        out = loc_mix(device, CHUNKS[c], mixed, lane, mean_t, done)
+        sent.update(zip(CHUNKS[c], out[:4]))
+        return out[4:]
+
+    done, lane0 = mix(0, [factors[b] for b in CHUNKS[0]], done)
+    lane1, done = tie(swap(lane0, 1), done)
+    lane2, done = tie(swap(lane0, 2), done)
+    (done,) = mix(1, [lane1], done)
+    (done,) = mix(2, [lane2], done)
+    lane3, done = tie(swap(lane2, 1), done)
+    mix(3, [lane3], done)
 
     got = {0: sent[0]}
     first, sent[CHUNKS[3][3]] = tie(sent[CHUNKS[0][0]], sent[CHUNKS[3][3]])
@@ -421,14 +422,11 @@
         message = sent[b]
         if i >= 3:
             message, got[FAR[i - 3]] = tie(message, got[FAR[i - 3]])
-        if 3 <= i < 7:
-            bits = CHUNKS[i - 3]
+        if i >= 4:
+            bits = CHUNKS[i - 4]
             messages = [first if b == CHUNKS[0][0] else sent[b] for b in bits]
-            sums = survive(device, bits, messages, pop_t, region_row, sums, i == 6)
+            sums = survive(device, bits, messages, pop_t, region_row, sums, i == 7)
             message, sums = tie(message, sums)
-        if i == 7:
-            small = exchange(*sums, sexes)
-            message, small = tie(message, small)
         got[b] = swap(message, b)
     for i, b in enumerate(NEAR):
         message = sent[b]
@@ -439,7 +437,7 @@
     shape = jax.ShapeDtypeStruct((sexes, ages, HALF, devices * rows), jnp.bfloat16)
     close = [got[b] for b in range(8)]
     half = turn(device, close, shape, None)
-    loc_survival, region_survival = small
+    loc_survival, region_survival = exchange(*sums, sexes)
     ready = (loc_survival, region_survival)
     log_rates = turn(device, [got[b] for b in range(8, 16)], shape, half, ready)
     return (log_rates, loc_survival, region_survival)

time: 221 us -> 219 us (level); the launches traced: 220 us -> 215 us
  waiting for transfers between devices: 95.8 us -> 38 us
  blocking collectives: 0 us -> 47.4 us
  starting transfers between devices: 33.4 us -> 38.8 us
  local copies, waits for them, and re-layouts: 5.67 us -> 10.9 us
  Pallas kernels: 82.6 us -> 78.4 us
    all_to_all x0 -> x1, blocking collectives: none -> 47.4 us  [exchange(): lax.all_to_all(packed, 'loc', split_axis=0, concat_axis=0, tiled=True)]
    ppermute x21, waiting for transfers between devices: 84.6 us -> 38 us  [swap(): return lax.ppermute(x, 'loc', [(i, i ^ bits) for i in range(devices)])]
    all_to_all x1 -> x0, waiting for transfers between devices: 11.2 us -> none  [exchange(): lax.all_to_all(packed, 'loc', split_axis=0, concat_axis=0, tiled=True)]
    ppermute x21, starting transfers between devices: 28.2 us -> 38.8 us  [swap(): return lax.ppermute(x, 'loc', [(i, i ^ bits) for i in range(devices)])]
    all_to_all x1 -> x0, starting transfers between devices: 5.18 us -> none  [exchange(): lax.all_to_all(packed, 'loc', split_axis=0, concat_axis=0, tiled=True)]
    unnamed x38 -> x42, local copies, waits for them, and re-layouts: 3.16 us -> 8.14 us
    pallas_call x2, Pallas kernels: 11.1 us -> 8.66 us  [turn(): pl.pallas_call(functools.partial(turn_kernel, near), out_shape=out_shape,...]
    pallas_call x5 -> x4, Pallas kernels: 27.2 us -> 25.5 us  [loc_mix(): pl.pallas_call(functools.partial(loc_mix_kernel, bits, len(factors)), out...]
  transfers between devices with their start and end apart: 22 -> 21, of which waited for: 10 -> 3; matrix products, arithmetic and copies ran while one was open for 2% -> 2% of each run, Pallas kernels for 34% -> 31%
where the time goes in v4:
time: 219 us; the launch traced here: 215 us
  Pallas kernels  78.4 us (36%)
  blocking collectives  47.4 us (22%)
  starting transfers between devices  38.8 us (18%)
  waiting for transfers between devices  38 us (17%)
  local copies, waits for them, and re-layouts  10.9 us (5%)
    all_to_all x1, blocking collectives, exchange(): lax.all_to_all(packed, 'loc', split_axis=0, concat_axis=0, tiled=True)  47.4 us
    ppermute x21, starting transfers between devices, swap(): return lax.ppermute(x, 'loc', [(i, i ^ bits) for i in range(devices)])  38.8 us
    ppermute x21, waiting for transfers between devices, swap(): return lax.ppermute(x, 'loc', [(i, i ^ bits) for i in range(devices)])  38 us
    pallas_call x4, Pallas kernels, survive(): pl.pallas_call(functools.partial(survive_kernel, bits, first, last), out_...  31.7 us
    pallas_call x4, Pallas kernels, loc_mix(): pl.pallas_call(functools.partial(loc_mix_kernel, bits, len(factors)), out...  25.5 us
    pallas_call x1, Pallas kernels, age_mix(): pl.pallas_call(age_mix_kernel, out_shape=(jax.ShapeDtypeStruct(noise.shap...  12.5 us
    pallas_call x2, Pallas kernels, turn(): pl.pallas_call(functools.partial(turn_kernel, near), out_shape=out_shape,...  8.66 us
    unnamed x42, local copies, waits for them, and re-layouts  8.14 us
  transfers between devices with their start and end apart: 21, of which 3 were waited for; matrix products, arithmetic and copies ran while one was open for 2% of the time, Pallas kernels for 31%

profile of v4, /device:TPU:17, one launch (start us, length us, event | category | flops | bytes accessed | tf_op | source)
XLA Modules:
  0.0 215.2 jit_solution(7943547913845557340)
XLA Ops:
  0.7 1.4 collective-permute-start
  2.1 1.3 collective-permute-start.2
  3.3 12.5 %age_mix.1 = (bf16[2,1776,1024]{2,1,0:T(8,128)(2,1)}, f32[8,128]{1,0:T(8,128)}) custom-call(bf16[111,111]{1,0:T(8,128)(2,1)} %age_ref.1, bf16[2,1776,1024]{2,1,0:T(8,128)(2,1)} %bitcast.70), custom_call_target="tpu_custom_call" | custom-call | flops 6459752448 | bytes 14548992 | tf_op jit(solution)/shard_map/age_mix/pallas_call | solution.py:93
  16.6 6.5 %loc_mix.4 = (bf16[111,16,128]{2,1,0:T(8,128)(2,1)}, bf16[111,16,128]{2,1,0:T(8,128)(2,1)}, bf16[111,16,128]{2,1,0:T(8,128)(2,1)}, bf16[111,16,128]{2,1,0:T(8,12...) custom-call(s32[1]{0:T(128)} %bitcast.d_ref, bf16[2,1776,1024]{2,1,0:T(8,128)(2,1)} %get-tuple-element.84.x_ref, ...), custom_call_target="tpu_custom_call" | custom-call | flops 1862270976 | bytes 9093120 | tf_op jit(solution)/shard_map/loc_mix/pallas_call | solution.py:163
  23.1 1.6 collective-permute-start.3
  24.7 1.2 collective-permute-start.4
  25.9 2.2 %collective-permute-start.14 = (bf16[111,16,128]{2,1,0:T(8,128)(2,1)}, bf16[111,16,128]{2,1,0:T(8,128)(2,1)S(1)}, u32[]{:S(2)}, u32[]{:S(2)}) collective-permute-start(bf16[111,16,128]{2,1,0:T(8,128)(2,1)} %get-tuple-element.113.refs_2_), channel_id=1, source_target_pairs={{0,8},{2,10},{4,12},{6,14},{8,0},{10,2},{12,4},{14,6},{16,24},{18,... | collective-permute-start | bytes 1363976 | tf_op jit(solution)/shard_map/ppermute | solution.py:390
  28.1 1.2 collective-permute-start.8
  29.3 9.1 %collective-permute-done.4.refs_0_ = bf16[256,1024]{1,0:T(8,128)(2,1)S(1)} collective-permute-done((bf16[256,1024]{1,0:T(8,128)(2,1)}, bf16[256,1024]{1,0:T(8,128)(2,1)S(1)}, u32[]{:S(2)}, u32[]{:S(2)}) %collective-permute-start.4) | collective-permute-done | bytes 524320 | tf_op jit(solution)/shard_map/ppermute | solution.py:390
  39.2 6.3 %loc_mix.5 = (bf16[111,16,128]{2,1,0:T(8,128)(2,1)}, bf16[111,16,128]{2,1,0:T(8,128)(2,1)}, bf16[111,16,128]{2,1,0:T(8,128)(2,1)}, bf16[111,16,128]{2,1,0:T(8,128)(2,1)}, f32[8,128]{1,0:T(8,128)}) custom-call(s32[1]{0:T(128)} %bitcast.d_ref, bf16[2,1776,1024]{2,1,0:T(8,128)(2,1)} %get-tuple-element.84.x_ref, bf16[256,1024]{1,0:T(8,128)(2,1)} %copy-done.15, ...), custom_call_target="tpu_custom_call" | custom-call | flops 1862270976 | bytes 9093120 | tf_op jit(solution)/shard_map/loc_mix/pallas_call | solution.py:163
  45.6 2.3 %collective-permute-start.18 = (bf16[111,16,128]{2,1,0:T(8,128)(2,1)}, bf16[111,16,128]{2,1,0:T(8,128)(2,1)S(1)}, u32[]{:S(2)}, u32[]{:S(2)}) collective-permute-start(bf16[111,16,128]{2,1,0:T(8,128)(2,1)} %get-tuple-element.126.refs_2_), channel_id=1, source_target_pairs={{0,10},{2,8},{4,14},{6,12},{8,2},{10,0},{12,6},{14,4},{16,26},{18,... | collective-permute-start | bytes 1363976 | tf_op jit(solution)/shard_map/ppermute | solution.py:390
  48.2 12.2 %collective-permute-start.10 = (bf16[111,16,128]{2,1,0:T(8,128)(2,1)}, bf16[111,16,128]{2,1,0:T(8,128)(2,1)S(1)}, u32[]{:S(2)}, u32[]{:S(2)}) collective-permute-start(bf16[111,16,128]{2,1,0:T(8,128)(2,1)} %get-tuple-element.121.refs_1_), channel_id=1, source_target_pairs={{0,26},{2,24},{4,30},{6,28},{8,18},{10,16},{12,22},{14,20},{16,10}... | collective-permute-start | bytes 1363976 | tf_op jit(solution)/shard_map/ppermute | solution.py:390
  60.5 6.3 %loc_mix.6 = (bf16[111,16,128]{2,1,0:T(8,128)(2,1)}, bf16[111,16,128]{2,1,0:T(8,128)(2,1)}, bf16[111,16,128]{2,1,0:T(8,128)(2,1)}, bf16[111,16,128]{2,1,0:T(8,128)(2,1)}, f32[8,128]{1,0:T(8,128)}) custom-call(s32[1]{0:T(128)} %bitcast.d_ref, bf16[2,1776,1024]{2,1,0:T(8,128)(2,1)} %get-tuple-element.84.x_ref, bf16[256,1024]{1,0:T(8,128)(2,1)} %copy-done.13, ...), custom_call_target="tpu_custom_call" | custom-call | flops 1862270976 | bytes 9093120 | tf_op jit(solution)/shard_map/loc_mix/pallas_call | solution.py:163
  66.8 12.0 %collective-permute-done.8.refs_4_ = bf16[111,16,128]{2,1,0:T(8,128)(2,1)S(1)} collective-permute-done((bf16[111,16,128]{2,1,0:T(8,128)(2,1)}, bf16[111,16,128]{2,1,0:T(8,128)(2,1)S(1)}, u32[]{:S(2)}, u32[]{:S(2)}) %collective-permute-start.8) | collective-permute-done | bytes 454688 | tf_op jit(solution)/shard_map/ppermute | solution.py:390
  79.1 4.2 %collective-permute-start.19 = (bf16[111,16,128]{2,1,0:T(8,128)(2,1)}, bf16[111,16,128]{2,1,0:T(8,128)(2,1)S(1)}, u32[]{:S(2)}, u32[]{:S(2)}) collective-permute-start(bf16[111,16,128]{2,1,0:T(8,128)(2,1)} %get-tuple-element.160.refs_2_), channel_id=1, source_target_pairs={{0,12},{2,14},{4,8},{6,10},{8,4},{10,6},{12,0},{14,2},{16,28},{18,... | collective-permute-start | bytes 1363976 | tf_op jit(solution)/shard_map/ppermute | solution.py:390
  84.1 6.4 %loc_mix.7 = (bf16[111,16,128]{2,1,0:T(8,128)(2,1)}, bf16[111,16,128]{2,1,0:T(8,128)(2,1)}, bf16[111,16,128]{2,1,0:T(8,128)(2,1)}, bf16[111,16,128]{2,1,0:T(8,128)(2,1)}, f32[8,128]{1,0:T(8,128)}) custom-call(s32[1]{0:T(128)} %bitcast.d_ref, bf16[2,1776,1024]{2,1,0:T(8,128)(2,1)} %get-tuple-element.84.x_ref, bf16[256,1024]{1,0:T(8,128)(2,1)} %copy-done.14, ...), custom_call_target="tpu_custom_call" | custom-call | flops 1862270976 | bytes 9093120 | tf_op jit(solution)/shard_map/loc_mix/pallas_call | solution.py:163
  90.5 7.5 %survive.4 = (f32[16,16,128]{2,1,0:T(8,128)}, f32[1776,128]{1,0:T(8,128)}, f32[111,128]{1,0:T(8,128)}) custom-call(s32[1]{0:T(128)} %bitcast.d_ref, bf16[111,16,128]{2,1,0:T(8,128)(2,1)} %get-tuple-element.112.refs_0_, bf16[111,16,128]{2,1,0:T(8,128)(2,1)} %get-tuple-element.109.refs_1_, bf16[111,16,128]{2,1,0:T(8,128)(2,1)} %get-tuple-element.113.refs_2_, ...), custom_call_target="tpu_custom_call" | custom-call | flops 54558720 | bytes 3637248 | tf_op jit(solution)/shard_map/survive/pallas_call | solution.py:302
  99.0 16.8 %collective-permute-done.6.refs_1_ = bf16[111,16,128]{2,1,0:T(8,128)(2,1)S(1)} collective-permute-done((bf16[111,16,128]{2,1,0:T(8,128)(2,1)S(1)}, bf16[111,16,128]{2,1,0:T(8,128)(2,1)S(1)}, u32[]{:S(2)}, u32[]{:S(2)}) %collective-permute-start.6) | collective-permute-done | bytes 454688 | tf_op jit(solution)/shard_map/ppermute | solution.py:390
  115.8 7.9 %survive.5 = (f32[16,16,128]{2,1,0:T(8,128)}, f32[1776,128]{1,0:T(8,128)}, f32[111,128]{1,0:T(8,128)}) custom-call(s32[1]{0:T(128)} %bitcast.d_ref, bf16[111,16,128]{2,1,0:T(8,128)(2,1)} %get-tuple-element.102.refs_0_, bf16[111,16,128]{2,1,0:T(8,128)(2,1)} %get-tuple-element.121.refs_1_, bf16[111,16,128]{2,1,0:T(8,128)(2,1)} %get-tuple-element.126.refs_2_, ...), custom_call_target="tpu_custom_call" | custom-call | flops 54558720 | bytes 3637248 | tf_op jit(solution)/shard_map/survive/pallas_call | solution.py:302
  123.7 7.9 %survive.6 = (f32[16,16,128]{2,1,0:T(8,128)}, f32[1776,128]{1,0:T(8,128)}, f32[111,128]{1,0:T(8,128)}) custom-call(s32[1]{0:T(128)} %bitcast.d_ref, bf16[111,16,128]{2,1,0:T(8,128)(2,1)} %get-tuple-element.118.refs_0_, bf16[111,16,128]{2,1,0:T(8,128)(2,1)} %get-tuple-element.143.refs_1_, bf16[111,16,128]{2,1,0:T(8,128)(2,1)} %get-tuple-element.160.refs_2_, ...), custom_call_target="tpu_custom_call" | custom-call | flops 54558720 | bytes 3637248 | tf_op jit(solution)/shard_map/survive/pallas_call | solution.py:302
  131.5 3.3 %collective-permute-start.11 = (bf16[111,16,128]{2,1,0:T(8,128)(2,1)}, bf16[111,16,128]{2,1,0:T(8,128)(2,1)S(1)}, u32[]{:S(2)}, u32[]{:S(2)}) collective-permute-start(bf16[111,16,128]{2,1,0:T(8,128)(2,1)} %get-tuple-element.140.refs_0_), channel_id=1, source_target_pairs={{0,22},{2,20},{4,18},{6,16},{8,30},{10,28},{12,26},{14,24},{16,6},... | collective-permute-start | bytes 1363976 | tf_op jit(solution)/shard_map/ppermute | solution.py:390
  134.9 2.1 collective-permute-start.12
  137.0 8.5 %survive.7 = (f32[16,16,128]{2,1,0:T(8,128)}, f32[16,128]{1,0:T(8,128)}) custom-call(s32[1]{0:T(128)} %bitcast.d_ref, bf16[111,16,128]{2,1,0:T(8,128)(2,1)} %get-tuple-element.140.refs_0_, bf16[111,16,128]{2,1,0:T(8,128)(2,1)} %get-tuple-element.152.refs_1_, bf16[111,16,128]{2,1,0:T(8,128)(2,1)} %get-tuple-element.162.refs_2_, ...), custom_call_target="tpu_custom_call" | custom-call | flops 54558720 | bytes 3637248 | tf_op jit(solution)/shard_map/survive/pallas_call | solution.py:302
  146.2 1.8 collective-permute-start.17
  152.1 47.4 %all_to_all.5 = f32[16,17,128]{2,1,0:T(8,128)S(1)} all-to-all(f32[16,17,128]{2,1,0:T(8,128)S(1)} %pad_maximum_fusion), channel_id=1, replica_groups=mesh['loc'=16,'yr'=2] {'loc'}, dimensions={0} | all-to-all | bytes 278528 | tf_op jit(solution)/shard_map/all_to_all | solution.py:376
  201.5 1.0 copy-done.3
  202.5 1.0 copy-done.5
  203.5 1.0 copy-done.7
  204.5 1.0 copy-done.9
  205.5 1.0 copy-done.11
  206.6 4.3 %turn.2.refs_8_ = bf16[2,111,64,256]{3,2,1,0:T(8,128)(2,1)} custom-call(s32[1]{0:T(128)} %bitcast.d_ref, bf16[111,16,128]{2,1,0:T(8,128)(2,1)S(1)} %copy-done, bf16[111,16,128]{2,1,0:T(8,128)(2,1)S(1)} %copy-done.7, bf16[111,16,128]{2,1,0:T(8,128)(2,1)S(1)} %copy-done.9, bf16[111,16,128]{2,1,0:T(8,128)(2,1)} %collective-permute-done.17.refs_3_, ...), custom_call_target="tpu_custom_call" | custom-call | flops 465567744 | bytes 7274496 | tf_op jit(solution)/shard_map/turn/pallas_call | solution.py:351
  210.9 4.3 %turn.3 = bf16[2,111,64,256]{3,2,1,0:T(8,128)(2,1)} custom-call(s32[1]{0:T(128)} %bitcast.d_ref, bf16[111,16,128]{2,1,0:T(8,128)(2,1)S(1)} %collective-permute-done.5.refs_0_, bf16[111,16,128]{2,1,0:T(8,128)(2,1)S(1)} %collective-permute-done.6.refs_1_, bf16[111,16,128]{2,1,0:T(8,128)(2,1)S(1)} %collective-permute-done.9.refs_2_, ...), custom_call_target="tpu_custom_call", output_to_operand_aliasing={{}: (9, {})} | custom-call | flops 465567744 | bytes 7274496 | tf_op jit(solution)/shard_map/turn/pallas_call | solution.py:351
  (74 shorter events, 10.9 us)
Async XLA Ops:
  0.6 15.2 %collective-permute-start.1 = (bf16[64,1024]{1,0:T(8,128)(2,1)}, bf16[64,1024]{1,0:T(8,128)(2,1)S(1)}, u32[]{:S(2)}, u32[]{:S(2)}) collective-permute-start(bf16[64,1024]{1,0:T(8,128)(2,1)} %refs_3_), channel_id=1, source_target_pairs={{0,16},{2,18},{4,20},{6,22},{8,24},{10,26},{12,28},{14,30},{16,0},... | collective-permute-start | bytes 393224 | tf_op jit(solution)/shard_map/ppermute | solution.py:390
  0.7 15.1 %collective-permute-start = (bf16[64,1024]{1,0:T(8,128)(2,1)}, bf16[64,1024]{1,0:T(8,128)(2,1)S(1)}, u32[]{:S(2)}, u32[]{:S(2)}) collective-permute-start(bf16[64,1024]{1,0:T(8,128)(2,1)} %refs_3_), channel_id=1, source_target_pairs={{0,8},{2,10},{4,12},{6,14},{8,0},{10,2},{12,4},{14,6},{16,24},{18,... | collective-permute-start | bytes 393224 | tf_op jit(solution)/shard_map/ppermute | solution.py:390
  2.1 13.8 %collective-permute-start.2 = (bf16[64,1024]{1,0:T(8,128)(2,1)}, bf16[64,1024]{1,0:T(8,128)(2,1)S(1)}, u32[]{:S(2)}, u32[]{:S(2)}) collective-permute-start(bf16[64,1024]{1,0:T(8,128)(2,1)} %refs_3_), channel_id=1, source_target_pairs={{0,24},{2,26},{4,28},{6,30},{8,16},{10,18},{12,20},{14,22},{16,8},... | collective-permute-start | bytes 393224 | tf_op jit(solution)/shard_map/ppermute | solution.py:390
  23.1 6.2 %collective-permute-start.3 = (bf16[256,1024]{1,0:T(8,128)(2,1)}, bf16[256,1024]{1,0:T(8,128)(2,1)S(1)}, u32[]{:S(2)}, u32[]{:S(2)}) collective-permute-start(bf16[256,1024]{1,0:T(8,128)(2,1)} %get-tuple-element.91), channel_id=1, source_target_pairs={{0,2},{2,0},{4,6},{6,4},{8,10},{10,8},{12,14},{14,12},{16,18},{18,... | collective-permute-start | bytes 1572872 | tf_op jit(solution)/shard_map/ppermute | solution.py:390
  24.7 13.7 %collective-permute-start.4 = (bf16[256,1024]{1,0:T(8,128)(2,1)}, bf16[256,1024]{1,0:T(8,128)(2,1)S(1)}, u32[]{:S(2)}, u32[]{:S(2)}) collective-permute-start(bf16[256,1024]{1,0:T(8,128)(2,1)} %get-tuple-element.91), channel_id=1, source_target_pairs={{0,4},{2,6},{4,0},{6,2},{8,12},{10,14},{12,8},{14,10},{16,20},{18,... | collective-permute-start | bytes 1572872 | tf_op jit(solution)/shard_map/ppermute | solution.py:390
  25.9 22.0 %collective-permute-start.14 = (bf16[111,16,128]{2,1,0:T(8,128)(2,1)}, bf16[111,16,128]{2,1,0:T(8,128)(2,1)S(1)}, u32[]{:S(2)}, u32[]{:S(2)}) collective-permute-start(bf16[111,16,128]{2,1,0:T(8,128)(2,1)} %get-tuple-element.113.refs_2_), channel_id=1, source_target_pairs={{0,8},{2,10},{4,12},{6,14},{8,0},{10,2},{12,4},{14,6},{16,24},{18,... | collective-permute-start | bytes 1363976 | tf_op jit(solution)/shard_map/ppermute | solution.py:390
  28.1 20.1 %collective-permute-start.5 = (bf16[111,16,128]{2,1,0:T(8,128)(2,1)}, bf16[111,16,128]{2,1,0:T(8,128)(2,1)S(1)}, u32[]{:S(2)}, u32[]{:S(2)}) collective-permute-start(bf16[111,16,128]{2,1,0:T(8,128)(2,1)} %get-tuple-element.112.refs_0_), channel_id=1, source_target_pairs={{0,16},{2,18},{4,20},{6,22},{8,24},{10,26},{12,28},{14,30},{16,0},... | collective-permute-start | bytes 1363976 | tf_op jit(solution)/shard_map/ppermute | solution.py:390
  28.1 50.7 %collective-permute-start.8 = (bf16[111,16,128]{2,1,0:T(8,128)(2,1)}, bf16[111,16,128]{2,1,0:T(8,128)(2,1)S(1)}, u32[]{:S(2)}, u32[]{:S(2)}) collective-permute-start(bf16[111,16,128]{2,1,0:T(8,128)(2,1)} %get-tuple-element.109.refs_1_), channel_id=1, source_target_pairs={{0,24},{2,26},{4,28},{6,30},{8,16},{10,18},{12,20},{14,22},{16,8},... | collective-permute-start | bytes 1363976 | tf_op jit(solution)/shard_map/ppermute | solution.py:390
  29.3 10.0 %copy-start.15 = (bf16[256,1024]{1,0:T(8,128)(2,1)}, bf16[256,1024]{1,0:T(8,128)(2,1)S(1)}, u32[]{:S(2)}) copy-start(bf16[256,1024]{1,0:T(8,128)(2,1)S(1)} %collective-permute-done.3.refs_0_) | copy-start | bytes 1572868
  38.4 22.1 %copy-start.13 = (bf16[256,1024]{1,0:T(8,128)(2,1)}, bf16[256,1024]{1,0:T(8,128)(2,1)S(1)}, u32[]{:S(2)}) copy-start(bf16[256,1024]{1,0:T(8,128)(2,1)S(1)} %collective-permute-done.4.refs_0_) | copy-start | bytes 1572868
  38.4 44.9 %collective-permute-start.7 = (bf16[256,1024]{1,0:T(8,128)(2,1)S(1)}, bf16[256,1024]{1,0:T(8,128)(2,1)S(1)}, u32[]{:S(2)}, u32[]{:S(2)}) collective-permute-start(bf16[256,1024]{1,0:T(8,128)(2,1)S(1)} %collective-permute-done.4.refs_0_), channel_id=1, source_target_pairs={{0,2},{2,0},{4,6},{6,4},{8,10},{10,8},{12,14},{14,12},{16,18},{18,... | collective-permute-start | bytes 1572872 | tf_op jit(solution)/shard_map/ppermute | solution.py:390
  45.6 33.2 %copy-start.17 = (bf16[111,16,128]{2,1,0:T(8,128)(2,1)S(1)}, bf16[111,16,128]{2,1,0:T(8,128)(2,1)}, u32[]{:S(2)}) copy-start(bf16[111,16,128]{2,1,0:T(8,128)(2,1)} %get-tuple-element.102.refs_0_) | copy-start | bytes 1363972
  45.6 33.2 %collective-permute-start.18 = (bf16[111,16,128]{2,1,0:T(8,128)(2,1)}, bf16[111,16,128]{2,1,0:T(8,128)(2,1)S(1)}, u32[]{:S(2)}, u32[]{:S(2)}) collective-permute-start(bf16[111,16,128]{2,1,0:T(8,128)(2,1)} %get-tuple-element.126.refs_2_), channel_id=1, source_target_pairs={{0,10},{2,8},{4,14},{6,12},{8,2},{10,0},{12,6},{14,4},{16,26},{18,... | collective-permute-start | bytes 1363976 | tf_op jit(solution)/shard_map/ppermute | solution.py:390
  47.9 42.6 %copy-start.2 = (bf16[111,16,128]{2,1,0:T(8,128)(2,1)}, bf16[111,16,128]{2,1,0:T(8,128)(2,1)S(1)}, u32[]{:S(2)}) copy-start(bf16[111,16,128]{2,1,0:T(8,128)(2,1)S(1)} %collective-permute-done.14.refs_4_) | copy-start | bytes 1363972
  47.9 30.9 %collective-permute-start.15 = (bf16[111,16,128]{2,1,0:T(8,128)(2,1)}, bf16[111,16,128]{2,1,0:T(8,128)(2,1)S(1)}, u32[]{:S(2)}, u32[]{:S(2)}) collective-permute-start(bf16[111,16,128]{2,1,0:T(8,128)(2,1)} %get-tuple-element.153.refs_3_), channel_id=1, source_target_pairs={{0,2},{2,0},{4,6},{6,4},{8,10},{10,8},{12,14},{14,12},{16,18},{18,... | collective-permute-start | bytes 1363976 | tf_op jit(solution)/shard_map/ppermute | solution.py:390
  48.2 67.6 %collective-permute-start.10 = (bf16[111,16,128]{2,1,0:T(8,128)(2,1)}, bf16[111,16,128]{2,1,0:T(8,128)(2,1)S(1)}, u32[]{:S(2)}, u32[]{:S(2)}) collective-permute-start(bf16[111,16,128]{2,1,0:T(8,128)(2,1)} %get-tuple-element.121.refs_1_), channel_id=1, source_target_pairs={{0,26},{2,24},{4,30},{6,28},{8,18},{10,16},{12,22},{14,20},{16,10}... | collective-permute-start | bytes 1363976 | tf_op jit(solution)/shard_map/ppermute | solution.py:390
  78.8 37.0 %collective-permute-start.6 = (bf16[111,16,128]{2,1,0:T(8,128)(2,1)S(1)}, bf16[111,16,128]{2,1,0:T(8,128)(2,1)S(1)}, u32[]{:S(2)}, u32[]{:S(2)}) collective-permute-start(bf16[111,16,128]{2,1,0:T(8,128)(2,1)S(1)} %copy-done.17), channel_id=1, source_target_pairs={{0,18},{2,16},{4,22},{6,20},{8,26},{10,24},{12,30},{14,28},{16,2},... | collective-permute-start | bytes 1363976 | tf_op jit(solution)/shard_map/ppermute | solution.py:390
  78.8 19.2 %copy-start.4 = (bf16[111,16,128]{2,1,0:T(8,128)(2,1)}, bf16[111,16,128]{2,1,0:T(8,128)(2,1)S(1)}, u32[]{:S(2)}) copy-start(bf16[111,16,128]{2,1,0:T(8,128)(2,1)S(1)} %collective-permute-done.18.refs_5_) | copy-start | bytes 1363972
  78.8 19.2 %copy-start.6 = (bf16[111,16,128]{2,1,0:T(8,128)(2,1)}, bf16[111,16,128]{2,1,0:T(8,128)(2,1)S(1)}, u32[]{:S(2)}) copy-start(bf16[111,16,128]{2,1,0:T(8,128)(2,1)S(1)} %collective-permute-done.15.refs_1_) | copy-start | bytes 1363972
  78.8 66.7 %collective-permute-start.16 = (bf16[111,16,128]{2,1,0:T(8,128)(2,1)}, bf16[111,16,128]{2,1,0:T(8,128)(2,1)S(1)}, u32[]{:S(2)}, u32[]{:S(2)}) collective-permute-start(bf16[111,16,128]{2,1,0:T(8,128)(2,1)} %get-tuple-element.155.refs_3_), channel_id=1, source_target_pairs={{0,4},{2,6},{4,0},{6,2},{8,12},{10,14},{12,8},{14,10},{16,20},{18,... | collective-permute-start | bytes 1363976 | tf_op jit(solution)/shard_map/ppermute | solution.py:390
  79.1 68.9 %collective-permute-start.19 = (bf16[111,16,128]{2,1,0:T(8,128)(2,1)}, bf16[111,16,128]{2,1,0:T(8,128)(2,1)S(1)}, u32[]{:S(2)}, u32[]{:S(2)}) collective-permute-start(bf16[111,16,128]{2,1,0:T(8,128)(2,1)} %get-tuple-element.160.refs_2_), channel_id=1, source_target_pairs={{0,12},{2,14},{4,8},{6,10},{8,4},{10,6},{12,0},{14,2},{16,28},{18,... | collective-permute-start | bytes 1363976 | tf_op jit(solution)/shard_map/ppermute | solution.py:390
  84.1 13.9 %copy-start.16 = (bf16[111,16,128]{2,1,0:T(8,128)(2,1)S(1)}, bf16[111,16,128]{2,1,0:T(8,128)(2,1)}, u32[]{:S(2)}) copy-start(bf16[111,16,128]{2,1,0:T(8,128)(2,1)} %get-tuple-element.118.refs_0_) | copy-start | bytes 1363972
  98.0 51.3 %collective-permute-start.9 = (bf16[111,16,128]{2,1,0:T(8,128)(2,1)S(1)}, bf16[111,16,128]{2,1,0:T(8,128)(2,1)S(1)}, u32[]{:S(2)}, u32[]{:S(2)}) collective-permute-start(bf16[111,16,128]{2,1,0:T(8,128)(2,1)S(1)} %copy-done.16), channel_id=1, source_target_pairs={{0,20},{2,22},{4,16},{6,18},{8,28},{10,30},{12,24},{14,26},{16,4},... | collective-permute-start | bytes 1363976 | tf_op jit(solution)/shard_map/ppermute | solution.py:390
  123.7 77.8 %copy-start = (bf16[111,16,128]{2,1,0:T(8,128)(2,1)S(1)}, bf16[111,16,128]{2,1,0:T(8,128)(2,1)}, u32[]{:S(2)}) copy-start(bf16[111,16,128]{2,1,0:T(8,128)(2,1)} %get-tuple-element.114.refs_3_.refs_0_) | copy-start | bytes 1363972
  131.5 79.3 %collective-permute-start.11 = (bf16[111,16,128]{2,1,0:T(8,128)(2,1)}, bf16[111,16,128]{2,1,0:T(8,128)(2,1)S(1)}, u32[]{:S(2)}, u32[]{:S(2)}) collective-permute-start(bf16[111,16,128]{2,1,0:T(8,128)(2,1)} %get-tuple-element.140.refs_0_), channel_id=1, source_target_pairs={{0,22},{2,20},{4,18},{6,16},{8,30},{10,28},{12,26},{14,24},{16,6},... | collective-permute-start | bytes 1363976 | tf_op jit(solution)/shard_map/ppermute | solution.py:390
  134.9 76.0 %collective-permute-start.12 = (bf16[111,16,128]{2,1,0:T(8,128)(2,1)}, bf16[111,16,128]{2,1,0:T(8,128)(2,1)}, u32[]{:S(2)}, u32[]{:S(2)}) collective-permute-start(bf16[111,16,128]{2,1,0:T(8,128)(2,1)} %get-tuple-element.143.refs_1_), channel_id=1, source_target_pairs={{0,28},{2,30},{4,24},{6,26},{8,20},{10,22},{12,16},{14,18},{16,12}... | collective-permute-start | bytes 1363976 | tf_op jit(solution)/shard_map/ppermute | solution.py:390
  146.2 55.2 %collective-permute-start.17 = (bf16[111,16,128]{2,1,0:T(8,128)(2,1)}, bf16[111,16,128]{2,1,0:T(8,128)(2,1)}, u32[]{:S(2)}, u32[]{:S(2)}) collective-permute-start(bf16[111,16,128]{2,1,0:T(8,128)(2,1)} %get-tuple-element.157.refs_3_), channel_id=1, source_target_pairs={{0,6},{2,4},{4,2},{6,0},{8,14},{10,12},{12,10},{14,8},{16,22},{18,... | collective-permute-start | bytes 1363976 | tf_op jit(solution)/shard_map/ppermute | solution.py:390
  148.8 52.6 %collective-permute-start.20 = (bf16[111,16,128]{2,1,0:T(8,128)(2,1)}, bf16[111,16,128]{2,1,0:T(8,128)(2,1)}, u32[]{:S(2)}, u32[]{:S(2)}) collective-permute-start(bf16[111,16,128]{2,1,0:T(8,128)(2,1)} %get-tuple-element.162.refs_2_), channel_id=1, source_target_pairs={{0,14},{2,12},{4,10},{6,8},{8,6},{10,4},{12,2},{14,0},{16,30},{18,... | collective-permute-start | bytes 1363976 | tf_op jit(solution)/shard_map/ppermute | solution.py:390
  150.2 60.6 %collective-permute-start.13 = (bf16[111,16,128]{2,1,0:T(8,128)(2,1)}, bf16[111,16,128]{2,1,0:T(8,128)(2,1)}, u32[]{:S(2)}, u32[]{:S(2)}) collective-permute-start(bf16[111,16,128]{2,1,0:T(8,128)(2,1)} %get-tuple-element.152.refs_1_), channel_id=1, source_target_pairs={{0,30},{2,28},{4,26},{6,24},{8,22},{10,20},{12,18},{14,16},{16,14}... | collective-permute-start | bytes 1363976 | tf_op jit(solution)/shard_map/ppermute | solution.py:390
  201.2 14.1 %copy-start.1 = (f32[256,128]{0,1:T(8,128)}, f32[256,128]{0,1:T(8,128)S(1)}, u32[]{:S(2)}) copy-start(f32[256,128]{0,1:T(8,128)S(1)} %copy.15) | copy-start | bytes 393220
  201.4 13.8 %copy-start.12 = (f32[2,4,256]{2,1,0:T(4,128)}, f32[2,4,256]{2,1,0:T(4,128)S(1)}, u32[]{:S(2)}) copy-start(f32[2,4,256]{2,1,0:T(4,128)S(1)} %reshape.33.refs_10_) | copy-start | bytes 24580
  201.5 1.0 copy-start.3
  (10 other events, 8.5 us)

commit v5 on v4

v5 whole, which is shorter than its diff:
```python
import functools

import jax
import jax.numpy as jnp
from jax import lax
from jax.experimental import pallas as pl
from jax.experimental.pallas import tpu as pltpu
from jax.sharding import PartitionSpec as P

REGIONS = 64
LANES = 128
HALF = 64
NT = (((1,), (1,)), ((), ()))
CHUNKS = ((8, 12, 4, 0), (9, 13, 5, 1), (10, 14, 6, 2), (11, 15, 7, 3))
FAR = (8, 12, 9, 13, 10, 14, 11, 15)
NEAR = (4, 5, 1, 6, 2, 7, 3)
LONG = pl.CostEstimate(flops=20_000_000_000, bytes_accessed=1000, transcendentals=0)


def survival(rates):
    hazard = jnp.cumsum(rates, axis=1)
    after = jnp.exp(-hazard)
    total = 0.5 + jnp.sum(after, axis=1) - 0.5 * after[:, -1]
    return total / rates.shape[1]


def shards_any(noise, loc_factor, age_factor, mean_rate, population, region_of):
    highest = lax.Precision.HIGHEST
    spread = jnp.einsum(
        "sark,lk->sarl",
        noise,
        lax.all_gather(loc_factor, "loc", axis=0, tiled=True),
        preferred_element_type=jnp.float32,
    ).astype(jnp.bfloat16)
    mixed = jnp.einsum("ab,sbrl->sarl", age_factor, spread, preferred_element_type=jnp.float32)
    log_section = (mean_rate[:, :, None, :] + mixed).astype(jnp.bfloat16)
    rates = jnp.exp(log_section.astype(jnp.float32))
    onehot = (region_of == jnp.arange(REGIONS, dtype=jnp.int32)[None, :]).astype(jnp.float32)
    totals = jnp.einsum("sal,lg->sag", population, onehot, precision=highest)
    weighted = jnp.einsum(
        "sarl,lg->sarg", population[:, :, None, :] * rates, onehot, precision=highest
    )
    region_section = survival(weighted / totals[:, :, None, :])
    region_moved = lax.all_to_all(region_section, "loc", split_axis=2, concat_axis=1, tiled=True)
    region_survival = jnp.transpose(region_moved, (0, 2, 1))
    turned = jnp.transpose(
        lax.all_to_all(log_section, "loc", split_axis=3, concat_axis=2, tiled=True), (0, 1, 3, 2)
    )
    loc_survival = survival(jnp.exp(turned.astype(jnp.float32)))
    return (turned, loc_survival, region_survival)


def tie(x, other):
    return lax.optimization_barrier((x, other))


def split_bf16(x):
    hi = x.astype(jnp.bfloat16)
    return hi, (x - hi.astype(jnp.float32)).astype(jnp.bfloat16)


def age_mix_kernel(age_ref, x_ref, o_ref, done_ref, wide_ref):
    ages = age_ref.shape[0]
    rows = x_ref.shape[1]
    step = 256

    @pl.when(jnp.logical_and(pl.program_id(0) == 0, pl.program_id(1) == 0))
    def _():
        pick = lax.broadcasted_iota(jnp.int32, (rows, ages), 0) >> 4
        pick = (pick == lax.broadcasted_iota(jnp.int32, (rows, ages), 1)).astype(jnp.bfloat16)
        tall = jnp.dot(pick, age_ref[...], preferred_element_type=jnp.float32).astype(jnp.bfloat16)
        spread = lax.broadcasted_iota(jnp.int32, (ages, rows), 1) >> 4
        spread = (spread == lax.broadcasted_iota(jnp.int32, (ages, rows), 0)).astype(jnp.bfloat16)
        for lo in range(0, rows, step):
            hi = min(lo + step, rows)
            both = jnp.dot(tall[lo:hi], spread[:, :hi], preferred_element_type=jnp.float32)
            same = (lax.broadcasted_iota(jnp.int32, both.shape, 0) & 15) == (
                lax.broadcasted_iota(jnp.int32, both.shape, 1) & 15
            )
            wide_ref[lo:hi, :hi] = jnp.where(same, both, 0.0).astype(jnp.bfloat16)

    done_ref[...] = jnp.zeros_like(done_ref)
    for lo in range(0, rows, step):
        hi = min(lo + step, rows)
        o_ref[0, lo:hi, :] = jnp.dot(
            wide_ref[lo:hi, :hi], x_ref[0, :hi, :], preferred_element_type=jnp.float32
        ).astype(jnp.bfloat16)


def age_mix(age_factor, noise):
    sexes, rows, cols = noise.shape
    ages = age_factor.shape[0]
    width = 512
    return pl.pallas_call(
        age_mix_kernel,
        out_shape=(jax.ShapeDtypeStruct(noise.shape, jnp.bfloat16), jax.ShapeDtypeStruct((8, LANES), jnp.float32)),
        grid=(sexes, cols // width),
        in_specs=[
            pl.BlockSpec((ages, ages), lambda s, k: (0, 0)),
            pl.BlockSpec((1, rows, width), lambda s, k: (s, 0, k)),
        ],
        out_specs=(pl.BlockSpec((1, rows, width), lambda s, k: (s, 0, k)), pl.BlockSpec((8, LANES), lambda s, k: (0, 0))),
        scratch_shapes=[pltpu.VMEM((rows, rows), jnp.bfloat16)],
        compiler_params=pltpu.CompilerParams(vmem_limit_bytes=57 << 20),
        cost_estimate=LONG,
        name="age_mix",
    )(age_factor, noise)


def merge_pair(pair, odd_device, swapped):
    axis = pair.ndim - 1
    turned = pltpu.roll(pair, HALF, axis)
    first = jnp.where(odd_device, turned, pair)
    second = jnp.where(odd_device, pair, turned)
    low = lax.broadcasted_iota(jnp.int32, pair.shape[:-2] + (1, LANES), axis) < HALF
    s = 1 if swapped else 0
    return jnp.where(low, first[..., s : s + 1, :], second[..., 1 - s : 2 - s, :])


def loc_mix_kernel(groups, blocks, d_ref, x_ref, *refs):
    factors, refs = refs[:blocks], refs[blocks:]
    count = 4 * len(groups)
    means, outs, done_ref = refs[:count], refs[count + 1 : 2 * count + 1], refs[2 * count + 1]
    done_ref[...] = jnp.zeros_like(done_ref)
    if blocks > len(groups):
        joined_ref = refs[2 * count + 2]
        for i, f in enumerate(factors):
            joined_ref[i * HALF : (i + 1) * HALF, :] = f[...]
        factors = (joined_ref,)
    ages, rows, _ = outs[0].shape
    low = lax.broadcasted_iota(jnp.int32, (1, LANES), 1) < HALF
    for c, bits in enumerate(groups):
        parts = [factors[c][i * HALF : (i + 1) * HALF, :] for i in range(4)]
        sums = []
        for s, order in enumerate(((0, 1, 2, 3), (1, 0, 3, 2))):
            factor = jnp.concatenate([parts[i] for i in order], 0)
            sums.append(lax.dot_general(x_ref[s], factor, NT, preferred_element_type=jnp.float32))
        for q in range(4):
            g = (q // 2) * LANES
            a, b = [x[:, g : g + LANES] for x in sums]
            v = jnp.where(low, a, b) if q % 2 == 0 else jnp.where(low, b, a)
            at = 4 * c + q
            m = merge_pair(means[at][...], ((d_ref[0] ^ bits[q]) & 1) == 1, q % 2 == 1)
            outs[at][...] = (v.reshape(ages, rows, LANES) + m).astype(jnp.bfloat16)


def loc_mix(device, groups, mixed, factors, mean_t, done):
    sexes, rows, cols = mixed.shape
    ages = mean_t.shape[0]
    steps = 3
    block = ages // steps
    per_age = rows // ages
    every = [b for bits in groups for b in bits]
    msg = pltpu.HBM((ages, per_age, LANES), jnp.bfloat16)
    flag_spec = pl.BlockSpec(done.shape, lambda i, d: (0, 0))

    def mean_spec(b):
        return pl.BlockSpec((block, sexes, LANES), lambda i, d: (i, 0, (d[0] ^ b) // 2))

    outs = [msg] * len(every) + [jax.ShapeDtypeStruct(done.shape, done.dtype)]
    out_specs = [pl.BlockSpec((block, per_age, LANES), lambda i, d: (i, 0, 0))] * len(every) + [flag_spec]
    if len(factors) > len(groups):
        outs.append(jax.ShapeDtypeStruct((4 * HALF, cols), jnp.bfloat16))
        out_specs.append(pl.BlockSpec((4 * HALF, cols), lambda i, d: (0, 0)))
    return pl.pallas_call(
        functools.partial(loc_mix_kernel, groups, len(factors)),
        out_shape=outs,
        grid_spec=pltpu.PrefetchScalarGridSpec(
            num_scalar_prefetch=1,
            grid=(steps,),
            in_specs=[pl.BlockSpec((sexes, block * per_age, cols), lambda i, d: (0, i, 0))]
            + [pl.BlockSpec(f.shape, lambda i, d: (0, 0)) for f in factors]
            + [mean_spec(b) for b in every]
            + [flag_spec],
            out_specs=out_specs,
        ),
        compiler_params=pltpu.CompilerParams(vmem_limit_bytes=57 << 20),
        cost_estimate=LONG,
        name="loc_mix",
    )(device, mixed, *factors, *([mean_t] * len(every)), done)


def survive_kernel(d_ref, *refs):
    count = 4 * len(CHUNKS)
    xs, pops, regs = refs[:count], refs[count : 2 * count], refs[2 * count : 3 * count]
    locs, region_ref, hi_ref, lo_ref, pop_ref, wsum_ref, psum_ref = refs[3 * count :]
    ages, rows, _ = xs[0].shape
    zero = jnp.zeros((rows, LANES), jnp.float32)
    lane = lax.broadcasted_iota(jnp.int32, (1, LANES), 1)
    low = lane < HALF
    for c, bits in enumerate(CHUNKS):
        dests = [d_ref[0] ^ b for b in bits]
        odd = [(e & 1) == 1 for e in dests]
        first = 4 * c

        def age_step(a, carry):
            hazards, totals = carry
            new_h, new_t = [], []
            at = pl.ds(pl.multiple_of(a * rows, rows), rows)
            for q in range(4):
                lanes = slice(q * LANES, (q + 1) * LANES)
                rate = jnp.exp(xs[first + q][a].astype(jnp.float32))
                h = hazards[q] + rate
                new_h.append(h)
                new_t.append(totals[q] + jnp.exp(-h))
                pop = merge_pair(pops[first + q][a], odd[q], q % 2 == 1)
                pop_ref[q, pl.ds(a, 1), :] = pop
                hi, lo = split_bf16(rate * pop)
                hi_ref[at, lanes] = hi
                lo_ref[at, lanes] = lo
            return tuple(new_h), tuple(new_t)

        hazards, totals = lax.fori_loop(0, ages, age_step, ((zero,) * 4, (zero,) * 4), unroll=3)
        onehots = []
        for q in range(4):
            out = (totals[q] + (0.5 - 0.5 * jnp.exp(-hazards[q]))) * (1.0 / ages)
            if q % 2 == 1:
                out = pltpu.roll(out, HALF, 1)
            locs[dests[q]] = out
            pair = regs[first + q][...]
            turned = pltpu.roll(pair, HALF, 1)
            mine = jnp.where(low, jnp.where(odd[q], turned, pair), jnp.where(odd[q], pair, turned))
            upper = low if q % 2 == 1 else jnp.logical_not(low)
            target = mine + jnp.where(upper, REGIONS, 0)
            region = lax.broadcasted_iota(jnp.int32, (LANES, LANES), 0)
            onehots.append(jnp.where(region == target, 1.0, 0.0).astype(jnp.bfloat16))
        onehot = jnp.concatenate(onehots, 1)

        def regions(x):
            return lax.dot_general(x, onehot, NT, preferred_element_type=jnp.float32)

        pop_hi, pop_lo = split_bf16(jnp.concatenate([pop_ref[q] for q in range(4)], 1))
        wsum = regions(hi_ref[...]) + regions(lo_ref[...])
        psum = regions(pop_hi) + regions(pop_lo)
        if c > 0:
            wsum = wsum + wsum_ref[...]
            psum = psum + psum_ref[...]
        wsum_ref[...] = wsum
        psum_ref[...] = psum

    def region_step(a, carry):
        h, t = carry
        at = pl.ds(pl.multiple_of(a * rows, rows), rows)
        h = h + wsum_ref[at, :] / psum_ref[pl.ds(a, 1), :]
        return h, t + jnp.exp(-h)

    h, t = lax.fori_loop(0, ages, region_step, (zero, zero), unroll=3)
    region_ref[...] = (t + (0.5 - 0.5 * jnp.exp(-h))) * (1.0 / ages)


def survive(device, sent, pop_t, region_row):
    every = [b for bits in CHUNKS for b in bits]
    ages, rows, _ = sent[0].shape
    sexes, locs = pop_t.shape[1], pop_t.shape[2] // HALF
    f32 = jnp.float32
    whole = lambda *shape: pl.BlockSpec(shape, lambda i, d: (0,) * len(shape))

    def pop_spec(b):
        return pl.BlockSpec((ages, sexes, LANES), lambda i, d: (0, 0, (d[0] ^ b) // 2))

    def region_spec(b):
        return pl.BlockSpec((1, LANES), lambda i, d: (0, (d[0] ^ b) // 2))

    return pl.pallas_call(
        survive_kernel,
        out_shape=(
            jax.ShapeDtypeStruct((locs, rows, LANES), f32),
            jax.ShapeDtypeStruct((rows, LANES), f32),
        ),
        grid_spec=pltpu.PrefetchScalarGridSpec(
            num_scalar_prefetch=1,
            grid=(1,),
            in_specs=[whole(ages, rows, LANES)] * len(every)
            + [pop_spec(b) for b in every]
            + [region_spec(b) for b in every],
            out_specs=(whole(locs, rows, LANES), whole(rows, LANES)),
            scratch_shapes=[
                pltpu.VMEM((ages * rows, 4 * LANES), jnp.bfloat16),
                pltpu.VMEM((ages * rows, 4 * LANES), jnp.bfloat16),
                pltpu.VMEM((4, ages, LANES), f32),
                pltpu.VMEM((ages * rows, LANES), f32),
                pltpu.VMEM((ages, LANES), f32),
            ],
        ),
        compiler_params=pltpu.CompilerParams(vmem_limit_bytes=57 << 20),
        cost_estimate=LONG,
        name="survive",
    )(device, *[sent[b] for b in every], *([pop_t] * len(every)), *([region_row] * len(every)))


def turn_kernel(near, d_ref, *refs):
    xs, out_ref, order_ref = refs[:8], refs[-2], refs[-1]
    d = d_ref[0]
    ages = xs[0].shape[0]
    for m in range(8):
        order_ref[(d & 7) ^ m] = xs[m][...]
    upper = (lax.broadcasted_iota(jnp.int32, (HALF, LANES), 1) >= HALF).astype(jnp.int32)
    swapped = (upper ^ ((d >> 2) & 1) ^ (1 if near else 0)) == 1
    for a in range(ages):
        tile = order_ref[:, a].reshape(LANES, LANES)
        t = tile.T.astype(jnp.float32)
        top, bottom = t[:HALF], t[HALF:]
        out_ref[0, a] = jnp.where(swapped, bottom, top).astype(jnp.bfloat16)
        out_ref[1, a] = jnp.where(swapped, top, bottom).astype(jnp.bfloat16)


def turn(device, messages, out_shape, previous, ready=()):
    near = previous is None
    ages, rows, _ = messages[0].shape
    steps = 3
    block = ages // steps
    in_specs = [pl.BlockSpec((block, rows, LANES), lambda i, d: (i, 0, 0))] * 8
    args = list(messages)
    flip = 0 if near else 1
    aliases = {}
    if not near:
        in_specs += [pl.BlockSpec(memory_space=pl.ANY)] * (1 + len(ready))
        args += [previous, *ready]
        aliases = {9: 0}
    return pl.pallas_call(
        functools.partial(turn_kernel, near),
        out_shape=out_shape,
        grid_spec=pltpu.PrefetchScalarGridSpec(
            num_scalar_prefetch=1,
            grid=(steps,),
            in_specs=in_specs,
            out_specs=pl.BlockSpec((2, block, HALF, LANES), lambda i, d: (0, i, 0, (d[0] // 8) ^ flip)),
            scratch_shapes=[pltpu.VMEM((8, block, rows, LANES), jnp.bfloat16)],
        ),
        input_output_aliases=aliases,
        compiler_params=pltpu.CompilerParams(vmem_limit_bytes=(57 if near else 24) << 20),
        cost_estimate=LONG,
        name="turn",
    )(device, *args)


def exchange(by_device, region_part, sexes):
    devices, rows, _ = by_device.shape
    mine = REGIONS // devices
    region_out = region_part.reshape(rows, sexes, devices, mine)
    region_out = jnp.transpose(region_out, (2, 1, 3, 0)).reshape(devices, 1, sexes * mine * rows)
    packed = jnp.concatenate([by_device, region_out], axis=1)
    small = lax.all_to_all(packed, "loc", split_axis=0, concat_axis=0, tiled=True)
    loc_survival = jnp.transpose(small[:, :rows].reshape(devices * rows, LANES), (1, 0))
    region_survival = jnp.transpose(
        small[:, rows].reshape(devices, sexes, mine, rows), (1, 2, 0, 3)
    ).reshape(sexes, mine, devices * rows)
    return loc_survival.reshape(sexes, HALF, devices * rows), region_survival


def shards_sixteen(noise, loc_factor, age_factor, mean_rate, population, region_of):
    sexes, ages, rows, locs = noise.shape
    devices = lax.axis_size("loc")
    here = lax.axis_index("loc")

    def swap(x, bits):
        return lax.ppermute(x, "loc", [(i, i ^ bits) for i in range(devices)])

    mean_t = jnp.transpose(mean_rate, (1, 0, 2))
    pop_t = jnp.transpose(population, (1, 0, 2))
    region_row = region_of.reshape(1, locs)
    device = here[None]

    factors = {0: loc_factor}
    for bits in (8, 12, 4):
        factors[bits] = swap(loc_factor, bits)
    mixed, done = age_mix(age_factor, noise.reshape(sexes, ages * rows, locs))
    factors, done = tie(factors, done)

    sent = {}

    def mix(groups, lanes, done):
        out = loc_mix(device, groups, mixed, lanes, mean_t, done)
        count = 4 * len(groups)
        sent.update(zip([b for bits in groups for b in bits], out[:count]))
        return out[count:]

    done, lane0 = mix(CHUNKS[:1], [factors[b] for b in CHUNKS[0]], done)
    lanes = [swap(lane0, bits) for bits in (1, 2, 3)]
    (done,) = mix(CHUNKS[1:2], lanes[:1], done)
    lanes, done = tie(lanes, done)
    (done,) = mix(CHUNKS[2:], lanes[1:], done)

    got = {0: sent[0]}
    for i, b in enumerate(NEAR):
        message = sent[b]
        if i >= 2:
            message, got[NEAR[i - 2]] = tie(message, got[NEAR[i - 2]])
        got[b] = swap(message, b)
    sums = None
    for i, b in enumerate(FAR):
        message = sent[b]
        if i >= 2:
            ahead = FAR[max(i - 3, min(i - 2, 1))]
            message, got[ahead] = tie(message, got[ahead])
        if i == 5:
            sums = survive(device, sent, pop_t, region_row)
            message, sums = tie(message, sums)
        if i == 7:
            small = exchange(*sums, sexes)
            message, small = tie(message, small)
        got[b] = swap(message, b)

    shape = jax.ShapeDtypeStruct((sexes, ages, HALF, devices * rows), jnp.bfloat16)
    close = [got[b] for b in range(8)]
    half = turn(device, close, shape, None)
    loc_survival, region_survival = small
    ready = (loc_survival, region_survival)
    log_rates = turn(device, [got[b] for b in range(8, 16)], shape, half, ready)
    return (log_rates, loc_survival, region_survival)


def shards(noise, loc_factor, *rest):
    sixteen = lax.axis_size("loc") == 16 and noise.shape[2] == 16 and noise.shape[1] % 3 == 0
    if sixteen and noise.shape[0] == 2 and loc_factor.shape == (HALF, 1024):
        return shards_sixteen(noise, loc_factor, *rest)
    return shards_any(noise, loc_factor, *rest)


def solution(mesh):
    placed = (
        P(None, None, ("yr", "loc"), None),
        P("loc", None),
        P(),
        P("yr", None, None),
        P("yr", None, None),
        P(),
    )
    return jax.shard_map(
        shards,
        mesh=mesh,
        in_specs=placed,
        out_specs=(P(None, None, "loc", "yr"), P(None, "loc", "yr"), P(None, "loc", "yr")),
        check_vma=False,
    )
```

time: 219 us -> 211 us (0.963); the launches traced: 215 us -> 210 us
  waiting for transfers between devices: 38 us -> 97.9 us
  blocking collectives: 47.4 us -> 0 us
  Pallas kernels: 78.4 us -> 70.2 us
  local copies, waits for them, and re-layouts: 10.9 us -> 4.19 us
  starting transfers between devices: 38.8 us -> 34.7 us
    all_to_all x1 -> x0, blocking collectives: 47.4 us -> none  [exchange(): lax.all_to_all(packed, 'loc', split_axis=0, concat_axis=0, tiled=True)]
    ppermute x21, waiting for transfers between devices: 38 us -> 77.6 us  [swap(): return lax.ppermute(x, 'loc', [(i, i ^ bits) for i in range(devices)])]
    all_to_all x0 -> x1, waiting for transfers between devices: none -> 20.3 us  [exchange(): lax.all_to_all(packed, 'loc', split_axis=0, concat_axis=0, tiled=True)]
    ppermute x21, starting transfers between devices: 38.8 us -> 30.8 us  [swap(): return lax.ppermute(x, 'loc', [(i, i ^ bits) for i in range(devices)])]
    pallas_call x8 -> x4, Pallas kernels: 57.2 us -> 49.2 us  [the longest x1 28.5 us: survive(): pl.pallas_call(survive_kernel, out_shape=(jax.ShapeDtypeStruct((locs, row...]
    unnamed x42 -> x28, local copies, waits for them, and re-layouts: 8.14 us -> 1.38 us
    all_to_all x0 -> x1, starting transfers between devices: none -> 3.97 us  [exchange(): lax.all_to_all(packed, 'loc', split_axis=0, concat_axis=0, tiled=True)]
  transfers between devices with their start and end apart: 21 -> 22, of which waited for: 3 -> 8; matrix products, arithmetic and copies ran while one was open for 2% -> 2% of each run, Pallas kernels for 31% -> 29%
where the time goes in v5:
time: 211 us; the launch traced here: 210 us
  waiting for transfers between devices  97.9 us (46%)
  Pallas kernels  70.2 us (33%)
  starting transfers between devices  34.7 us (16%)
  local copies, waits for them, and re-layouts  4.19 us (2%)
    ppermute x21, waiting for transfers between devices, swap(): return lax.ppermute(x, 'loc', [(i, i ^ bits) for i in range(devices)])  77.6 us
    ppermute x21, starting transfers between devices, swap(): return lax.ppermute(x, 'loc', [(i, i ^ bits) for i in range(devices)])  30.8 us
    pallas_call x1, Pallas kernels, survive(): pl.pallas_call(survive_kernel, out_shape=(jax.ShapeDtypeStruct((locs, row...  28.5 us
    pallas_call x3, Pallas kernels, loc_mix(): pl.pallas_call(functools.partial(loc_mix_kernel, groups, len(factors)), o...  20.7 us
    all_to_all x1, waiting for transfers between devices, exchange(): lax.all_to_all(packed, 'loc', split_axis=0, concat_axis=0, tiled=True)  20.3 us
    pallas_call x1, Pallas kernels, age_mix(): pl.pallas_call(age_mix_kernel, out_shape=(jax.ShapeDtypeStruct(noise.shap...  12.5 us
    pallas_call x2, Pallas kernels, turn(): pl.pallas_call(functools.partial(turn_kernel, near), out_shape=out_shape,...  8.53 us
  transfers between devices with their start and end apart: 22, of which 8 were waited for; matrix products, arithmetic and copies ran while one was open for 2% of the time, Pallas kernels for 29%

profile of v5, /device:TPU:17, one launch (start us, length us, event | category | flops | bytes accessed | tf_op | source)
XLA Modules:
  0.0 209.5 jit_solution(14741401078142035336)
XLA Ops:
  0.7 1.4 collective-permute-start
  2.1 1.3 collective-permute-start.2
  3.3 12.5 %age_mix.1 = (bf16[2,1776,1024]{2,1,0:T(8,128)(2,1)}, f32[8,128]{1,0:T(8,128)}) custom-call(bf16[111,111]{1,0:T(8,128)(2,1)} %age_ref.1, bf16[2,1776,1024]{2,1,0:T(8,128)(2,1)} %bitcast.22), custom_call_target="tpu_custom_call" | custom-call | flops 20000000000 | bytes 1000 | tf_op jit(solution)/shard_map/age_mix/pallas_call | solution.py:94
  16.6 6.3 %loc_mix.3 = (bf16[111,16,128]{2,1,0:T(8,128)(2,1)}, bf16[111,16,128]{2,1,0:T(8,128)(2,1)}, bf16[111,16,128]{2,1,0:T(8,128)(2,1)}, bf16[111,16,128]{2,1,0:T(8,12...) custom-call(s32[1]{0:T(128)} %bitcast.d_ref, bf16[2,1776,1024]{2,1,0:T(8,128)(2,1)} %get-tuple-element.62.x_ref, ...), custom_call_target="tpu_custom_call" | custom-call | flops 20000000000 | bytes 1000 | tf_op jit(solution)/shard_map/loc_mix/pallas_call | solution.py:165
  22.9 1.6 collective-permute-start.3
  24.5 1.2 collective-permute-start.6
  26.7 2.6 %collective-permute-start.8 = (bf16[111,16,128]{2,1,0:T(8,128)(2,1)}, bf16[111,16,128]{2,1,0:T(8,128)(2,1)S(1)}, u32[]{:S(2)}, u32[]{:S(2)}) collective-permute-start(bf16[111,16,128]{2,1,0:T(8,128)(2,1)} %get-tuple-element.84.refs_1_), channel_id=1, source_target_pairs={{0,24},{2,26},{4,28},{6,30},{8,16},{10,18},{12,20},{14,22},{16,8},... | collective-permute-start | bytes 1363976 | tf_op jit(solution)/shard_map/ppermute | solution.py:357
  30.1 6.3 %loc_mix.4 = (bf16[111,16,128]{2,1,0:T(8,128)(2,1)}, bf16[111,16,128]{2,1,0:T(8,128)(2,1)}, bf16[111,16,128]{2,1,0:T(8,128)(2,1)}, bf16[111,16,128]{2,1,0:T(8,128)(2,1)}, f32[8,128]{1,0:T(8,128)}) custom-call(s32[1]{0:T(128)} %bitcast.d_ref, bf16[2,1776,1024]{2,1,0:T(8,128)(2,1)} %get-tuple-element.62.x_ref, bf16[256,1024]{1,0:T(8,128)(2,1)} %copy-done.4, ...), custom_call_target="tpu_custom_call" | custom-call | flops 20000000000 | bytes 1000 | tf_op jit(solution)/shard_map/loc_mix/pallas_call | solution.py:165
  36.4 2.8 %collective-permute-done.6.refs_1_ = bf16[256,1024]{1,0:T(8,128)(2,1)S(1)} collective-permute-done((bf16[256,1024]{1,0:T(8,128)(2,1)}, bf16[256,1024]{1,0:T(8,128)(2,1)S(1)}, u32[]{:S(2)}, u32[]{:S(2)}) %collective-permute-start.6) | collective-permute-done | bytes 524320 | tf_op jit(solution)/shard_map/ppermute | solution.py:357
  39.2 10.1 %collective-permute-done.5.refs_0_ = bf16[256,1024]{1,0:T(8,128)(2,1)S(1)} collective-permute-done((bf16[256,1024]{1,0:T(8,128)(2,1)}, bf16[256,1024]{1,0:T(8,128)(2,1)S(1)}, u32[]{:S(2)}, u32[]{:S(2)}) %collective-permute-start.5) | collective-permute-done | bytes 524320 | tf_op jit(solution)/shard_map/ppermute | solution.py:357
  49.3 8.7 %collective-permute-done.14.refs_4_ = bf16[111,16,128]{2,1,0:T(8,128)(2,1)S(1)} collective-permute-done((bf16[111,16,128]{2,1,0:T(8,128)(2,1)}, bf16[111,16,128]{2,1,0:T(8,128)(2,1)S(1)}, u32[]{:S(2)}, u32[]{:S(2)}) %collective-permute-start.14) | collective-permute-done | bytes 454688 | tf_op jit(solution)/shard_map/ppermute | solution.py:357
  58.0 1.9 collective-permute-start.15
  59.9 2.1 collective-permute-start.18
  61.9 8.1 %loc_mix.5 = (bf16[111,16,128]{2,1,0:T(8,128)(2,1)}, bf16[111,16,128]{2,1,0:T(8,128)(2,1)}, bf16[111,16,128]{2,1,0:T(8,128)(2,1)}, bf16[111,16,128]{2,1,0:T(8,12...) custom-call(s32[1]{0:T(128)} %bitcast.d_ref, ...), custom_call_target="tpu_custom_call" | custom-call | flops 20000000000 | bytes 1000 | tf_op jit(solution)/shard_map/loc_mix/pallas_call | solution.py:165
  71.0 1.9 collective-permute-start.10
  72.8 1.8 collective-permute-start.7
  74.7 1.8 collective-permute-start.19
  76.5 28.5 %survive.1 = (f32[16,16,128]{2,1,0:T(8,128)}, f32[16,128]{1,0:T(8,128)}) custom-call(s32[1]{0:T(128)} %bitcast.d_ref, bf16[111,16,128]{2,1,0:T(8,128)(2,1)} %get-tuple-element.72.refs_0_, bf16[111,16,128]{2,1,0:T(8,128)(2,1)} %get-tuple-element.84.refs_1_, bf16[111,16,128]{2,1,0:T(8,128)(2,1)} %get-tuple-element.94.refs_2_, ...), custom_call_target="tpu_custom_call" | custom-call | flops 20000000000 | bytes 1000 | tf_op jit(solution)/shard_map/survive/pallas_call | solution.py:264
  105.0 24.5 %collective-permute-done.7.refs_1_ = bf16[111,16,128]{2,1,0:T(8,128)(2,1)S(1)} collective-permute-done((bf16[111,16,128]{2,1,0:T(8,128)(2,1)S(1)}, bf16[111,16,128]{2,1,0:T(8,128)(2,1)S(1)}, u32[]{:S(2)}, u32[]{:S(2)}) %collective-permute-start.7) | collective-permute-done | bytes 454688 | tf_op jit(solution)/shard_map/ppermute | solution.py:357
  130.5 1.4 collective-permute-start.17
  131.9 3.8 %collective-permute-start.20 = (bf16[111,16,128]{2,1,0:T(8,128)(2,1)}, bf16[111,16,128]{2,1,0:T(8,128)(2,1)}, u32[]{:S(2)}, u32[]{:S(2)}) collective-permute-start(bf16[111,16,128]{2,1,0:T(8,128)(2,1)} %get-tuple-element.118.refs_14_), channel_id=1, source_target_pairs={{0,14},{2,12},{4,10},{6,8},{8,6},{10,4},{12,2},{14,0},{16,30},{18,... | collective-permute-start | bytes 1363976 | tf_op jit(solution)/shard_map/ppermute | solution.py:357
  135.8 1.6 pad_maximum_fusion
  137.3 4.0 %all-to-all-start = ((f32[16,17,128]{2,1,0:T(8,128)}), f32[16,17,128]{2,1,0:T(8,128)S(1)}, u32[]{:S(2)}, u32[]{:S(2)}) async-start(f32[16,17,128]{2,1,0:T(8,128)} %pad_maximum_fusion), calls=%async_computation | async-start | bytes 393216 | tf_op jit(solution)/shard_map/all_to_all | solution.py:343
  141.3 1.5 collective-permute-start.11
  142.8 2.1 collective-permute-start.12
  144.9 20.3 %all-to-all-done = f32[16,17,128]{2,1,0:T(8,128)S(1)} async-done(((f32[16,17,128]{2,1,0:T(8,128)}), f32[16,17,128]{2,1,0:T(8,128)S(1)}, u32[]{:S(2)}, u32[]{:S(2)}) %all-to-all-start) | async-done | bytes 139296 | tf_op jit(solution)/shard_map/all_to_all | solution.py:343
  167.2 2.3 %collective-permute-start.13 = (bf16[111,16,128]{2,1,0:T(8,128)(2,1)}, bf16[111,16,128]{2,1,0:T(8,128)(2,1)S(1)}, u32[]{:S(2)}, u32[]{:S(2)}) collective-permute-start(bf16[111,16,128]{2,1,0:T(8,128)(2,1)} %get-tuple-element.108.refs_13_), channel_id=1, source_target_pairs={{0,30},{2,28},{4,26},{6,24},{8,22},{10,20},{12,18},{14,16},{16,14}... | collective-permute-start | bytes 1363976 | tf_op jit(solution)/shard_map/ppermute | solution.py:357
  169.5 5.6 %turn.2.refs_8_ = bf16[2,111,64,256]{3,2,1,0:T(8,128)(2,1)} custom-call(s32[1]{0:T(128)} %bitcast.d_ref, bf16[111,16,128]{2,1,0:T(8,128)(2,1)} %get-tuple-element.95.refs_3_.refs_0_, bf16[111,16,128]{2,1,0:T(8,128)(2,1)} %copy-done.6, bf16[111,16,128]{2,1,0:T(8,128)(2,1)} %copy-done.9, bf16[111,16,128]{2,1,0:T(8,128)(2,1)} %collective-permute-done.17.refs_3_, ...), custom_call_target="tpu_custom_call" | custom-call | flops 20000000000 | bytes 1000 | tf_op jit(solution)/shard_map/turn/pallas_call | solution.py:320
  175.0 9.8 %collective-permute-done.11.refs_3_ = bf16[111,16,128]{2,1,0:T(8,128)(2,1)S(1)} collective-permute-done((bf16[111,16,128]{2,1,0:T(8,128)(2,1)}, bf16[111,16,128]{2,1,0:T(8,128)(2,1)S(1)}, u32[]{:S(2)}, u32[]{:S(2)}) %collective-permute-start.11) | collective-permute-done | bytes 454688 | tf_op jit(solution)/shard_map/ppermute | solution.py:357
  184.8 12.0 %collective-permute-done.12.refs_6_ = bf16[111,16,128]{2,1,0:T(8,128)(2,1)S(1)} collective-permute-done((bf16[111,16,128]{2,1,0:T(8,128)(2,1)}, bf16[111,16,128]{2,1,0:T(8,128)(2,1)S(1)}, u32[]{:S(2)}, u32[]{:S(2)}) %collective-permute-start.12) | collective-permute-done | bytes 454688 | tf_op jit(solution)/shard_map/ppermute | solution.py:357
  196.8 9.7 %collective-permute-done.13.refs_7_ = bf16[111,16,128]{2,1,0:T(8,128)(2,1)S(1)} collective-permute-done((bf16[111,16,128]{2,1,0:T(8,128)(2,1)}, bf16[111,16,128]{2,1,0:T(8,128)(2,1)S(1)}, u32[]{:S(2)}, u32[]{:S(2)}) %collective-permute-start.13) | collective-permute-done | bytes 454688 | tf_op jit(solution)/shard_map/ppermute | solution.py:357
  206.5 3.0 %turn.3 = bf16[2,111,64,256]{3,2,1,0:T(8,128)(2,1)} custom-call(s32[1]{0:T(128)} %bitcast.d_ref, bf16[111,16,128]{2,1,0:T(8,128)(2,1)S(1)} %collective-permute-done.4.refs_0_, bf16[111,16,128]{2,1,0:T(8,128)(2,1)S(1)} %collective-permute-done.7.refs_1_, bf16[111,16,128]{2,1,0:T(8,128)(2,1)S(1)} %collective-permute-done.9.refs_2_, ...), custom_call_target="tpu_custom_call", output_to_operand_aliasing={{}: (9, {})} | custom-call | flops 20000000000 | bytes 1000 | tf_op jit(solution)/shard_map/turn/pallas_call | solution.py:320
  (57 shorter events, 6.4 us)
Async XLA Ops:
  0.6 15.2 %collective-permute-start.1 = (bf16[64,1024]{1,0:T(8,128)(2,1)}, bf16[64,1024]{1,0:T(8,128)(2,1)S(1)}, u32[]{:S(2)}, u32[]{:S(2)}) collective-permute-start(bf16[64,1024]{1,0:T(8,128)(2,1)} %refs_3_), channel_id=1, source_target_pairs={{0,16},{2,18},{4,20},{6,22},{8,24},{10,26},{12,28},{14,30},{16,0},... | collective-permute-start | bytes 393224 | tf_op jit(solution)/shard_map/ppermute | solution.py:357
  0.7 15.1 %collective-permute-start = (bf16[64,1024]{1,0:T(8,128)(2,1)}, bf16[64,1024]{1,0:T(8,128)(2,1)S(1)}, u32[]{:S(2)}, u32[]{:S(2)}) collective-permute-start(bf16[64,1024]{1,0:T(8,128)(2,1)} %refs_3_), channel_id=1, source_target_pairs={{0,8},{2,10},{4,12},{6,14},{8,0},{10,2},{12,4},{14,6},{16,24},{18,... | collective-permute-start | bytes 393224 | tf_op jit(solution)/shard_map/ppermute | solution.py:357
  2.1 13.8 %collective-permute-start.2 = (bf16[64,1024]{1,0:T(8,128)(2,1)}, bf16[64,1024]{1,0:T(8,128)(2,1)S(1)}, u32[]{:S(2)}, u32[]{:S(2)}) collective-permute-start(bf16[64,1024]{1,0:T(8,128)(2,1)} %refs_3_), channel_id=1, source_target_pairs={{0,24},{2,26},{4,28},{6,30},{8,16},{10,18},{12,20},{14,22},{16,8},... | collective-permute-start | bytes 393224 | tf_op jit(solution)/shard_map/ppermute | solution.py:357
  22.9 6.4 %collective-permute-start.3 = (bf16[256,1024]{1,0:T(8,128)(2,1)}, bf16[256,1024]{1,0:T(8,128)(2,1)S(1)}, u32[]{:S(2)}, u32[]{:S(2)}) collective-permute-start(bf16[256,1024]{1,0:T(8,128)(2,1)} %get-tuple-element.69), channel_id=1, source_target_pairs={{0,2},{2,0},{4,6},{6,4},{8,10},{10,8},{12,14},{14,12},{16,18},{18,... | collective-permute-start | bytes 1572872 | tf_op jit(solution)/shard_map/ppermute | solution.py:357
  24.5 14.7 %collective-permute-start.6 = (bf16[256,1024]{1,0:T(8,128)(2,1)}, bf16[256,1024]{1,0:T(8,128)(2,1)S(1)}, u32[]{:S(2)}, u32[]{:S(2)}) collective-permute-start(bf16[256,1024]{1,0:T(8,128)(2,1)} %get-tuple-element.69), channel_id=1, source_target_pairs={{0,6},{2,4},{4,2},{6,0},{8,14},{10,12},{12,10},{14,8},{16,22},{18,... | collective-permute-start | bytes 1572872 | tf_op jit(solution)/shard_map/ppermute | solution.py:357
  25.7 23.6 %collective-permute-start.5 = (bf16[256,1024]{1,0:T(8,128)(2,1)}, bf16[256,1024]{1,0:T(8,128)(2,1)S(1)}, u32[]{:S(2)}, u32[]{:S(2)}) collective-permute-start(bf16[256,1024]{1,0:T(8,128)(2,1)} %get-tuple-element.69), channel_id=1, source_target_pairs={{0,4},{2,6},{4,0},{6,2},{8,12},{10,14},{12,8},{14,10},{16,20},{18,... | collective-permute-start | bytes 1572872 | tf_op jit(solution)/shard_map/ppermute | solution.py:357
  25.9 44.1 %collective-permute-start.4 = (bf16[111,16,128]{2,1,0:T(8,128)(2,1)}, bf16[111,16,128]{2,1,0:T(8,128)(2,1)S(1)}, u32[]{:S(2)}, u32[]{:S(2)}) collective-permute-start(bf16[111,16,128]{2,1,0:T(8,128)(2,1)} %get-tuple-element.72.refs_0_), channel_id=1, source_target_pairs={{0,16},{2,18},{4,20},{6,22},{8,24},{10,26},{12,28},{14,30},{16,0},... | collective-permute-start | bytes 1363976 | tf_op jit(solution)/shard_map/ppermute | solution.py:357
  26.7 43.4 %collective-permute-start.8 = (bf16[111,16,128]{2,1,0:T(8,128)(2,1)}, bf16[111,16,128]{2,1,0:T(8,128)(2,1)S(1)}, u32[]{:S(2)}, u32[]{:S(2)}) collective-permute-start(bf16[111,16,128]{2,1,0:T(8,128)(2,1)} %get-tuple-element.84.refs_1_), channel_id=1, source_target_pairs={{0,24},{2,26},{4,28},{6,30},{8,16},{10,18},{12,20},{14,22},{16,8},... | collective-permute-start | bytes 1363976 | tf_op jit(solution)/shard_map/ppermute | solution.py:357
  29.3 28.7 %collective-permute-start.14 = (bf16[111,16,128]{2,1,0:T(8,128)(2,1)}, bf16[111,16,128]{2,1,0:T(8,128)(2,1)S(1)}, u32[]{:S(2)}, u32[]{:S(2)}) collective-permute-start(bf16[111,16,128]{2,1,0:T(8,128)(2,1)} %get-tuple-element.94.refs_2_), channel_id=1, source_target_pairs={{0,8},{2,10},{4,12},{6,14},{8,0},{10,2},{12,4},{14,6},{16,24},{18,... | collective-permute-start | bytes 1363976 | tf_op jit(solution)/shard_map/ppermute | solution.py:357
  39.2 22.8 %copy-start.2 = (bf16[256,1024]{1,0:T(8,128)(2,1)}, bf16[256,1024]{1,0:T(8,128)(2,1)S(1)}, u32[]{:S(2)}) copy-start(bf16[256,1024]{1,0:T(8,128)(2,1)S(1)} %collective-permute-done.6.refs_1_) | copy-start | bytes 1572868
  49.3 12.7 %copy-start.3 = (bf16[256,1024]{1,0:T(8,128)(2,1)}, bf16[256,1024]{1,0:T(8,128)(2,1)S(1)}, u32[]{:S(2)}) copy-start(bf16[256,1024]{1,0:T(8,128)(2,1)S(1)} %collective-permute-done.5.refs_0_) | copy-start | bytes 1572868
  58.0 12.0 %copy-start.5 = (bf16[111,16,128]{2,1,0:T(8,128)(2,1)}, bf16[111,16,128]{2,1,0:T(8,128)(2,1)S(1)}, u32[]{:S(2)}) copy-start(bf16[111,16,128]{2,1,0:T(8,128)(2,1)S(1)} %collective-permute-done.14.refs_4_) | copy-start | bytes 1363972
  58.0 16.6 %collective-permute-start.15 = (bf16[111,16,128]{2,1,0:T(8,128)(2,1)}, bf16[111,16,128]{2,1,0:T(8,128)(2,1)S(1)}, u32[]{:S(2)}, u32[]{:S(2)}) collective-permute-start(bf16[111,16,128]{2,1,0:T(8,128)(2,1)} %get-tuple-element.109.refs_7_), channel_id=1, source_target_pairs={{0,2},{2,0},{4,6},{6,4},{8,10},{10,8},{12,14},{14,12},{16,18},{18,... | collective-permute-start | bytes 1363976 | tf_op jit(solution)/shard_map/ppermute | solution.py:357
  59.9 11.1 %copy-start.8 = (bf16[111,16,128]{2,1,0:T(8,128)(2,1)S(1)}, bf16[111,16,128]{2,1,0:T(8,128)(2,1)}, u32[]{:S(2)}) copy-start(bf16[111,16,128]{2,1,0:T(8,128)(2,1)} %get-tuple-element.89.refs_5_) | copy-start | bytes 1363972
  59.9 12.9 %copy-start.10 = (bf16[111,16,128]{2,1,0:T(8,128)(2,1)S(1)}, bf16[111,16,128]{2,1,0:T(8,128)(2,1)}, u32[]{:S(2)}) copy-start(bf16[111,16,128]{2,1,0:T(8,128)(2,1)} %get-tuple-element.79.refs_4_) | copy-start | bytes 1363972
  59.9 14.8 %collective-permute-start.18 = (bf16[111,16,128]{2,1,0:T(8,128)(2,1)}, bf16[111,16,128]{2,1,0:T(8,128)(2,1)S(1)}, u32[]{:S(2)}, u32[]{:S(2)}) collective-permute-start(bf16[111,16,128]{2,1,0:T(8,128)(2,1)} %get-tuple-element.96.refs_6_), channel_id=1, source_target_pairs={{0,10},{2,8},{4,14},{6,12},{8,2},{10,0},{12,6},{14,4},{16,26},{18,... | collective-permute-start | bytes 1363976 | tf_op jit(solution)/shard_map/ppermute | solution.py:357
  70.1 71.2 %collective-permute-start.9 = (bf16[111,16,128]{2,1,0:T(8,128)(2,1)}, bf16[111,16,128]{2,1,0:T(8,128)(2,1)S(1)}, u32[]{:S(2)}, u32[]{:S(2)}) collective-permute-start(bf16[111,16,128]{2,1,0:T(8,128)(2,1)} %get-tuple-element.86.refs_8_), channel_id=1, source_target_pairs={{0,20},{2,22},{4,16},{6,18},{8,28},{10,30},{12,24},{14,26},{16,4},... | collective-permute-start | bytes 1363976 | tf_op jit(solution)/shard_map/ppermute | solution.py:357
  71.0 70.4 %collective-permute-start.10 = (bf16[111,16,128]{2,1,0:T(8,128)(2,1)S(1)}, bf16[111,16,128]{2,1,0:T(8,128)(2,1)S(1)}, u32[]{:S(2)}, u32[]{:S(2)}) collective-permute-start(bf16[111,16,128]{2,1,0:T(8,128)(2,1)S(1)} %copy-done.8), channel_id=1, source_target_pairs={{0,26},{2,24},{4,30},{6,28},{8,18},{10,16},{12,22},{14,20},{16,10}... | collective-permute-start | bytes 1363976 | tf_op jit(solution)/shard_map/ppermute | solution.py:357
  72.8 56.7 %collective-permute-start.7 = (bf16[111,16,128]{2,1,0:T(8,128)(2,1)S(1)}, bf16[111,16,128]{2,1,0:T(8,128)(2,1)S(1)}, u32[]{:S(2)}, u32[]{:S(2)}) collective-permute-start(bf16[111,16,128]{2,1,0:T(8,128)(2,1)S(1)} %copy-done.10), channel_id=1, source_target_pairs={{0,18},{2,16},{4,22},{6,20},{8,26},{10,24},{12,30},{14,28},{16,2},... | collective-permute-start | bytes 1363976 | tf_op jit(solution)/shard_map/ppermute | solution.py:357
  74.6 30.4 %copy-start.6 = (bf16[111,16,128]{2,1,0:T(8,128)(2,1)}, bf16[111,16,128]{2,1,0:T(8,128)(2,1)S(1)}, u32[]{:S(2)}) copy-start(bf16[111,16,128]{2,1,0:T(8,128)(2,1)S(1)} %collective-permute-done.15.refs_1_) | copy-start | bytes 1363972
  74.6 55.8 %collective-permute-start.16 = (bf16[111,16,128]{2,1,0:T(8,128)(2,1)}, bf16[111,16,128]{2,1,0:T(8,128)(2,1)S(1)}, u32[]{:S(2)}, u32[]{:S(2)}) collective-permute-start(bf16[111,16,128]{2,1,0:T(8,128)(2,1)} %get-tuple-element.111.refs_11_), channel_id=1, source_target_pairs={{0,4},{2,6},{4,0},{6,2},{8,12},{10,14},{12,8},{14,10},{16,20},{18,... | collective-permute-start | bytes 1363976 | tf_op jit(solution)/shard_map/ppermute | solution.py:357
  74.7 30.3 %copy-start.7 = (bf16[111,16,128]{2,1,0:T(8,128)(2,1)}, bf16[111,16,128]{2,1,0:T(8,128)(2,1)S(1)}, u32[]{:S(2)}) copy-start(bf16[111,16,128]{2,1,0:T(8,128)(2,1)S(1)} %collective-permute-done.18.refs_5_) | copy-start | bytes 1363972
  74.7 57.2 %collective-permute-start.19 = (bf16[111,16,128]{2,1,0:T(8,128)(2,1)}, bf16[111,16,128]{2,1,0:T(8,128)(2,1)}, u32[]{:S(2)}, u32[]{:S(2)}) collective-permute-start(bf16[111,16,128]{2,1,0:T(8,128)(2,1)} %get-tuple-element.116.refs_10_), channel_id=1, source_target_pairs={{0,12},{2,14},{4,8},{6,10},{8,4},{10,6},{12,0},{14,2},{16,28},{18,... | collective-permute-start | bytes 1363976 | tf_op jit(solution)/shard_map/ppermute | solution.py:357
  130.5 10.9 %copy-start.9 = (bf16[111,16,128]{2,1,0:T(8,128)(2,1)}, bf16[111,16,128]{2,1,0:T(8,128)(2,1)S(1)}, u32[]{:S(2)}) copy-start(bf16[111,16,128]{2,1,0:T(8,128)(2,1)S(1)} %collective-permute-done.16.refs_2_) | copy-start | bytes 1363972
  130.5 39.0 %collective-permute-start.17 = (bf16[111,16,128]{2,1,0:T(8,128)(2,1)}, bf16[111,16,128]{2,1,0:T(8,128)(2,1)}, u32[]{:S(2)}, u32[]{:S(2)}) collective-permute-start(bf16[111,16,128]{2,1,0:T(8,128)(2,1)} %get-tuple-element.113.refs_15_), channel_id=1, source_target_pairs={{0,6},{2,4},{4,2},{6,0},{8,14},{10,12},{12,10},{14,8},{16,22},{18,... | collective-permute-start | bytes 1363976 | tf_op jit(solution)/shard_map/ppermute | solution.py:357
  131.9 37.5 %collective-permute-start.20 = (bf16[111,16,128]{2,1,0:T(8,128)(2,1)}, bf16[111,16,128]{2,1,0:T(8,128)(2,1)}, u32[]{:S(2)}, u32[]{:S(2)}) collective-permute-start(bf16[111,16,128]{2,1,0:T(8,128)(2,1)} %get-tuple-element.118.refs_14_), channel_id=1, source_target_pairs={{0,14},{2,12},{4,10},{6,8},{8,6},{10,4},{12,2},{14,0},{16,30},{18,... | collective-permute-start | bytes 1363976 | tf_op jit(solution)/shard_map/ppermute | solution.py:357
  137.3 27.9 %all-to-all-start = ((f32[16,17,128]{2,1,0:T(8,128)}), f32[16,17,128]{2,1,0:T(8,128)S(1)}, u32[]{:S(2)}, u32[]{:S(2)}) async-start(f32[16,17,128]{2,1,0:T(8,128)} %pad_maximum_fusion), calls=%async_computation | async-start | bytes 393216 | tf_op jit(solution)/shard_map/all_to_all | solution.py:343
  141.3 43.5 %collective-permute-start.11 = (bf16[111,16,128]{2,1,0:T(8,128)(2,1)}, bf16[111,16,128]{2,1,0:T(8,128)(2,1)S(1)}, u32[]{:S(2)}, u32[]{:S(2)}) collective-permute-start(bf16[111,16,128]{2,1,0:T(8,128)(2,1)} %get-tuple-element.90.refs_12_), channel_id=1, source_target_pairs={{0,22},{2,20},{4,18},{6,16},{8,30},{10,28},{12,26},{14,24},{16,6},... | collective-permute-start | bytes 1363976 | tf_op jit(solution)/shard_map/ppermute | solution.py:357
  142.8 54.0 %collective-permute-start.12 = (bf16[111,16,128]{2,1,0:T(8,128)(2,1)}, bf16[111,16,128]{2,1,0:T(8,128)(2,1)S(1)}, u32[]{:S(2)}, u32[]{:S(2)}) collective-permute-start(bf16[111,16,128]{2,1,0:T(8,128)(2,1)} %get-tuple-element.104.refs_9_), channel_id=1, source_target_pairs={{0,28},{2,30},{4,24},{6,26},{8,20},{10,22},{12,16},{14,18},{16,12}... | collective-permute-start | bytes 1363976 | tf_op jit(solution)/shard_map/ppermute | solution.py:357
  166.9 39.7 %copy-start = (f32[256,128]{0,1:T(8,128)}, f32[256,128]{0,1:T(8,128)S(1)}, u32[]{:S(2)}) copy-start(f32[256,128]{0,1:T(8,128)S(1)} %copy.15) | copy-start | bytes 393220
  167.1 39.4 %copy-start.1 = (f32[2,4,256]{2,1,0:T(4,128)}, f32[2,4,256]{2,1,0:T(4,128)S(1)}, u32[]{:S(2)}) copy-start(f32[2,4,256]{2,1,0:T(4,128)S(1)} %reshape.33.refs_10_) | copy-start | bytes 24580
  167.2 39.4 %collective-permute-start.13 = (bf16[111,16,128]{2,1,0:T(8,128)(2,1)}, bf16[111,16,128]{2,1,0:T(8,128)(2,1)S(1)}, u32[]{:S(2)}, u32[]{:S(2)}) collective-permute-start(bf16[111,16,128]{2,1,0:T(8,128)(2,1)} %get-tuple-element.108.refs_13_), channel_id=1, source_target_pairs={{0,30},{2,28},{4,26},{6,24},{8,22},{10,20},{12,18},{14,16},{16,14}... | collective-permute-start | bytes 1363976 | tf_op jit(solution)/shard_map/ppermute | solution.py:357
  (4 other events, 2.8 us)

commit v6 on v5

--- a/solution.py
+++ b/solution.py
@@ -183,7 +183,7 @@
 def survive_kernel(d_ref, *refs):
     count = 4 * len(CHUNKS)
     xs, pops, regs = refs[:count], refs[count : 2 * count], refs[2 * count : 3 * count]
-    locs, region_ref, hi_ref, lo_ref, pop_ref, wsum_ref, psum_ref = refs[3 * count :]
+    locs, region_ref, hi_ref, lo_ref, pop_ref, wsum_ref, psum_ref = refs[3 * count + 1 :]
     ages, rows, _ = xs[0].shape
     zero = jnp.zeros((rows, LANES), jnp.float32)
     lane = lax.broadcasted_iota(jnp.int32, (1, LANES), 1)
@@ -248,7 +248,7 @@
     region_ref[...] = (t + (0.5 - 0.5 * jnp.exp(-h))) * (1.0 / ages)
 
 
-def survive(device, sent, pop_t, region_row):
+def survive(device, sent, pop_t, region_row, done):
     every = [b for bits in CHUNKS for b in bits]
     ages, rows, _ = sent[0].shape
     sexes, locs = pop_t.shape[1], pop_t.shape[2] // HALF
@@ -272,7 +272,8 @@
             grid=(1,),
             in_specs=[whole(ages, rows, LANES)] * len(every)
             + [pop_spec(b) for b in every]
-            + [region_spec(b) for b in every],
+            + [region_spec(b) for b in every]
+            + [whole(*done.shape)],
             out_specs=(whole(locs, rows, LANES), whole(rows, LANES)),
             scratch_shapes=[
                 pltpu.VMEM((ages * rows, 4 * LANES), jnp.bfloat16),
@@ -285,7 +286,7 @@
         compiler_params=pltpu.CompilerParams(vmem_limit_bytes=57 << 20),
         cost_estimate=LONG,
         name="survive",
-    )(device, *[sent[b] for b in every], *([pop_t] * len(every)), *([region_row] * len(every)))
+    )(device, *[sent[b] for b in every], *([pop_t] * len(every)), *([region_row] * len(every)), done)
 
 
 def turn_kernel(near, d_ref, *refs):
@@ -340,7 +341,12 @@
     region_out = region_part.reshape(rows, sexes, devices, mine)
     region_out = jnp.transpose(region_out, (2, 1, 3, 0)).reshape(devices, 1, sexes * mine * rows)
     packed = jnp.concatenate([by_device, region_out], axis=1)
-    small = lax.all_to_all(packed, "loc", split_axis=0, concat_axis=0, tiled=True)
+    return lax.all_to_all(packed, "loc", split_axis=0, concat_axis=0, tiled=True)
+
+
+def unpack(small, rows, sexes):
+    devices = small.shape[0]
+    mine = REGIONS // devices
     loc_survival = jnp.transpose(small[:, :rows].reshape(devices * rows, LANES), (1, 0))
     region_survival = jnp.transpose(
         small[:, rows].reshape(devices, sexes, mine, rows), (1, 2, 0, 3)
@@ -384,6 +390,8 @@
     got = {0: sent[0]}
     for i, b in enumerate(NEAR):
         message = sent[b]
+        if 0 < i < 3:
+            message, done = tie(message, done)
         if i >= 2:
             message, got[NEAR[i - 2]] = tie(message, got[NEAR[i - 2]])
         got[b] = swap(message, b)
@@ -394,9 +402,7 @@
             ahead = FAR[max(i - 3, min(i - 2, 1))]
             message, got[ahead] = tie(message, got[ahead])
         if i == 5:
-            sums = survive(device, sent, pop_t, region_row)
-            message, sums = tie(message, sums)
-        if i == 7:
+            sums = survive(device, sent, pop_t, region_row, done)
             small = exchange(*sums, sexes)
             message, small = tie(message, small)
         got[b] = swap(message, b)
@@ -404,7 +410,7 @@
     shape = jax.ShapeDtypeStruct((sexes, ages, HALF, devices * rows), jnp.bfloat16)
     close = [got[b] for b in range(8)]
     half = turn(device, close, shape, None)
-    loc_survival, region_survival = small
+    loc_survival, region_survival = unpack(small, rows, sexes)
     ready = (loc_survival, region_survival)
     log_rates = turn(device, [got[b] for b in range(8, 16)], shape, half, ready)
     return (log_rates, loc_survival, region_survival)

time: 211 us -> 197 us (0.934); the launches traced: 210 us -> 193 us
  waiting for transfers between devices: 97.9 us -> 80.7 us
    all_to_all x1, waiting for transfers between devices: 20.3 us -> 3.73 us  [exchange(): lax.all_to_all(packed, 'loc', split_axis=0, concat_axis=0, tiled=True)]
    all_to_all x1, starting transfers between devices: 3.97 us -> 6.68 us  [exchange(): lax.all_to_all(packed, 'loc', split_axis=0, concat_axis=0, tiled=True)]
    ppermute x21, starting transfers between devices: 30.8 us -> 28.2 us  [swap(): return lax.ppermute(x, 'loc', [(i, i ^ bits) for i in range(devices)])]
  transfers between devices with their start and end apart: 22 -> 22, of which waited for: 8 -> 10; matrix products, arithmetic and copies ran while one was open for 2% -> 2% of each run, Pallas kernels for 29% -> 32%
where the time goes in v6:
time: 197 us; the launch traced here: 193 us
  waiting for transfers between devices  80.7 us (41%)
  Pallas kernels  70.4 us (36%)
  starting transfers between devices  34.9 us (18%)
  local copies, waits for them, and re-layouts  5 us (3%)
    ppermute x21, waiting for transfers between devices, swap(): return lax.ppermute(x, 'loc', [(i, i ^ bits) for i in range(devices)])  76.9 us
    pallas_call x1, Pallas kernels, survive(): pl.pallas_call(survive_kernel, out_shape=(jax.ShapeDtypeStruct((locs, row...  28.5 us
    ppermute x21, starting transfers between devices, swap(): return lax.ppermute(x, 'loc', [(i, i ^ bits) for i in range(devices)])  28.2 us
    pallas_call x3, Pallas kernels, loc_mix(): pl.pallas_call(functools.partial(loc_mix_kernel, groups, len(factors)), o...  20.8 us
    pallas_call x1, Pallas kernels, age_mix(): pl.pallas_call(age_mix_kernel, out_shape=(jax.ShapeDtypeStruct(noise.shap...  12.5 us
    pallas_call x2, Pallas kernels, turn(): pl.pallas_call(functools.partial(turn_kernel, near), out_shape=out_shape,...  8.53 us
    all_to_all x1, starting transfers between devices, exchange(): lax.all_to_all(packed, 'loc', split_axis=0, concat_axis=0, tiled=True)  6.68 us
  transfers between devices with their start and end apart: 22, of which 10 were waited for; matrix products, arithmetic and copies ran while one was open for 2% of the time, Pallas kernels for 32%

profile of v6, /device:TPU:17, one launch (start us, length us, event | category | flops | bytes accessed | tf_op | source)
XLA Modules:
  0.0 193.3 jit_solution(11678355641494159378)
XLA Ops:
  0.7 1.4 collective-permute-start
  2.1 1.3 collective-permute-start.2
  3.3 12.5 %age_mix.1 = (bf16[2,1776,1024]{2,1,0:T(8,128)(2,1)}, f32[8,128]{1,0:T(8,128)}) custom-call(bf16[111,111]{1,0:T(8,128)(2,1)} %age_ref.1, bf16[2,1776,1024]{2,1,0:T(8,128)(2,1)} %bitcast.22), custom_call_target="tpu_custom_call" | custom-call | flops 20000000000 | bytes 1000 | tf_op jit(solution)/shard_map/age_mix/pallas_call | solution.py:94
  16.6 6.3 %loc_mix.3 = (bf16[111,16,128]{2,1,0:T(8,128)(2,1)}, bf16[111,16,128]{2,1,0:T(8,128)(2,1)}, bf16[111,16,128]{2,1,0:T(8,128)(2,1)}, bf16[111,16,128]{2,1,0:T(8,12...) custom-call(s32[1]{0:T(128)} %bitcast.d_ref, bf16[2,1776,1024]{2,1,0:T(8,128)(2,1)} %get-tuple-element.63.x_ref, ...), custom_call_target="tpu_custom_call" | custom-call | flops 20000000000 | bytes 1000 | tf_op jit(solution)/shard_map/loc_mix/pallas_call | solution.py:165
  22.9 1.6 collective-permute-start.3
  24.5 1.2 collective-permute-start.6
  26.7 2.6 %collective-permute-start.8 = (bf16[111,16,128]{2,1,0:T(8,128)(2,1)}, bf16[111,16,128]{2,1,0:T(8,128)(2,1)S(1)}, u32[]{:S(2)}, u32[]{:S(2)}) collective-permute-start(bf16[111,16,128]{2,1,0:T(8,128)(2,1)} %get-tuple-element.85.refs_1_), channel_id=1, source_target_pairs={{0,24},{2,26},{4,28},{6,30},{8,16},{10,18},{12,20},{14,22},{16,8},... | collective-permute-start | bytes 1363976 | tf_op jit(solution)/shard_map/ppermute | solution.py:363
  30.1 6.3 %loc_mix.4 = (bf16[111,16,128]{2,1,0:T(8,128)(2,1)}, bf16[111,16,128]{2,1,0:T(8,128)(2,1)}, bf16[111,16,128]{2,1,0:T(8,128)(2,1)}, bf16[111,16,128]{2,1,0:T(8,128)(2,1)}, f32[8,128]{1,0:T(8,128)}) custom-call(s32[1]{0:T(128)} %bitcast.d_ref, bf16[2,1776,1024]{2,1,0:T(8,128)(2,1)} %get-tuple-element.63.x_ref, bf16[256,1024]{1,0:T(8,128)(2,1)} %copy-done.4, ...), custom_call_target="tpu_custom_call" | custom-call | flops 20000000000 | bytes 1000 | tf_op jit(solution)/shard_map/loc_mix/pallas_call | solution.py:165
  36.4 2.8 %collective-permute-done.6.refs_1_ = bf16[256,1024]{1,0:T(8,128)(2,1)S(1)} collective-permute-done((bf16[256,1024]{1,0:T(8,128)(2,1)}, bf16[256,1024]{1,0:T(8,128)(2,1)S(1)}, u32[]{:S(2)}, u32[]{:S(2)}) %collective-permute-start.6) | collective-permute-done | bytes 524320 | tf_op jit(solution)/shard_map/ppermute | solution.py:363
  39.2 10.1 %collective-permute-done.5.refs_0_ = bf16[256,1024]{1,0:T(8,128)(2,1)S(1)} collective-permute-done((bf16[256,1024]{1,0:T(8,128)(2,1)}, bf16[256,1024]{1,0:T(8,128)(2,1)S(1)}, u32[]{:S(2)}, u32[]{:S(2)}) %collective-permute-start.5) | collective-permute-done | bytes 524320 | tf_op jit(solution)/shard_map/ppermute | solution.py:363
  50.1 8.2 %loc_mix.5 = (bf16[111,16,128]{2,1,0:T(8,128)(2,1)}, bf16[111,16,128]{2,1,0:T(8,128)(2,1)}, bf16[111,16,128]{2,1,0:T(8,128)(2,1)}, bf16[111,16,128]{2,1,0:T(8,12...) custom-call(s32[1]{0:T(128)} %bitcast.d_ref, ...), custom_call_target="tpu_custom_call" | custom-call | flops 20000000000 | bytes 1000 | tf_op jit(solution)/shard_map/loc_mix/pallas_call | solution.py:165
  58.3 1.5 collective-permute-start.15
  59.9 2.1 %collective-permute-start.18 = (bf16[111,16,128]{2,1,0:T(8,128)(2,1)S(1)}, bf16[111,16,128]{2,1,0:T(8,128)(2,1)}, u32[]{:S(2)}, u32[]{:S(2)}) collective-permute-start(bf16[111,16,128]{2,1,0:T(8,128)(2,1)S(1)} %copy-done.7), channel_id=1, source_target_pairs={{0,10},{2,8},{4,14},{6,12},{8,2},{10,0},{12,6},{14,4},{16,26},{18,... | collective-permute-start | bytes 1363976 | tf_op jit(solution)/shard_map/ppermute | solution.py:363
  61.9 6.8 %collective-permute-done.8.refs_4_ = bf16[111,16,128]{2,1,0:T(8,128)(2,1)S(1)} collective-permute-done((bf16[111,16,128]{2,1,0:T(8,128)(2,1)}, bf16[111,16,128]{2,1,0:T(8,128)(2,1)S(1)}, u32[]{:S(2)}, u32[]{:S(2)}) %collective-permute-start.8) | collective-permute-done | bytes 454688 | tf_op jit(solution)/shard_map/ppermute | solution.py:363
  69.0 3.6 %collective-permute-start.7 = (bf16[111,16,128]{2,1,0:T(8,128)(2,1)}, bf16[111,16,128]{2,1,0:T(8,128)(2,1)S(1)}, u32[]{:S(2)}, u32[]{:S(2)}) collective-permute-start(bf16[111,16,128]{2,1,0:T(8,128)(2,1)} %get-tuple-element.80.refs_4_), channel_id=1, source_target_pairs={{0,18},{2,16},{4,22},{6,20},{8,26},{10,24},{12,30},{14,28},{16,2},... | collective-permute-start | bytes 1363976 | tf_op jit(solution)/shard_map/ppermute | solution.py:363
  72.9 2.7 %collective-permute-done.18.refs_5_ = bf16[111,16,128]{2,1,0:T(8,128)(2,1)} collective-permute-done((bf16[111,16,128]{2,1,0:T(8,128)(2,1)S(1)}, bf16[111,16,128]{2,1,0:T(8,128)(2,1)}, u32[]{:S(2)}, u32[]{:S(2)}) %collective-permute-start.18) | collective-permute-done | bytes 454688 | tf_op jit(solution)/shard_map/ppermute | solution.py:363
  75.6 3.1 %collective-permute-start.19 = (bf16[111,16,128]{2,1,0:T(8,128)(2,1)}, bf16[111,16,128]{2,1,0:T(8,128)(2,1)}, u32[]{:S(2)}, u32[]{:S(2)}) collective-permute-start(bf16[111,16,128]{2,1,0:T(8,128)(2,1)} %get-tuple-element.119.refs_10_), channel_id=1, source_target_pairs={{0,12},{2,14},{4,8},{6,10},{8,4},{10,6},{12,0},{14,2},{16,28},{18,... | collective-permute-start | bytes 1363976 | tf_op jit(solution)/shard_map/ppermute | solution.py:363
  78.7 28.5 %survive.1 = (f32[16,16,128]{2,1,0:T(8,128)}, f32[16,128]{1,0:T(8,128)}) custom-call(s32[1]{0:T(128)} %bitcast.d_ref, bf16[111,16,128]{2,1,0:T(8,128)(2,1)} %get-tuple-element.73.refs_0_, bf16[111,16,128]{2,1,0:T(8,128)(2,1)} %get-tuple-element.85.refs_1_, bf16[111,16,128]{2,1,0:T(8,128)(2,1)} %get-tuple-element.95.refs_2_, ...), custom_call_target="tpu_custom_call" | custom-call | flops 20000000000 | bytes 1000 | tf_op jit(solution)/shard_map/survive/pallas_call | solution.py:264
  108.2 1.1 collective-permute-start.17
  109.3 3.6 %collective-permute-done.19.refs_6_ = bf16[111,16,128]{2,1,0:T(8,128)(2,1)} collective-permute-done((bf16[111,16,128]{2,1,0:T(8,128)(2,1)}, bf16[111,16,128]{2,1,0:T(8,128)(2,1)}, u32[]{:S(2)}, u32[]{:S(2)}) %collective-permute-start.19) | collective-permute-done | bytes 454688 | tf_op jit(solution)/shard_map/ppermute | solution.py:363
  112.8 1.6 pad_maximum_fusion
  114.4 6.7 %all-to-all-start = ((f32[16,17,128]{2,1,0:T(8,128)}), f32[16,17,128]{2,1,0:T(8,128)S(1)}, u32[]{:S(2)}, u32[]{:S(2)}) async-start(f32[16,17,128]{2,1,0:T(8,128)} %pad_maximum_fusion), calls=%async_computation | async-start | bytes 393216 | tf_op jit(solution)/shard_map/all_to_all | solution.py:344
  121.1 1.5 collective-permute-start.13
  122.6 3.0 %collective-permute-start.11 = (bf16[111,16,128]{2,1,0:T(8,128)(2,1)}, bf16[111,16,128]{2,1,0:T(8,128)(2,1)S(1)}, u32[]{:S(2)}, u32[]{:S(2)}) collective-permute-start(bf16[111,16,128]{2,1,0:T(8,128)(2,1)} %get-tuple-element.91.refs_12_), channel_id=1, source_target_pairs={{0,22},{2,20},{4,18},{6,16},{8,30},{10,28},{12,26},{14,24},{16,6},... | collective-permute-start | bytes 1363976 | tf_op jit(solution)/shard_map/ppermute | solution.py:363
  125.7 23.6 %collective-permute-done.7.refs_1_ = bf16[111,16,128]{2,1,0:T(8,128)(2,1)S(1)} collective-permute-done((bf16[111,16,128]{2,1,0:T(8,128)(2,1)}, bf16[111,16,128]{2,1,0:T(8,128)(2,1)S(1)}, u32[]{:S(2)}, u32[]{:S(2)}) %collective-permute-start.7) | collective-permute-done | bytes 454688 | tf_op jit(solution)/shard_map/ppermute | solution.py:363
  149.3 3.7 %all-to-all-done = f32[16,17,128]{2,1,0:T(8,128)S(1)} async-done(((f32[16,17,128]{2,1,0:T(8,128)}), f32[16,17,128]{2,1,0:T(8,128)S(1)}, u32[]{:S(2)}, u32[]{:S(2)}) %all-to-all-start) | async-done | bytes 139296 | tf_op jit(solution)/shard_map/all_to_all | solution.py:344
  154.9 2.5 %collective-permute-start.12 = (bf16[111,16,128]{2,1,0:T(8,128)(2,1)}, bf16[111,16,128]{2,1,0:T(8,128)(2,1)S(1)}, u32[]{:S(2)}, u32[]{:S(2)}) collective-permute-start(bf16[111,16,128]{2,1,0:T(8,128)(2,1)} %get-tuple-element.108.refs_9_), channel_id=1, source_target_pairs={{0,28},{2,30},{4,24},{6,26},{8,20},{10,22},{12,16},{14,18},{16,12}... | collective-permute-start | bytes 1363976 | tf_op jit(solution)/shard_map/ppermute | solution.py:363
  157.4 5.6 %turn.2.refs_8_ = bf16[2,111,64,256]{3,2,1,0:T(8,128)(2,1)} custom-call(s32[1]{0:T(128)} %bitcast.d_ref, bf16[111,16,128]{2,1,0:T(8,128)(2,1)} %get-tuple-element.96.refs_3_.refs_0_, bf16[111,16,128]{2,1,0:T(8,128)(2,1)} %collective-permute-done.15.refs_1_, bf16[111,16,128]{2,1,0:T(8,128)(2,1)} %collective-permute-done.16.refs_2_, ...), custom_call_target="tpu_custom_call" | custom-call | flops 20000000000 | bytes 1000 | tf_op jit(solution)/shard_map/turn/pallas_call | solution.py:321
  163.0 10.3 %collective-permute-done.13.refs_7_ = bf16[111,16,128]{2,1,0:T(8,128)(2,1)S(1)} collective-permute-done((bf16[111,16,128]{2,1,0:T(8,128)(2,1)}, bf16[111,16,128]{2,1,0:T(8,128)(2,1)S(1)}, u32[]{:S(2)}, u32[]{:S(2)}) %collective-permute-start.13) | collective-permute-done | bytes 454688 | tf_op jit(solution)/shard_map/ppermute | solution.py:363
  173.2 7.4 %collective-permute-done.11.refs_3_ = bf16[111,16,128]{2,1,0:T(8,128)(2,1)S(1)} collective-permute-done((bf16[111,16,128]{2,1,0:T(8,128)(2,1)}, bf16[111,16,128]{2,1,0:T(8,128)(2,1)S(1)}, u32[]{:S(2)}, u32[]{:S(2)}) %collective-permute-start.11) | collective-permute-done | bytes 454688 | tf_op jit(solution)/shard_map/ppermute | solution.py:363
  180.6 9.7 %collective-permute-done.12.refs_6_ = bf16[111,16,128]{2,1,0:T(8,128)(2,1)S(1)} collective-permute-done((bf16[111,16,128]{2,1,0:T(8,128)(2,1)}, bf16[111,16,128]{2,1,0:T(8,128)(2,1)S(1)}, u32[]{:S(2)}, u32[]{:S(2)}) %collective-permute-start.12) | collective-permute-done | bytes 454688 | tf_op jit(solution)/shard_map/ppermute | solution.py:363
  190.4 3.0 %turn.3 = bf16[2,111,64,256]{3,2,1,0:T(8,128)(2,1)} custom-call(s32[1]{0:T(128)} %bitcast.d_ref, bf16[111,16,128]{2,1,0:T(8,128)(2,1)S(1)} %collective-permute-done.4.refs_0_, bf16[111,16,128]{2,1,0:T(8,128)(2,1)S(1)} %collective-permute-done.7.refs_1_, bf16[111,16,128]{2,1,0:T(8,128)(2,1)S(1)} %collective-permute-done.9.refs_2_, ...), custom_call_target="tpu_custom_call", output_to_operand_aliasing={{}: (9, {})} | custom-call | flops 20000000000 | bytes 1000 | tf_op jit(solution)/shard_map/turn/pallas_call | solution.py:321
  (53 shorter events, 6.8 us)
Async XLA Ops:
  0.6 15.2 %collective-permute-start.1 = (bf16[64,1024]{1,0:T(8,128)(2,1)}, bf16[64,1024]{1,0:T(8,128)(2,1)S(1)}, u32[]{:S(2)}, u32[]{:S(2)}) collective-permute-start(bf16[64,1024]{1,0:T(8,128)(2,1)} %refs_3_), channel_id=1, source_target_pairs={{0,16},{2,18},{4,20},{6,22},{8,24},{10,26},{12,28},{14,30},{16,0},... | collective-permute-start | bytes 393224 | tf_op jit(solution)/shard_map/ppermute | solution.py:363
  0.7 15.1 %collective-permute-start = (bf16[64,1024]{1,0:T(8,128)(2,1)}, bf16[64,1024]{1,0:T(8,128)(2,1)S(1)}, u32[]{:S(2)}, u32[]{:S(2)}) collective-permute-start(bf16[64,1024]{1,0:T(8,128)(2,1)} %refs_3_), channel_id=1, source_target_pairs={{0,8},{2,10},{4,12},{6,14},{8,0},{10,2},{12,4},{14,6},{16,24},{18,... | collective-permute-start | bytes 393224 | tf_op jit(solution)/shard_map/ppermute | solution.py:363
  2.1 13.8 %collective-permute-start.2 = (bf16[64,1024]{1,0:T(8,128)(2,1)}, bf16[64,1024]{1,0:T(8,128)(2,1)S(1)}, u32[]{:S(2)}, u32[]{:S(2)}) collective-permute-start(bf16[64,1024]{1,0:T(8,128)(2,1)} %refs_3_), channel_id=1, source_target_pairs={{0,24},{2,26},{4,28},{6,30},{8,16},{10,18},{12,20},{14,22},{16,8},... | collective-permute-start | bytes 393224 | tf_op jit(solution)/shard_map/ppermute | solution.py:363
  15.9 0.7 copy-start.11
  22.9 6.4 %collective-permute-start.3 = (bf16[256,1024]{1,0:T(8,128)(2,1)}, bf16[256,1024]{1,0:T(8,128)(2,1)S(1)}, u32[]{:S(2)}, u32[]{:S(2)}) collective-permute-start(bf16[256,1024]{1,0:T(8,128)(2,1)} %get-tuple-element.70), channel_id=1, source_target_pairs={{0,2},{2,0},{4,6},{6,4},{8,10},{10,8},{12,14},{14,12},{16,18},{18,... | collective-permute-start | bytes 1572872 | tf_op jit(solution)/shard_map/ppermute | solution.py:363
  24.5 14.7 %collective-permute-start.6 = (bf16[256,1024]{1,0:T(8,128)(2,1)}, bf16[256,1024]{1,0:T(8,128)(2,1)S(1)}, u32[]{:S(2)}, u32[]{:S(2)}) collective-permute-start(bf16[256,1024]{1,0:T(8,128)(2,1)} %get-tuple-element.70), channel_id=1, source_target_pairs={{0,6},{2,4},{4,2},{6,0},{8,14},{10,12},{12,10},{14,8},{16,22},{18,... | collective-permute-start | bytes 1572872 | tf_op jit(solution)/shard_map/ppermute | solution.py:363
  25.6 23.6 %collective-permute-start.5 = (bf16[256,1024]{1,0:T(8,128)(2,1)}, bf16[256,1024]{1,0:T(8,128)(2,1)S(1)}, u32[]{:S(2)}, u32[]{:S(2)}) collective-permute-start(bf16[256,1024]{1,0:T(8,128)(2,1)} %get-tuple-element.70), channel_id=1, source_target_pairs={{0,4},{2,6},{4,0},{6,2},{8,12},{10,14},{12,8},{14,10},{16,20},{18,... | collective-permute-start | bytes 1572872 | tf_op jit(solution)/shard_map/ppermute | solution.py:363
  25.9 36.0 %collective-permute-start.4 = (bf16[111,16,128]{2,1,0:T(8,128)(2,1)}, bf16[111,16,128]{2,1,0:T(8,128)(2,1)S(1)}, u32[]{:S(2)}, u32[]{:S(2)}) collective-permute-start(bf16[111,16,128]{2,1,0:T(8,128)(2,1)} %get-tuple-element.73.refs_0_), channel_id=1, source_target_pairs={{0,16},{2,18},{4,20},{6,22},{8,24},{10,26},{12,28},{14,30},{16,0},... | collective-permute-start | bytes 1363976 | tf_op jit(solution)/shard_map/ppermute | solution.py:363
  26.7 42.1 %collective-permute-start.8 = (bf16[111,16,128]{2,1,0:T(8,128)(2,1)}, bf16[111,16,128]{2,1,0:T(8,128)(2,1)S(1)}, u32[]{:S(2)}, u32[]{:S(2)}) collective-permute-start(bf16[111,16,128]{2,1,0:T(8,128)(2,1)} %get-tuple-element.85.refs_1_), channel_id=1, source_target_pairs={{0,24},{2,26},{4,28},{6,30},{8,16},{10,18},{12,20},{14,22},{16,8},... | collective-permute-start | bytes 1363976 | tf_op jit(solution)/shard_map/ppermute | solution.py:363
  29.3 0.8 copy-start.4
  29.3 29.0 %collective-permute-start.14 = (bf16[111,16,128]{2,1,0:T(8,128)(2,1)}, bf16[111,16,128]{2,1,0:T(8,128)(2,1)S(1)}, u32[]{:S(2)}, u32[]{:S(2)}) collective-permute-start(bf16[111,16,128]{2,1,0:T(8,128)(2,1)} %get-tuple-element.95.refs_2_), channel_id=1, source_target_pairs={{0,8},{2,10},{4,12},{6,14},{8,0},{10,2},{12,4},{14,6},{16,24},{18,... | collective-permute-start | bytes 1363976 | tf_op jit(solution)/shard_map/ppermute | solution.py:363
  39.2 10.1 %copy-start.2 = (bf16[256,1024]{1,0:T(8,128)(2,1)}, bf16[256,1024]{1,0:T(8,128)(2,1)S(1)}, u32[]{:S(2)}) copy-start(bf16[256,1024]{1,0:T(8,128)(2,1)S(1)} %collective-permute-done.6.refs_1_) | copy-start | bytes 1572868
  49.3 0.8 copy-start.3
  50.1 8.2 %copy-start.8 = (bf16[111,16,128]{2,1,0:T(8,128)(2,1)S(1)}, bf16[111,16,128]{2,1,0:T(8,128)(2,1)}, u32[]{:S(2)}) copy-start(bf16[111,16,128]{2,1,0:T(8,128)(2,1)} %get-tuple-element.111.refs_7_) | copy-start | bytes 1363972
  50.1 9.8 %copy-start.7 = (bf16[111,16,128]{2,1,0:T(8,128)(2,1)S(1)}, bf16[111,16,128]{2,1,0:T(8,128)(2,1)}, u32[]{:S(2)}) copy-start(bf16[111,16,128]{2,1,0:T(8,128)(2,1)} %get-tuple-element.117.refs_6_) | copy-start | bytes 1363972
  50.1 18.7 %copy-start.6 = (bf16[111,16,128]{2,1,0:T(8,128)(2,1)S(1)}, bf16[111,16,128]{2,1,0:T(8,128)(2,1)}, u32[]{:S(2)}) copy-start(bf16[111,16,128]{2,1,0:T(8,128)(2,1)} %get-tuple-element.90.refs_5_) | copy-start | bytes 1363972
  58.3 10.4 %copy-start.5 = (bf16[111,16,128]{2,1,0:T(8,128)(2,1)}, bf16[111,16,128]{2,1,0:T(8,128)(2,1)S(1)}, u32[]{:S(2)}) copy-start(bf16[111,16,128]{2,1,0:T(8,128)(2,1)S(1)} %collective-permute-done.14.refs_4_) | copy-start | bytes 1363972
  58.3 14.3 %collective-permute-start.15 = (bf16[111,16,128]{2,1,0:T(8,128)(2,1)S(1)}, bf16[111,16,128]{2,1,0:T(8,128)(2,1)}, u32[]{:S(2)}, u32[]{:S(2)}) collective-permute-start(bf16[111,16,128]{2,1,0:T(8,128)(2,1)S(1)} %copy-done.8), channel_id=1, source_target_pairs={{0,2},{2,0},{4,6},{6,4},{8,10},{10,8},{12,14},{14,12},{16,18},{18,... | collective-permute-start | bytes 1363976 | tf_op jit(solution)/shard_map/ppermute | solution.py:363
  59.9 15.7 %collective-permute-start.18 = (bf16[111,16,128]{2,1,0:T(8,128)(2,1)S(1)}, bf16[111,16,128]{2,1,0:T(8,128)(2,1)}, u32[]{:S(2)}, u32[]{:S(2)}) collective-permute-start(bf16[111,16,128]{2,1,0:T(8,128)(2,1)S(1)} %copy-done.7), channel_id=1, source_target_pairs={{0,10},{2,8},{4,14},{6,12},{8,2},{10,0},{12,6},{14,4},{16,26},{18,... | collective-permute-start | bytes 1363976 | tf_op jit(solution)/shard_map/ppermute | solution.py:363
  68.8 52.4 %collective-permute-start.9 = (bf16[111,16,128]{2,1,0:T(8,128)(2,1)}, bf16[111,16,128]{2,1,0:T(8,128)(2,1)S(1)}, u32[]{:S(2)}, u32[]{:S(2)}) collective-permute-start(bf16[111,16,128]{2,1,0:T(8,128)(2,1)} %get-tuple-element.87.refs_8_), channel_id=1, source_target_pairs={{0,20},{2,22},{4,16},{6,18},{8,28},{10,30},{12,24},{14,26},{16,4},... | collective-permute-start | bytes 1363976 | tf_op jit(solution)/shard_map/ppermute | solution.py:363
  68.8 53.9 %collective-permute-start.10 = (bf16[111,16,128]{2,1,0:T(8,128)(2,1)S(1)}, bf16[111,16,128]{2,1,0:T(8,128)(2,1)S(1)}, u32[]{:S(2)}, u32[]{:S(2)}) collective-permute-start(bf16[111,16,128]{2,1,0:T(8,128)(2,1)S(1)} %copy-done.6), channel_id=1, source_target_pairs={{0,26},{2,24},{4,30},{6,28},{8,18},{10,16},{12,22},{14,20},{16,10}... | collective-permute-start | bytes 1363976 | tf_op jit(solution)/shard_map/ppermute | solution.py:363
  69.0 80.3 %collective-permute-start.7 = (bf16[111,16,128]{2,1,0:T(8,128)(2,1)}, bf16[111,16,128]{2,1,0:T(8,128)(2,1)S(1)}, u32[]{:S(2)}, u32[]{:S(2)}) collective-permute-start(bf16[111,16,128]{2,1,0:T(8,128)(2,1)} %get-tuple-element.80.refs_4_), channel_id=1, source_target_pairs={{0,18},{2,16},{4,22},{6,20},{8,26},{10,24},{12,30},{14,28},{16,2},... | collective-permute-start | bytes 1363976 | tf_op jit(solution)/shard_map/ppermute | solution.py:363
  72.6 35.5 %collective-permute-start.16 = (bf16[111,16,128]{2,1,0:T(8,128)(2,1)}, bf16[111,16,128]{2,1,0:T(8,128)(2,1)}, u32[]{:S(2)}, u32[]{:S(2)}) collective-permute-start(bf16[111,16,128]{2,1,0:T(8,128)(2,1)} %get-tuple-element.113.refs_11_), channel_id=1, source_target_pairs={{0,4},{2,6},{4,0},{6,2},{8,12},{10,14},{12,8},{14,10},{16,20},{18,... | collective-permute-start | bytes 1363976 | tf_op jit(solution)/shard_map/ppermute | solution.py:363
  75.6 37.3 %collective-permute-start.19 = (bf16[111,16,128]{2,1,0:T(8,128)(2,1)}, bf16[111,16,128]{2,1,0:T(8,128)(2,1)}, u32[]{:S(2)}, u32[]{:S(2)}) collective-permute-start(bf16[111,16,128]{2,1,0:T(8,128)(2,1)} %get-tuple-element.119.refs_10_), channel_id=1, source_target_pairs={{0,12},{2,14},{4,8},{6,10},{8,4},{10,6},{12,0},{14,2},{16,28},{18,... | collective-permute-start | bytes 1363976 | tf_op jit(solution)/shard_map/ppermute | solution.py:363
  108.2 49.3 %collective-permute-start.17 = (bf16[111,16,128]{2,1,0:T(8,128)(2,1)}, bf16[111,16,128]{2,1,0:T(8,128)(2,1)}, u32[]{:S(2)}, u32[]{:S(2)}) collective-permute-start(bf16[111,16,128]{2,1,0:T(8,128)(2,1)} %get-tuple-element.115.refs_15_), channel_id=1, source_target_pairs={{0,6},{2,4},{4,2},{6,0},{8,14},{10,12},{12,10},{14,8},{16,22},{18,... | collective-permute-start | bytes 1363976 | tf_op jit(solution)/shard_map/ppermute | solution.py:363
  112.8 44.6 %collective-permute-start.20 = (bf16[111,16,128]{2,1,0:T(8,128)(2,1)}, bf16[111,16,128]{2,1,0:T(8,128)(2,1)}, u32[]{:S(2)}, u32[]{:S(2)}) collective-permute-start(bf16[111,16,128]{2,1,0:T(8,128)(2,1)} %get-tuple-element.121.refs_14_), channel_id=1, source_target_pairs={{0,14},{2,12},{4,10},{6,8},{8,6},{10,4},{12,2},{14,0},{16,30},{18,... | collective-permute-start | bytes 1363976 | tf_op jit(solution)/shard_map/ppermute | solution.py:363
  114.4 38.6 %all-to-all-start = ((f32[16,17,128]{2,1,0:T(8,128)}), f32[16,17,128]{2,1,0:T(8,128)S(1)}, u32[]{:S(2)}, u32[]{:S(2)}) async-start(f32[16,17,128]{2,1,0:T(8,128)} %pad_maximum_fusion), calls=%async_computation | async-start | bytes 393216 | tf_op jit(solution)/shard_map/all_to_all | solution.py:344
  121.1 52.1 %collective-permute-start.13 = (bf16[111,16,128]{2,1,0:T(8,128)(2,1)}, bf16[111,16,128]{2,1,0:T(8,128)(2,1)S(1)}, u32[]{:S(2)}, u32[]{:S(2)}) collective-permute-start(bf16[111,16,128]{2,1,0:T(8,128)(2,1)} %get-tuple-element.109.refs_13_), channel_id=1, source_target_pairs={{0,30},{2,28},{4,26},{6,24},{8,22},{10,20},{12,18},{14,16},{16,14}... | collective-permute-start | bytes 1363976 | tf_op jit(solution)/shard_map/ppermute | solution.py:363
  122.6 58.0 %collective-permute-start.11 = (bf16[111,16,128]{2,1,0:T(8,128)(2,1)}, bf16[111,16,128]{2,1,0:T(8,128)(2,1)S(1)}, u32[]{:S(2)}, u32[]{:S(2)}) collective-permute-start(bf16[111,16,128]{2,1,0:T(8,128)(2,1)} %get-tuple-element.91.refs_12_), channel_id=1, source_target_pairs={{0,22},{2,20},{4,18},{6,16},{8,30},{10,28},{12,26},{14,24},{16,6},... | collective-permute-start | bytes 1363976 | tf_op jit(solution)/shard_map/ppermute | solution.py:363
  154.7 35.7 %copy-start = (f32[256,128]{0,1:T(8,128)}, f32[256,128]{0,1:T(8,128)S(1)}, u32[]{:S(2)}) copy-start(f32[256,128]{0,1:T(8,128)S(1)} %copy.15) | copy-start | bytes 393220
  154.9 35.4 %copy-start.1 = (f32[2,4,256]{2,1,0:T(4,128)}, f32[2,4,256]{2,1,0:T(4,128)S(1)}, u32[]{:S(2)}) copy-start(f32[2,4,256]{2,1,0:T(4,128)S(1)} %reshape.33.refs_10_) | copy-start | bytes 24580
  154.9 35.4 %collective-permute-start.12 = (bf16[111,16,128]{2,1,0:T(8,128)(2,1)}, bf16[111,16,128]{2,1,0:T(8,128)(2,1)S(1)}, u32[]{:S(2)}, u32[]{:S(2)}) collective-permute-start(bf16[111,16,128]{2,1,0:T(8,128)(2,1)} %get-tuple-element.108.refs_9_), channel_id=1, source_target_pairs={{0,28},{2,30},{4,24},{6,26},{8,20},{10,22},{12,16},{14,18},{16,12}... | collective-permute-start | bytes 1363976 | tf_op jit(solution)/shard_map/ppermute | solution.py:363
  (2 other events, 1.3 us)

commit v7 on v6

--- a/solution.py
+++ b/solution.py
@@ -59,52 +59,70 @@
     return hi, (x - hi.astype(jnp.float32)).astype(jnp.bfloat16)
 
 
-def age_mix_kernel(age_ref, x_ref, o_ref, done_ref, wide_ref):
+PARTS = 4
+TILE = 8
+
+
+def age_mix_kernel(age_ref, *refs):
+    xs, o_ref, done_ref, wide_ref = refs[:PARTS], *refs[PARTS:]
     ages = age_ref.shape[0]
-    rows = x_ref.shape[1]
+    rows = ages * TILE
     step = 256
 
     @pl.when(jnp.logical_and(pl.program_id(0) == 0, pl.program_id(1) == 0))
     def _():
-        pick = lax.broadcasted_iota(jnp.int32, (rows, ages), 0) >> 4
+        pick = lax.broadcasted_iota(jnp.int32, (rows, ages), 0) >> 3
         pick = (pick == lax.broadcasted_iota(jnp.int32, (rows, ages), 1)).astype(jnp.bfloat16)
         tall = jnp.dot(pick, age_ref[...], preferred_element_type=jnp.float32).astype(jnp.bfloat16)
-        spread = lax.broadcasted_iota(jnp.int32, (ages, rows), 1) >> 4
+        spread = lax.broadcasted_iota(jnp.int32, (ages, rows), 1) >> 3
         spread = (spread == lax.broadcasted_iota(jnp.int32, (ages, rows), 0)).astype(jnp.bfloat16)
         for lo in range(0, rows, step):
             hi = min(lo + step, rows)
             both = jnp.dot(tall[lo:hi], spread[:, :hi], preferred_element_type=jnp.float32)
-            same = (lax.broadcasted_iota(jnp.int32, both.shape, 0) & 15) == (
-                lax.broadcasted_iota(jnp.int32, both.shape, 1) & 15
+            same = (lax.broadcasted_iota(jnp.int32, both.shape, 0) & 7) == (
+                lax.broadcasted_iota(jnp.int32, both.shape, 1) & 7
             )
             wide_ref[lo:hi, :hi] = jnp.where(same, both, 0.0).astype(jnp.bfloat16)
 
     done_ref[...] = jnp.zeros_like(done_ref)
-    for lo in range(0, rows, step):
-        hi = min(lo + step, rows)
-        o_ref[0, lo:hi, :] = jnp.dot(
-            wide_ref[lo:hi, :hi], x_ref[0, :hi, :], preferred_element_type=jnp.float32
-        ).astype(jnp.bfloat16)
+    for part, x_ref in enumerate(xs):
+        width = x_ref.shape[-1]
+        x = x_ref[...].reshape(rows, width)
+        for lo in range(0, rows, step):
+            hi = min(lo + step, rows)
+            mixed = jnp.dot(wide_ref[lo:hi, :hi], x[:hi], preferred_element_type=jnp.float32)
+            o_ref[0, lo // TILE : hi // TILE, 0, :, part * width : (part + 1) * width] = (
+                mixed.astype(jnp.bfloat16).reshape((hi - lo) // TILE, TILE, width)
+            )
 
 
 def age_mix(age_factor, noise):
-    sexes, rows, cols = noise.shape
-    ages = age_factor.shape[0]
-    width = 512
-    return pl.pallas_call(
+    sexes, ages, rows, cols = noise.shape
+    tiles = rows // TILE
+    x = noise.reshape(sexes, ages, tiles, TILE, cols)
+    width = cols // PARTS
+
+    def part_spec(part):
+        return pl.BlockSpec((1, ages, 1, TILE, width), lambda s, t: (s, 0, t, 0, part))
+
+    mixed, done = pl.pallas_call(
         age_mix_kernel,
-        out_shape=(jax.ShapeDtypeStruct(noise.shape, jnp.bfloat16), jax.ShapeDtypeStruct((8, LANES), jnp.float32)),
-        grid=(sexes, cols // width),
-        in_specs=[
-            pl.BlockSpec((ages, ages), lambda s, k: (0, 0)),
-            pl.BlockSpec((1, rows, width), lambda s, k: (s, 0, k)),
-        ],
-        out_specs=(pl.BlockSpec((1, rows, width), lambda s, k: (s, 0, k)), pl.BlockSpec((8, LANES), lambda s, k: (0, 0))),
-        scratch_shapes=[pltpu.VMEM((rows, rows), jnp.bfloat16)],
+        out_shape=(
+            jax.ShapeDtypeStruct(x.shape, jnp.bfloat16),
+            jax.ShapeDtypeStruct((8, LANES), jnp.float32),
+        ),
+        grid=(sexes, tiles),
+        in_specs=[pl.BlockSpec((ages, ages), lambda s, t: (0, 0))] + [part_spec(p) for p in range(PARTS)],
+        out_specs=(
+            pl.BlockSpec((1, ages, 1, TILE, cols), lambda s, t: (s, 0, t, 0, 0)),
+            pl.BlockSpec((8, LANES), lambda s, t: (0, 0)),
+        ),
+        scratch_shapes=[pltpu.VMEM((ages * TILE, ages * TILE), jnp.bfloat16)],
         compiler_params=pltpu.CompilerParams(vmem_limit_bytes=57 << 20),
         cost_estimate=LONG,
         name="age_mix",
-    )(age_factor, noise)
+    )(age_factor, *([x] * PARTS))
+    return mixed.reshape(sexes, ages * rows, cols), done
 
 
 def merge_pair(pair, odd_device, swapped):
@@ -370,7 +388,7 @@
     factors = {0: loc_factor}
     for bits in (8, 12, 4):
         factors[bits] = swap(loc_factor, bits)
-    mixed, done = age_mix(age_factor, noise.reshape(sexes, ages * rows, locs))
+    mixed, done = age_mix(age_factor, noise)
     factors, done = tie(factors, done)
 
     sent = {}

time: 197 us -> 194 us (0.985)
  Pallas kernels: 70.4 us -> 67.2 us
  waiting for transfers between devices: 80.7 us -> 83.9 us
    all_to_all x1, waiting for transfers between devices: 3.73 us -> 25.7 us  [exchange(): lax.all_to_all(packed, 'loc', split_axis=0, concat_axis=0, tiled=True)]
    ppermute x21, waiting for transfers between devices: 76.9 us -> 58.3 us  [swap(): return lax.ppermute(x, 'loc', [(i, i ^ bits) for i in range(devices)])]
    pallas_call x1, Pallas kernels: 12.5 us -> 9.48 us  [age_mix(): pl.pallas_call(age_mix_kernel, out_shape=(jax.ShapeDtypeStruct(x.shape, j...]
  transfers between devices with their start and end apart: 22 -> 22, of which waited for: 10 -> 11; matrix products, arithmetic and copies ran while one was open for 2% -> 2% of each run, Pallas kernels for 32% -> 30%
where the time goes in v7:
time: 194 us; the launch traced here: 192 us
  waiting for transfers between devices  83.9 us (43%)
  Pallas kernels  67.2 us (35%)
  starting transfers between devices  34.2 us (18%)
  local copies, waits for them, and re-layouts  4.33 us (2%)
    ppermute x21, waiting for transfers between devices, swap(): return lax.ppermute(x, 'loc', [(i, i ^ bits) for i in range(devices)])  58.3 us
    pallas_call x1, Pallas kernels, survive(): pl.pallas_call(survive_kernel, out_shape=(jax.ShapeDtypeStruct((locs, row...  28.4 us
    ppermute x21, starting transfers between devices, swap(): return lax.ppermute(x, 'loc', [(i, i ^ bits) for i in range(devices)])  27.6 us
    all_to_all x1, waiting for transfers between devices, exchange(): lax.all_to_all(packed, 'loc', split_axis=0, concat_axis=0, tiled=True)  25.7 us
    pallas_call x3, Pallas kernels, loc_mix(): pl.pallas_call(functools.partial(loc_mix_kernel, groups, len(factors)), o...  20.8 us
    pallas_call x1, Pallas kernels, age_mix(): pl.pallas_call(age_mix_kernel, out_shape=(jax.ShapeDtypeStruct(x.shape, j...  9.48 us
    pallas_call x2, Pallas kernels, turn(): pl.pallas_call(functools.partial(turn_kernel, near), out_shape=out_shape,...  8.53 us
    all_to_all x1, starting transfers between devices, exchange(): lax.all_to_all(packed, 'loc', split_axis=0, concat_axis=0, tiled=True)  6.65 us
  transfers between devices with their start and end apart: 22, of which 11 were waited for; matrix products, arithmetic and copies ran while one was open for 2% of the time, Pallas kernels for 30%

profile of v7, /device:TPU:17, one launch (start us, length us, event | category | flops | bytes accessed | tf_op | source)
XLA Modules:
  0.0 192.1 jit_solution(2790145854250212608)
XLA Ops:
  0.7 1.4 collective-permute-start
  2.1 1.3 collective-permute-start.2
  3.3 9.5 %age_mix.1 = (bf16[2,111,2,8,1024]{4,3,2,1,0:T(8,128)(2,1)}, f32[8,128]{1,0:T(8,128)}) custom-call(bf16[111,111]{1,0:T(8,128)(2,1)} %age_ref.1, bf16[2,111,2,8,1024]{4,3,2,1,0:T(8,128)(2,1)} %bitcast.23, bf16[2,111,2,8,1024]{4,3,2,1,0:T(8,128)(2,1)} %bitcast.24, bf16[2,111,2,8,1024]{4,3,2,1,0:T(8,128)(2,1)} %bitcast.25, bf16[2,111,2,8,1024]{4,3,2,1,0:T(8,128)(2,1)} %bitcast.26), custom_call_target="tpu_custom_call" | custom-call | flops 20000000000 | bytes 1000 | tf_op jit(solution)/shard_map/age_mix/pallas_call | solution.py:108
  12.9 2.8 %collective-permute-done.2.refs_1_ = bf16[64,1024]{1,0:T(8,128)(2,1)S(1)} collective-permute-done((bf16[64,1024]{1,0:T(8,128)(2,1)}, bf16[64,1024]{1,0:T(8,128)(2,1)S(1)}, u32[]{:S(2)}, u32[]{:S(2)}) %collective-permute-start.2) | collective-permute-done | bytes 131104 | tf_op jit(solution)/shard_map/ppermute | solution.py:381
  16.3 6.3 %loc_mix.3 = (bf16[111,16,128]{2,1,0:T(8,128)(2,1)}, bf16[111,16,128]{2,1,0:T(8,128)(2,1)}, bf16[111,16,128]{2,1,0:T(8,128)(2,1)}, bf16[111,16,128]{2,1,0:T(8,12...) custom-call(s32[1]{0:T(128)} %bitcast.d_ref, bf16[2,1776,1024]{2,1,0:T(8,128)(2,1)} %bitcast.75, ...), custom_call_target="tpu_custom_call" | custom-call | flops 20000000000 | bytes 1000 | tf_op jit(solution)/shard_map/loc_mix/pallas_call | solution.py:183
  23.2 1.2 collective-permute-start.6
  24.6 1.7 collective-permute-start.8
  26.3 1.9 collective-permute-start.14
  28.2 6.3 %loc_mix.4 = (bf16[111,16,128]{2,1,0:T(8,128)(2,1)}, bf16[111,16,128]{2,1,0:T(8,128)(2,1)}, bf16[111,16,128]{2,1,0:T(8,128)(2,1)}, bf16[111,16,128]{2,1,0:T(8,128)(2,1)}, f32[8,128]{1,0:T(8,128)}) custom-call(s32[1]{0:T(128)} %bitcast.d_ref, bf16[2,1776,1024]{2,1,0:T(8,128)(2,1)} %bitcast.76, bf16[256,1024]{1,0:T(8,128)(2,1)} %copy-done.4, ...), custom_call_target="tpu_custom_call" | custom-call | flops 20000000000 | bytes 1000 | tf_op jit(solution)/shard_map/loc_mix/pallas_call | solution.py:183
  34.5 3.4 %collective-permute-done.6.refs_1_ = bf16[256,1024]{1,0:T(8,128)(2,1)S(1)} collective-permute-done((bf16[256,1024]{1,0:T(8,128)(2,1)}, bf16[256,1024]{1,0:T(8,128)(2,1)S(1)}, u32[]{:S(2)}, u32[]{:S(2)}) %collective-permute-start.6) | collective-permute-done | bytes 524320 | tf_op jit(solution)/shard_map/ppermute | solution.py:381
  37.9 10.1 %collective-permute-done.5.refs_0_ = bf16[256,1024]{1,0:T(8,128)(2,1)S(1)} collective-permute-done((bf16[256,1024]{1,0:T(8,128)(2,1)}, bf16[256,1024]{1,0:T(8,128)(2,1)S(1)}, u32[]{:S(2)}, u32[]{:S(2)}) %collective-permute-start.5) | collective-permute-done | bytes 524320 | tf_op jit(solution)/shard_map/ppermute | solution.py:381
  48.8 8.2 %loc_mix.5 = (bf16[111,16,128]{2,1,0:T(8,128)(2,1)}, bf16[111,16,128]{2,1,0:T(8,128)(2,1)}, bf16[111,16,128]{2,1,0:T(8,128)(2,1)}, bf16[111,16,128]{2,1,0:T(8,12...) custom-call(s32[1]{0:T(128)} %bitcast.d_ref, ...), custom_call_target="tpu_custom_call" | custom-call | flops 20000000000 | bytes 1000 | tf_op jit(solution)/shard_map/loc_mix/pallas_call | solution.py:183
  57.0 1.0 collective-permute-start.15
  58.1 1.8 collective-permute-start.18
  59.9 6.1 %collective-permute-done.8.refs_4_ = bf16[111,16,128]{2,1,0:T(8,128)(2,1)S(1)} collective-permute-done((bf16[111,16,128]{2,1,0:T(8,128)(2,1)}, bf16[111,16,128]{2,1,0:T(8,128)(2,1)S(1)}, u32[]{:S(2)}, u32[]{:S(2)}) %collective-permute-start.8) | collective-permute-done | bytes 454688 | tf_op jit(solution)/shard_map/ppermute | solution.py:381
  66.9 3.9 %collective-permute-start.7 = (bf16[111,16,128]{2,1,0:T(8,128)(2,1)}, bf16[111,16,128]{2,1,0:T(8,128)(2,1)S(1)}, u32[]{:S(2)}, u32[]{:S(2)}) collective-permute-start(bf16[111,16,128]{2,1,0:T(8,128)(2,1)} %get-tuple-element.80.refs_4_), channel_id=1, source_target_pairs={{0,18},{2,16},{4,22},{6,20},{8,26},{10,24},{12,30},{14,28},{16,2},... | collective-permute-start | bytes 1363976 | tf_op jit(solution)/shard_map/ppermute | solution.py:381
  71.0 1.6 collective-permute-done.18.refs_5_
  72.6 3.6 %collective-permute-start.19 = (bf16[111,16,128]{2,1,0:T(8,128)(2,1)}, bf16[111,16,128]{2,1,0:T(8,128)(2,1)}, u32[]{:S(2)}, u32[]{:S(2)}) collective-permute-start(bf16[111,16,128]{2,1,0:T(8,128)(2,1)} %get-tuple-element.119.refs_10_), channel_id=1, source_target_pairs={{0,12},{2,14},{4,8},{6,10},{8,4},{10,6},{12,0},{14,2},{16,28},{18,... | collective-permute-start | bytes 1363976 | tf_op jit(solution)/shard_map/ppermute | solution.py:381
  76.2 28.4 %survive.1 = (f32[16,16,128]{2,1,0:T(8,128)}, f32[16,128]{1,0:T(8,128)}) custom-call(s32[1]{0:T(128)} %bitcast.d_ref, bf16[111,16,128]{2,1,0:T(8,128)(2,1)} %get-tuple-element.73.refs_0_, bf16[111,16,128]{2,1,0:T(8,128)(2,1)} %get-tuple-element.85.refs_1_, bf16[111,16,128]{2,1,0:T(8,128)(2,1)} %get-tuple-element.95.refs_2_, ...), custom_call_target="tpu_custom_call" | custom-call | flops 20000000000 | bytes 1000 | tf_op jit(solution)/shard_map/survive/pallas_call | solution.py:282
  106.1 4.7 %collective-permute-done.19.refs_6_ = bf16[111,16,128]{2,1,0:T(8,128)(2,1)} collective-permute-done((bf16[111,16,128]{2,1,0:T(8,128)(2,1)}, bf16[111,16,128]{2,1,0:T(8,128)(2,1)}, u32[]{:S(2)}, u32[]{:S(2)}) %collective-permute-start.19) | collective-permute-done | bytes 454688 | tf_op jit(solution)/shard_map/ppermute | solution.py:381
  110.8 1.6 pad_maximum_fusion
  112.4 6.7 %all-to-all-start = ((f32[16,17,128]{2,1,0:T(8,128)}), f32[16,17,128]{2,1,0:T(8,128)S(1)}, u32[]{:S(2)}, u32[]{:S(2)}) async-start(f32[16,17,128]{2,1,0:T(8,128)} %pad_maximum_fusion), calls=%async_computation | async-start | bytes 393216 | tf_op jit(solution)/shard_map/all_to_all | solution.py:362
  119.1 1.5 collective-permute-start.13
  120.6 3.0 %collective-permute-start.11 = (bf16[111,16,128]{2,1,0:T(8,128)(2,1)}, bf16[111,16,128]{2,1,0:T(8,128)(2,1)S(1)}, u32[]{:S(2)}, u32[]{:S(2)}) collective-permute-start(bf16[111,16,128]{2,1,0:T(8,128)(2,1)} %get-tuple-element.91.refs_12_), channel_id=1, source_target_pairs={{0,22},{2,20},{4,18},{6,16},{8,30},{10,28},{12,26},{14,24},{16,6},... | collective-permute-start | bytes 1363976 | tf_op jit(solution)/shard_map/ppermute | solution.py:381
  123.6 1.4 collective-permute-done.7.refs_1_
  125.1 25.7 %all-to-all-done = f32[16,17,128]{2,1,0:T(8,128)S(1)} async-done(((f32[16,17,128]{2,1,0:T(8,128)}), f32[16,17,128]{2,1,0:T(8,128)S(1)}, u32[]{:S(2)}, u32[]{:S(2)}) %all-to-all-start) | async-done | bytes 139296 | tf_op jit(solution)/shard_map/all_to_all | solution.py:362
  152.7 2.9 %collective-permute-start.12 = (bf16[111,16,128]{2,1,0:T(8,128)(2,1)}, bf16[111,16,128]{2,1,0:T(8,128)(2,1)S(1)}, u32[]{:S(2)}, u32[]{:S(2)}) collective-permute-start(bf16[111,16,128]{2,1,0:T(8,128)(2,1)} %get-tuple-element.108.refs_9_), channel_id=1, source_target_pairs={{0,28},{2,30},{4,24},{6,26},{8,20},{10,22},{12,16},{14,18},{16,12}... | collective-permute-start | bytes 1363976 | tf_op jit(solution)/shard_map/ppermute | solution.py:381
  155.5 5.6 %turn.2.refs_8_ = bf16[2,111,64,256]{3,2,1,0:T(8,128)(2,1)} custom-call(s32[1]{0:T(128)} %bitcast.d_ref, bf16[111,16,128]{2,1,0:T(8,128)(2,1)} %get-tuple-element.96.refs_3_.refs_0_, bf16[111,16,128]{2,1,0:T(8,128)(2,1)} %collective-permute-done.15.refs_1_, bf16[111,16,128]{2,1,0:T(8,128)(2,1)} %collective-permute-done.16.refs_2_, ...), custom_call_target="tpu_custom_call" | custom-call | flops 20000000000 | bytes 1000 | tf_op jit(solution)/shard_map/turn/pallas_call | solution.py:339
  161.1 9.9 %collective-permute-done.13.refs_7_ = bf16[111,16,128]{2,1,0:T(8,128)(2,1)S(1)} collective-permute-done((bf16[111,16,128]{2,1,0:T(8,128)(2,1)}, bf16[111,16,128]{2,1,0:T(8,128)(2,1)S(1)}, u32[]{:S(2)}, u32[]{:S(2)}) %collective-permute-start.13) | collective-permute-done | bytes 454688 | tf_op jit(solution)/shard_map/ppermute | solution.py:381
  171.0 6.2 %collective-permute-done.11.refs_3_ = bf16[111,16,128]{2,1,0:T(8,128)(2,1)S(1)} collective-permute-done((bf16[111,16,128]{2,1,0:T(8,128)(2,1)}, bf16[111,16,128]{2,1,0:T(8,128)(2,1)S(1)}, u32[]{:S(2)}, u32[]{:S(2)}) %collective-permute-start.11) | collective-permute-done | bytes 454688 | tf_op jit(solution)/shard_map/ppermute | solution.py:381
  177.2 12.0 %collective-permute-done.12.refs_6_ = bf16[111,16,128]{2,1,0:T(8,128)(2,1)S(1)} collective-permute-done((bf16[111,16,128]{2,1,0:T(8,128)(2,1)}, bf16[111,16,128]{2,1,0:T(8,128)(2,1)S(1)}, u32[]{:S(2)}, u32[]{:S(2)}) %collective-permute-start.12) | collective-permute-done | bytes 454688 | tf_op jit(solution)/shard_map/ppermute | solution.py:381
  189.1 3.0 %turn.3 = bf16[2,111,64,256]{3,2,1,0:T(8,128)(2,1)} custom-call(s32[1]{0:T(128)} %bitcast.d_ref, bf16[111,16,128]{2,1,0:T(8,128)(2,1)S(1)} %collective-permute-done.4.refs_0_, bf16[111,16,128]{2,1,0:T(8,128)(2,1)S(1)} %collective-permute-done.7.refs_1_, bf16[111,16,128]{2,1,0:T(8,128)(2,1)S(1)} %collective-permute-done.9.refs_2_, ...), custom_call_target="tpu_custom_call", output_to_operand_aliasing={{}: (9, {})} | custom-call | flops 20000000000 | bytes 1000 | tf_op jit(solution)/shard_map/turn/pallas_call | solution.py:339
  (53 shorter events, 6.9 us)
Async XLA Ops:
  0.6 12.2 %collective-permute-start.1 = (bf16[64,1024]{1,0:T(8,128)(2,1)}, bf16[64,1024]{1,0:T(8,128)(2,1)S(1)}, u32[]{:S(2)}, u32[]{:S(2)}) collective-permute-start(bf16[64,1024]{1,0:T(8,128)(2,1)} %refs_3_), channel_id=1, source_target_pairs={{0,16},{2,18},{4,20},{6,22},{8,24},{10,26},{12,28},{14,30},{16,0},... | collective-permute-start | bytes 393224 | tf_op jit(solution)/shard_map/ppermute | solution.py:381
  0.7 12.1 %collective-permute-start = (bf16[64,1024]{1,0:T(8,128)(2,1)}, bf16[64,1024]{1,0:T(8,128)(2,1)S(1)}, u32[]{:S(2)}, u32[]{:S(2)}) collective-permute-start(bf16[64,1024]{1,0:T(8,128)(2,1)} %refs_3_), channel_id=1, source_target_pairs={{0,8},{2,10},{4,12},{6,14},{8,0},{10,2},{12,4},{14,6},{16,24},{18,... | collective-permute-start | bytes 393224 | tf_op jit(solution)/shard_map/ppermute | solution.py:381
  2.1 13.6 %collective-permute-start.2 = (bf16[64,1024]{1,0:T(8,128)(2,1)}, bf16[64,1024]{1,0:T(8,128)(2,1)S(1)}, u32[]{:S(2)}, u32[]{:S(2)}) collective-permute-start(bf16[64,1024]{1,0:T(8,128)(2,1)} %refs_3_), channel_id=1, source_target_pairs={{0,24},{2,26},{4,28},{6,30},{8,16},{10,18},{12,20},{14,22},{16,8},... | collective-permute-start | bytes 393224 | tf_op jit(solution)/shard_map/ppermute | solution.py:381
  12.8 2.8 %copy-start.9 = (bf16[64,1024]{1,0:T(8,128)(2,1)}, bf16[64,1024]{1,0:T(8,128)(2,1)S(1)}, u32[]{:S(2)}) copy-start(bf16[64,1024]{1,0:T(8,128)(2,1)S(1)} %collective-permute-done.1.refs_0_) | copy-start | bytes 393220
  12.8 2.8 %copy-start.10 = (bf16[64,1024]{1,0:T(8,128)(2,1)}, bf16[64,1024]{1,0:T(8,128)(2,1)S(1)}, u32[]{:S(2)}) copy-start(bf16[64,1024]{1,0:T(8,128)(2,1)S(1)} %collective-permute-done.refs_2_) | copy-start | bytes 393220
  22.6 3.6 %collective-permute-start.3 = (bf16[256,1024]{1,0:T(8,128)(2,1)}, bf16[256,1024]{1,0:T(8,128)(2,1)S(1)}, u32[]{:S(2)}, u32[]{:S(2)}) collective-permute-start(bf16[256,1024]{1,0:T(8,128)(2,1)} %get-tuple-element.70), channel_id=1, source_target_pairs={{0,2},{2,0},{4,6},{6,4},{8,10},{10,8},{12,14},{14,12},{16,18},{18,... | collective-permute-start | bytes 1572872 | tf_op jit(solution)/shard_map/ppermute | solution.py:381
  23.2 14.7 %collective-permute-start.6 = (bf16[256,1024]{1,0:T(8,128)(2,1)}, bf16[256,1024]{1,0:T(8,128)(2,1)S(1)}, u32[]{:S(2)}, u32[]{:S(2)}) collective-permute-start(bf16[256,1024]{1,0:T(8,128)(2,1)} %get-tuple-element.70), channel_id=1, source_target_pairs={{0,6},{2,4},{4,2},{6,0},{8,14},{10,12},{12,10},{14,8},{16,22},{18,... | collective-permute-start | bytes 1572872 | tf_op jit(solution)/shard_map/ppermute | solution.py:381
  24.3 23.6 %collective-permute-start.5 = (bf16[256,1024]{1,0:T(8,128)(2,1)}, bf16[256,1024]{1,0:T(8,128)(2,1)S(1)}, u32[]{:S(2)}, u32[]{:S(2)}) collective-permute-start(bf16[256,1024]{1,0:T(8,128)(2,1)} %get-tuple-element.70), channel_id=1, source_target_pairs={{0,4},{2,6},{4,0},{6,2},{8,12},{10,14},{12,8},{14,10},{16,20},{18,... | collective-permute-start | bytes 1572872 | tf_op jit(solution)/shard_map/ppermute | solution.py:381
  24.6 35.3 %collective-permute-start.4 = (bf16[111,16,128]{2,1,0:T(8,128)(2,1)}, bf16[111,16,128]{2,1,0:T(8,128)(2,1)S(1)}, u32[]{:S(2)}, u32[]{:S(2)}) collective-permute-start(bf16[111,16,128]{2,1,0:T(8,128)(2,1)} %get-tuple-element.73.refs_0_), channel_id=1, source_target_pairs={{0,16},{2,18},{4,20},{6,22},{8,24},{10,26},{12,28},{14,30},{16,0},... | collective-permute-start | bytes 1363976 | tf_op jit(solution)/shard_map/ppermute | solution.py:381
  24.6 41.4 %collective-permute-start.8 = (bf16[111,16,128]{2,1,0:T(8,128)(2,1)}, bf16[111,16,128]{2,1,0:T(8,128)(2,1)S(1)}, u32[]{:S(2)}, u32[]{:S(2)}) collective-permute-start(bf16[111,16,128]{2,1,0:T(8,128)(2,1)} %get-tuple-element.85.refs_1_), channel_id=1, source_target_pairs={{0,24},{2,26},{4,28},{6,30},{8,16},{10,18},{12,20},{14,22},{16,8},... | collective-permute-start | bytes 1363976 | tf_op jit(solution)/shard_map/ppermute | solution.py:381
  26.3 1.9 copy-start.4
  26.3 30.7 %collective-permute-start.14 = (bf16[111,16,128]{2,1,0:T(8,128)(2,1)}, bf16[111,16,128]{2,1,0:T(8,128)(2,1)S(1)}, u32[]{:S(2)}, u32[]{:S(2)}) collective-permute-start(bf16[111,16,128]{2,1,0:T(8,128)(2,1)} %get-tuple-element.95.refs_2_), channel_id=1, source_target_pairs={{0,8},{2,10},{4,12},{6,14},{8,0},{10,2},{12,4},{14,6},{16,24},{18,... | collective-permute-start | bytes 1363976 | tf_op jit(solution)/shard_map/ppermute | solution.py:381
  37.9 10.1 %copy-start.2 = (bf16[256,1024]{1,0:T(8,128)(2,1)}, bf16[256,1024]{1,0:T(8,128)(2,1)S(1)}, u32[]{:S(2)}) copy-start(bf16[256,1024]{1,0:T(8,128)(2,1)S(1)} %collective-permute-done.6.refs_1_) | copy-start | bytes 1572868
  48.8 8.2 %copy-start.8 = (bf16[111,16,128]{2,1,0:T(8,128)(2,1)S(1)}, bf16[111,16,128]{2,1,0:T(8,128)(2,1)}, u32[]{:S(2)}) copy-start(bf16[111,16,128]{2,1,0:T(8,128)(2,1)} %get-tuple-element.111.refs_7_) | copy-start | bytes 1363972
  48.8 9.3 %copy-start.7 = (bf16[111,16,128]{2,1,0:T(8,128)(2,1)S(1)}, bf16[111,16,128]{2,1,0:T(8,128)(2,1)}, u32[]{:S(2)}) copy-start(bf16[111,16,128]{2,1,0:T(8,128)(2,1)} %get-tuple-element.117.refs_6_) | copy-start | bytes 1363972
  48.8 17.2 %copy-start.6 = (bf16[111,16,128]{2,1,0:T(8,128)(2,1)S(1)}, bf16[111,16,128]{2,1,0:T(8,128)(2,1)}, u32[]{:S(2)}) copy-start(bf16[111,16,128]{2,1,0:T(8,128)(2,1)} %get-tuple-element.90.refs_5_) | copy-start | bytes 1363972
  57.0 9.0 %copy-start.5 = (bf16[111,16,128]{2,1,0:T(8,128)(2,1)}, bf16[111,16,128]{2,1,0:T(8,128)(2,1)S(1)}, u32[]{:S(2)}) copy-start(bf16[111,16,128]{2,1,0:T(8,128)(2,1)S(1)} %collective-permute-done.14.refs_4_) | copy-start | bytes 1363972
  57.0 13.7 %collective-permute-start.15 = (bf16[111,16,128]{2,1,0:T(8,128)(2,1)S(1)}, bf16[111,16,128]{2,1,0:T(8,128)(2,1)}, u32[]{:S(2)}, u32[]{:S(2)}) collective-permute-start(bf16[111,16,128]{2,1,0:T(8,128)(2,1)S(1)} %copy-done.8), channel_id=1, source_target_pairs={{0,2},{2,0},{4,6},{6,4},{8,10},{10,8},{12,14},{14,12},{16,18},{18,... | collective-permute-start | bytes 1363976 | tf_op jit(solution)/shard_map/ppermute | solution.py:381
  58.1 14.6 %collective-permute-start.18 = (bf16[111,16,128]{2,1,0:T(8,128)(2,1)S(1)}, bf16[111,16,128]{2,1,0:T(8,128)(2,1)}, u32[]{:S(2)}, u32[]{:S(2)}) collective-permute-start(bf16[111,16,128]{2,1,0:T(8,128)(2,1)S(1)} %copy-done.7), channel_id=1, source_target_pairs={{0,10},{2,8},{4,14},{6,12},{8,2},{10,0},{12,6},{14,4},{16,26},{18,... | collective-permute-start | bytes 1363976 | tf_op jit(solution)/shard_map/ppermute | solution.py:381
  66.0 53.1 %collective-permute-start.9 = (bf16[111,16,128]{2,1,0:T(8,128)(2,1)}, bf16[111,16,128]{2,1,0:T(8,128)(2,1)S(1)}, u32[]{:S(2)}, u32[]{:S(2)}) collective-permute-start(bf16[111,16,128]{2,1,0:T(8,128)(2,1)} %get-tuple-element.87.refs_8_), channel_id=1, source_target_pairs={{0,20},{2,22},{4,16},{6,18},{8,28},{10,30},{12,24},{14,26},{16,4},... | collective-permute-start | bytes 1363976 | tf_op jit(solution)/shard_map/ppermute | solution.py:381
  66.0 54.6 %collective-permute-start.10 = (bf16[111,16,128]{2,1,0:T(8,128)(2,1)S(1)}, bf16[111,16,128]{2,1,0:T(8,128)(2,1)S(1)}, u32[]{:S(2)}, u32[]{:S(2)}) collective-permute-start(bf16[111,16,128]{2,1,0:T(8,128)(2,1)S(1)} %copy-done.6), channel_id=1, source_target_pairs={{0,26},{2,24},{4,30},{6,28},{8,18},{10,16},{12,22},{14,20},{16,10}... | collective-permute-start | bytes 1363976 | tf_op jit(solution)/shard_map/ppermute | solution.py:381
  66.9 58.2 %collective-permute-start.7 = (bf16[111,16,128]{2,1,0:T(8,128)(2,1)}, bf16[111,16,128]{2,1,0:T(8,128)(2,1)S(1)}, u32[]{:S(2)}, u32[]{:S(2)}) collective-permute-start(bf16[111,16,128]{2,1,0:T(8,128)(2,1)} %get-tuple-element.80.refs_4_), channel_id=1, source_target_pairs={{0,18},{2,16},{4,22},{6,20},{8,26},{10,24},{12,30},{14,28},{16,2},... | collective-permute-start | bytes 1363976 | tf_op jit(solution)/shard_map/ppermute | solution.py:381
  70.8 34.8 %collective-permute-start.16 = (bf16[111,16,128]{2,1,0:T(8,128)(2,1)}, bf16[111,16,128]{2,1,0:T(8,128)(2,1)}, u32[]{:S(2)}, u32[]{:S(2)}) collective-permute-start(bf16[111,16,128]{2,1,0:T(8,128)(2,1)} %get-tuple-element.113.refs_11_), channel_id=1, source_target_pairs={{0,4},{2,6},{4,0},{6,2},{8,12},{10,14},{12,8},{14,10},{16,20},{18,... | collective-permute-start | bytes 1363976 | tf_op jit(solution)/shard_map/ppermute | solution.py:381
  72.6 38.2 %collective-permute-start.19 = (bf16[111,16,128]{2,1,0:T(8,128)(2,1)}, bf16[111,16,128]{2,1,0:T(8,128)(2,1)}, u32[]{:S(2)}, u32[]{:S(2)}) collective-permute-start(bf16[111,16,128]{2,1,0:T(8,128)(2,1)} %get-tuple-element.119.refs_10_), channel_id=1, source_target_pairs={{0,12},{2,14},{4,8},{6,10},{8,4},{10,6},{12,0},{14,2},{16,28},{18,... | collective-permute-start | bytes 1363976 | tf_op jit(solution)/shard_map/ppermute | solution.py:381
  105.6 50.0 %collective-permute-start.17 = (bf16[111,16,128]{2,1,0:T(8,128)(2,1)}, bf16[111,16,128]{2,1,0:T(8,128)(2,1)}, u32[]{:S(2)}, u32[]{:S(2)}) collective-permute-start(bf16[111,16,128]{2,1,0:T(8,128)(2,1)} %get-tuple-element.115.refs_15_), channel_id=1, source_target_pairs={{0,6},{2,4},{4,2},{6,0},{8,14},{10,12},{12,10},{14,8},{16,22},{18,... | collective-permute-start | bytes 1363976 | tf_op jit(solution)/shard_map/ppermute | solution.py:381
  110.8 44.7 %collective-permute-start.20 = (bf16[111,16,128]{2,1,0:T(8,128)(2,1)}, bf16[111,16,128]{2,1,0:T(8,128)(2,1)}, u32[]{:S(2)}, u32[]{:S(2)}) collective-permute-start(bf16[111,16,128]{2,1,0:T(8,128)(2,1)} %get-tuple-element.121.refs_14_), channel_id=1, source_target_pairs={{0,14},{2,12},{4,10},{6,8},{8,6},{10,4},{12,2},{14,0},{16,30},{18,... | collective-permute-start | bytes 1363976 | tf_op jit(solution)/shard_map/ppermute | solution.py:381
  112.4 38.3 %all-to-all-start = ((f32[16,17,128]{2,1,0:T(8,128)}), f32[16,17,128]{2,1,0:T(8,128)S(1)}, u32[]{:S(2)}, u32[]{:S(2)}) async-start(f32[16,17,128]{2,1,0:T(8,128)} %pad_maximum_fusion), calls=%async_computation | async-start | bytes 393216 | tf_op jit(solution)/shard_map/all_to_all | solution.py:362
  119.1 51.9 %collective-permute-start.13 = (bf16[111,16,128]{2,1,0:T(8,128)(2,1)}, bf16[111,16,128]{2,1,0:T(8,128)(2,1)S(1)}, u32[]{:S(2)}, u32[]{:S(2)}) collective-permute-start(bf16[111,16,128]{2,1,0:T(8,128)(2,1)} %get-tuple-element.109.refs_13_), channel_id=1, source_target_pairs={{0,30},{2,28},{4,26},{6,24},{8,22},{10,20},{12,18},{14,16},{16,14}... | collective-permute-start | bytes 1363976 | tf_op jit(solution)/shard_map/ppermute | solution.py:381
  120.6 56.6 %collective-permute-start.11 = (bf16[111,16,128]{2,1,0:T(8,128)(2,1)}, bf16[111,16,128]{2,1,0:T(8,128)(2,1)S(1)}, u32[]{:S(2)}, u32[]{:S(2)}) collective-permute-start(bf16[111,16,128]{2,1,0:T(8,128)(2,1)} %get-tuple-element.91.refs_12_), channel_id=1, source_target_pairs={{0,22},{2,20},{4,18},{6,16},{8,30},{10,28},{12,26},{14,24},{16,6},... | collective-permute-start | bytes 1363976 | tf_op jit(solution)/shard_map/ppermute | solution.py:381
  152.4 36.8 %copy-start = (f32[256,128]{0,1:T(8,128)}, f32[256,128]{0,1:T(8,128)S(1)}, u32[]{:S(2)}) copy-start(f32[256,128]{0,1:T(8,128)S(1)} %copy.15) | copy-start | bytes 393220
  152.6 36.5 %copy-start.1 = (f32[2,4,256]{2,1,0:T(4,128)}, f32[2,4,256]{2,1,0:T(4,128)S(1)}, u32[]{:S(2)}) copy-start(f32[2,4,256]{2,1,0:T(4,128)S(1)} %reshape.37.refs_10_) | copy-start | bytes 24580
  152.7 36.5 %collective-permute-start.12 = (bf16[111,16,128]{2,1,0:T(8,128)(2,1)}, bf16[111,16,128]{2,1,0:T(8,128)(2,1)S(1)}, u32[]{:S(2)}, u32[]{:S(2)}) collective-permute-start(bf16[111,16,128]{2,1,0:T(8,128)(2,1)} %get-tuple-element.108.refs_9_), channel_id=1, source_target_pairs={{0,28},{2,30},{4,24},{6,26},{8,20},{10,22},{12,16},{14,18},{16,12}... | collective-permute-start | bytes 1363976 | tf_op jit(solution)/shard_map/ppermute | solution.py:381
  (2 other events, 1.5 us)

commit v8 on v7

--- a/solution.py
+++ b/solution.py
@@ -109,7 +109,7 @@
         age_mix_kernel,
         out_shape=(
             jax.ShapeDtypeStruct(x.shape, jnp.bfloat16),
-            jax.ShapeDtypeStruct((8, LANES), jnp.float32),
+            pltpu.HBM((8, LANES), jnp.float32),
         ),
         grid=(sexes, tiles),
         in_specs=[pl.BlockSpec((ages, ages), lambda s, t: (0, 0))] + [part_spec(p) for p in range(PARTS)],
@@ -175,7 +175,7 @@
     def mean_spec(b):
         return pl.BlockSpec((block, sexes, LANES), lambda i, d: (i, 0, (d[0] ^ b) // 2))
 
-    outs = [msg] * len(every) + [jax.ShapeDtypeStruct(done.shape, done.dtype)]
+    outs = [msg] * len(every) + [pltpu.HBM(done.shape, done.dtype)]
     out_specs = [pl.BlockSpec((block, per_age, LANES), lambda i, d: (i, 0, 0))] * len(every) + [flag_spec]
     if len(factors) > len(groups):
         outs.append(jax.ShapeDtypeStruct((4 * HALF, cols), jnp.bfloat16))
@@ -189,10 +189,10 @@
             in_specs=[pl.BlockSpec((sexes, block * per_age, cols), lambda i, d: (0, i, 0))]
             + [pl.BlockSpec(f.shape, lambda i, d: (0, 0)) for f in factors]
             + [mean_spec(b) for b in every]
-            + [flag_spec],
+            + [pl.BlockSpec(memory_space=pl.ANY)],
             out_specs=out_specs,
         ),
-        compiler_params=pltpu.CompilerParams(vmem_limit_bytes=57 << 20),
+        compiler_params=pltpu.CompilerParams(vmem_limit_bytes=(57 if len(factors) == len(groups) else 52) << 20),
         cost_estimate=LONG,
         name="loc_mix",
     )(device, mixed, *factors, *([mean_t] * len(every)), done)
@@ -291,7 +291,7 @@
             in_specs=[whole(ages, rows, LANES)] * len(every)
             + [pop_spec(b) for b in every]
             + [region_spec(b) for b in every]
-            + [whole(*done.shape)],
+            + [pl.BlockSpec(memory_space=pl.ANY)],
             out_specs=(whole(locs, rows, LANES), whole(rows, LANES)),
             scratch_shapes=[
                 pltpu.VMEM((ages * rows, 4 * LANES), jnp.bfloat16),

time: 194 us -> 194 us (level)
  no operation moved by 1% of the time
where the time goes in v8:
time: 194 us; the launch traced here: 192 us
  waiting for transfers between devices  83.7 us (43%)
  Pallas kernels  67.1 us (35%)
  starting transfers between devices  34.4 us (18%)
  local copies, waits for them, and re-layouts  4.37 us (2%)
    ppermute x21, waiting for transfers between devices, swap(): return lax.ppermute(x, 'loc', [(i, i ^ bits) for i in range(devices)])  59.2 us
    pallas_call x1, Pallas kernels, survive(): pl.pallas_call(survive_kernel, out_shape=(jax.ShapeDtypeStruct((locs, row...  28.4 us
    ppermute x21, starting transfers between devices, swap(): return lax.ppermute(x, 'loc', [(i, i ^ bits) for i in range(devices)])  27.7 us
    all_to_all x1, waiting for transfers between devices, exchange(): lax.all_to_all(packed, 'loc', split_axis=0, concat_axis=0, tiled=True)  24.4 us
    pallas_call x3, Pallas kernels, loc_mix(): pl.pallas_call(functools.partial(loc_mix_kernel, groups, len(factors)), o...  20.7 us
    pallas_call x1, Pallas kernels, age_mix(): pl.pallas_call(age_mix_kernel, out_shape=(jax.ShapeDtypeStruct(x.shape, j...  9.57 us
    pallas_call x2, Pallas kernels, turn(): pl.pallas_call(functools.partial(turn_kernel, near), out_shape=out_shape,...  8.53 us
    all_to_all x1, starting transfers between devices, exchange(): lax.all_to_all(packed, 'loc', split_axis=0, concat_axis=0, tiled=True)  6.65 us
  transfers between devices with their start and end apart: 22, of which 11 were waited for; matrix products, arithmetic and copies ran while one was open for 2% of the time, Pallas kernels for 30%

profile of v8, /device:TPU:17, one launch (start us, length us, event | category | flops | bytes accessed | tf_op | source)
XLA Modules:
  0.0 191.9 jit_solution(13516653535225222627)
XLA Ops:
  0.7 1.4 collective-permute-start
  2.1 1.3 collective-permute-start.2
  3.3 9.6 %age_mix.1 = (bf16[2,111,2,8,1024]{4,3,2,1,0:T(8,128)(2,1)}, f32[8,128]{1,0:T(8,128)}) custom-call(bf16[111,111]{1,0:T(8,128)(2,1)} %age_ref.1, bf16[2,111,2,8,1024]{4,3,2,1,0:T(8,128)(2,1)} %bitcast.39, bf16[2,111,2,8,1024]{4,3,2,1,0:T(8,128)(2,1)} %bitcast.40, bf16[2,111,2,8,1024]{4,3,2,1,0:T(8,128)(2,1)} %bitcast.41, bf16[2,111,2,8,1024]{4,3,2,1,0:T(8,128)(2,1)} %bitcast.42), custom_call_target="tpu_custom_call" | custom-call | flops 20000000000 | bytes 1000 | tf_op jit(solution)/shard_map/age_mix/pallas_call | solution.py:108
  12.9 2.7 %collective-permute-done.2.refs_1_ = bf16[64,1024]{1,0:T(8,128)(2,1)S(1)} collective-permute-done((bf16[64,1024]{1,0:T(8,128)(2,1)}, bf16[64,1024]{1,0:T(8,128)(2,1)S(1)}, u32[]{:S(2)}, u32[]{:S(2)}) %collective-permute-start.2) | collective-permute-done | bytes 131104 | tf_op jit(solution)/shard_map/ppermute | solution.py:381
  16.3 6.1 %loc_mix.3 = (bf16[111,16,128]{2,1,0:T(8,128)(2,1)}, bf16[111,16,128]{2,1,0:T(8,128)(2,1)}, bf16[111,16,128]{2,1,0:T(8,128)(2,1)}, bf16[111,16,128]{2,1,0:T(8,12...) custom-call(s32[1]{0:T(128)} %bitcast.d_ref, bf16[2,1776,1024]{2,1,0:T(8,128)(2,1)} %bitcast.75, ...), custom_call_target="tpu_custom_call" | custom-call | flops 20000000000 | bytes 1000 | tf_op jit(solution)/shard_map/loc_mix/pallas_call | solution.py:183
  23.0 1.1 collective-permute-start.6
  24.4 1.7 collective-permute-start.8
  26.1 1.8 collective-permute-start.14
  27.9 6.3 %loc_mix.4 = (bf16[111,16,128]{2,1,0:T(8,128)(2,1)}, bf16[111,16,128]{2,1,0:T(8,128)(2,1)}, bf16[111,16,128]{2,1,0:T(8,128)(2,1)}, bf16[111,16,128]{2,1,0:T(8,128)(2,1)}, f32[8,128]{1,0:T(8,128)}) custom-call(s32[1]{0:T(128)} %bitcast.d_ref, bf16[2,1776,1024]{2,1,0:T(8,128)(2,1)} %bitcast.76, bf16[256,1024]{1,0:T(8,128)(2,1)} %copy-done.7, ...), custom_call_target="tpu_custom_call" | custom-call | flops 20000000000 | bytes 1000 | tf_op jit(solution)/shard_map/loc_mix/pallas_call | solution.py:183
  34.3 3.2 %collective-permute-done.6.refs_1_ = bf16[256,1024]{1,0:T(8,128)(2,1)S(1)} collective-permute-done((bf16[256,1024]{1,0:T(8,128)(2,1)S(1)}, bf16[256,1024]{1,0:T(8,128)(2,1)S(1)}, u32[]{:S(2)}, u32[]{:S(2)}) %collective-permute-start.6) | collective-permute-done | bytes 524320 | tf_op jit(solution)/shard_map/ppermute | solution.py:381
  37.5 10.1 %collective-permute-done.5.refs_0_ = bf16[256,1024]{1,0:T(8,128)(2,1)S(1)} collective-permute-done((bf16[256,1024]{1,0:T(8,128)(2,1)S(1)}, bf16[256,1024]{1,0:T(8,128)(2,1)S(1)}, u32[]{:S(2)}, u32[]{:S(2)}) %collective-permute-start.5) | collective-permute-done | bytes 524320 | tf_op jit(solution)/shard_map/ppermute | solution.py:381
  48.4 8.2 %loc_mix.5 = (bf16[111,16,128]{2,1,0:T(8,128)(2,1)}, bf16[111,16,128]{2,1,0:T(8,128)(2,1)}, bf16[111,16,128]{2,1,0:T(8,128)(2,1)}, bf16[111,16,128]{2,1,0:T(8,12...) custom-call(s32[1]{0:T(128)} %bitcast.d_ref, ...), custom_call_target="tpu_custom_call" | custom-call | flops 20000000000 | bytes 1000 | tf_op jit(solution)/shard_map/loc_mix/pallas_call | solution.py:183
  56.6 1.1 collective-permute-start.15
  57.7 2.0 %collective-permute-start.18 = (bf16[111,16,128]{2,1,0:T(8,128)(2,1)S(1)}, bf16[111,16,128]{2,1,0:T(8,128)(2,1)}, u32[]{:S(2)}, u32[]{:S(2)}) collective-permute-start(bf16[111,16,128]{2,1,0:T(8,128)(2,1)S(1)} %copy-done.10), channel_id=1, source_target_pairs={{0,10},{2,8},{4,14},{6,12},{8,2},{10,0},{12,6},{14,4},{16,26},{18,... | collective-permute-start | bytes 1363976 | tf_op jit(solution)/shard_map/ppermute | solution.py:381
  59.7 6.2 %collective-permute-done.8.refs_4_ = bf16[111,16,128]{2,1,0:T(8,128)(2,1)S(1)} collective-permute-done((bf16[111,16,128]{2,1,0:T(8,128)(2,1)}, bf16[111,16,128]{2,1,0:T(8,128)(2,1)S(1)}, u32[]{:S(2)}, u32[]{:S(2)}) %collective-permute-start.8) | collective-permute-done | bytes 454688 | tf_op jit(solution)/shard_map/ppermute | solution.py:381
  66.7 3.9 %collective-permute-start.7 = (bf16[111,16,128]{2,1,0:T(8,128)(2,1)}, bf16[111,16,128]{2,1,0:T(8,128)(2,1)S(1)}, u32[]{:S(2)}, u32[]{:S(2)}) collective-permute-start(bf16[111,16,128]{2,1,0:T(8,128)(2,1)} %get-tuple-element.80.refs_4_), channel_id=1, source_target_pairs={{0,18},{2,16},{4,22},{6,20},{8,26},{10,24},{12,30},{14,28},{16,2},... | collective-permute-start | bytes 1363976 | tf_op jit(solution)/shard_map/ppermute | solution.py:381
  70.8 1.7 collective-permute-done.18.refs_5_
  72.5 3.5 %collective-permute-start.19 = (bf16[111,16,128]{2,1,0:T(8,128)(2,1)}, bf16[111,16,128]{2,1,0:T(8,128)(2,1)}, u32[]{:S(2)}, u32[]{:S(2)}) collective-permute-start(bf16[111,16,128]{2,1,0:T(8,128)(2,1)} %get-tuple-element.119.refs_10_), channel_id=1, source_target_pairs={{0,12},{2,14},{4,8},{6,10},{8,4},{10,6},{12,0},{14,2},{16,28},{18,... | collective-permute-start | bytes 1363976 | tf_op jit(solution)/shard_map/ppermute | solution.py:381
  76.0 28.4 %survive.1 = (f32[16,16,128]{2,1,0:T(8,128)}, f32[16,128]{1,0:T(8,128)}) custom-call(s32[1]{0:T(128)} %bitcast.d_ref, bf16[111,16,128]{2,1,0:T(8,128)(2,1)} %get-tuple-element.73.refs_0_, bf16[111,16,128]{2,1,0:T(8,128)(2,1)} %get-tuple-element.85.refs_1_, bf16[111,16,128]{2,1,0:T(8,128)(2,1)} %get-tuple-element.95.refs_2_, ...), custom_call_target="tpu_custom_call" | custom-call | flops 20000000000 | bytes 1000 | tf_op jit(solution)/shard_map/survive/pallas_call | solution.py:282
  105.9 4.7 %collective-permute-done.19.refs_6_ = bf16[111,16,128]{2,1,0:T(8,128)(2,1)} collective-permute-done((bf16[111,16,128]{2,1,0:T(8,128)(2,1)}, bf16[111,16,128]{2,1,0:T(8,128)(2,1)}, u32[]{:S(2)}, u32[]{:S(2)}) %collective-permute-start.19) | collective-permute-done | bytes 454688 | tf_op jit(solution)/shard_map/ppermute | solution.py:381
  110.6 1.6 pad_maximum_fusion
  112.2 6.7 %all-to-all-start = ((f32[16,17,128]{2,1,0:T(8,128)}), f32[16,17,128]{2,1,0:T(8,128)S(1)}, u32[]{:S(2)}, u32[]{:S(2)}) async-start(f32[16,17,128]{2,1,0:T(8,128)} %pad_maximum_fusion), calls=%async_computation | async-start | bytes 393216 | tf_op jit(solution)/shard_map/all_to_all | solution.py:362
  118.9 1.5 collective-permute-start.13
  120.4 3.0 %collective-permute-start.11 = (bf16[111,16,128]{2,1,0:T(8,128)(2,1)}, bf16[111,16,128]{2,1,0:T(8,128)(2,1)S(1)}, u32[]{:S(2)}, u32[]{:S(2)}) collective-permute-start(bf16[111,16,128]{2,1,0:T(8,128)(2,1)} %get-tuple-element.91.refs_12_), channel_id=1, source_target_pairs={{0,22},{2,20},{4,18},{6,16},{8,30},{10,28},{12,26},{14,24},{16,6},... | collective-permute-start | bytes 1363976 | tf_op jit(solution)/shard_map/ppermute | solution.py:381
  123.4 2.6 %collective-permute-done.7.refs_1_ = bf16[111,16,128]{2,1,0:T(8,128)(2,1)S(1)} collective-permute-done((bf16[111,16,128]{2,1,0:T(8,128)(2,1)}, bf16[111,16,128]{2,1,0:T(8,128)(2,1)S(1)}, u32[]{:S(2)}, u32[]{:S(2)}) %collective-permute-start.7) | collective-permute-done | bytes 454688 | tf_op jit(solution)/shard_map/ppermute | solution.py:381
  126.1 24.4 %all-to-all-done = f32[16,17,128]{2,1,0:T(8,128)S(1)} async-done(((f32[16,17,128]{2,1,0:T(8,128)}), f32[16,17,128]{2,1,0:T(8,128)S(1)}, u32[]{:S(2)}, u32[]{:S(2)}) %all-to-all-start) | async-done | bytes 139296 | tf_op jit(solution)/shard_map/all_to_all | solution.py:362
  152.4 2.9 %collective-permute-start.12 = (bf16[111,16,128]{2,1,0:T(8,128)(2,1)}, bf16[111,16,128]{2,1,0:T(8,128)(2,1)S(1)}, u32[]{:S(2)}, u32[]{:S(2)}) collective-permute-start(bf16[111,16,128]{2,1,0:T(8,128)(2,1)} %get-tuple-element.108.refs_9_), channel_id=1, source_target_pairs={{0,28},{2,30},{4,24},{6,26},{8,20},{10,22},{12,16},{14,18},{16,12}... | collective-permute-start | bytes 1363976 | tf_op jit(solution)/shard_map/ppermute | solution.py:381
  155.3 5.6 %turn.2.refs_8_ = bf16[2,111,64,256]{3,2,1,0:T(8,128)(2,1)} custom-call(s32[1]{0:T(128)} %bitcast.d_ref, bf16[111,16,128]{2,1,0:T(8,128)(2,1)} %get-tuple-element.96.refs_3_.refs_0_, bf16[111,16,128]{2,1,0:T(8,128)(2,1)} %collective-permute-done.15.refs_1_, bf16[111,16,128]{2,1,0:T(8,128)(2,1)} %collective-permute-done.16.refs_2_, ...), custom_call_target="tpu_custom_call" | custom-call | flops 20000000000 | bytes 1000 | tf_op jit(solution)/shard_map/turn/pallas_call | solution.py:339
  160.9 9.8 %collective-permute-done.13.refs_7_ = bf16[111,16,128]{2,1,0:T(8,128)(2,1)S(1)} collective-permute-done((bf16[111,16,128]{2,1,0:T(8,128)(2,1)}, bf16[111,16,128]{2,1,0:T(8,128)(2,1)S(1)}, u32[]{:S(2)}, u32[]{:S(2)}) %collective-permute-start.13) | collective-permute-done | bytes 454688 | tf_op jit(solution)/shard_map/ppermute | solution.py:381
  170.7 6.3 %collective-permute-done.11.refs_3_ = bf16[111,16,128]{2,1,0:T(8,128)(2,1)S(1)} collective-permute-done((bf16[111,16,128]{2,1,0:T(8,128)(2,1)}, bf16[111,16,128]{2,1,0:T(8,128)(2,1)S(1)}, u32[]{:S(2)}, u32[]{:S(2)}) %collective-permute-start.11) | collective-permute-done | bytes 454688 | tf_op jit(solution)/shard_map/ppermute | solution.py:381
  177.1 11.9 %collective-permute-done.12.refs_6_ = bf16[111,16,128]{2,1,0:T(8,128)(2,1)S(1)} collective-permute-done((bf16[111,16,128]{2,1,0:T(8,128)(2,1)}, bf16[111,16,128]{2,1,0:T(8,128)(2,1)S(1)}, u32[]{:S(2)}, u32[]{:S(2)}) %collective-permute-start.12) | collective-permute-done | bytes 454688 | tf_op jit(solution)/shard_map/ppermute | solution.py:381
  188.9 3.0 %turn.3 = bf16[2,111,64,256]{3,2,1,0:T(8,128)(2,1)} custom-call(s32[1]{0:T(128)} %bitcast.d_ref, bf16[111,16,128]{2,1,0:T(8,128)(2,1)S(1)} %collective-permute-done.4.refs_0_, bf16[111,16,128]{2,1,0:T(8,128)(2,1)S(1)} %collective-permute-done.7.refs_1_, bf16[111,16,128]{2,1,0:T(8,128)(2,1)S(1)} %collective-permute-done.9.refs_2_, ...), custom_call_target="tpu_custom_call", output_to_operand_aliasing={{}: (9, {})} | custom-call | flops 20000000000 | bytes 1000 | tf_op jit(solution)/shard_map/turn/pallas_call | solution.py:339
  (53 shorter events, 6.9 us)
Async XLA Ops:
  0.6 12.3 %collective-permute-start.1 = (bf16[64,1024]{1,0:T(8,128)(2,1)}, bf16[64,1024]{1,0:T(8,128)(2,1)S(1)}, u32[]{:S(2)}, u32[]{:S(2)}) collective-permute-start(bf16[64,1024]{1,0:T(8,128)(2,1)} %refs_3_), channel_id=1, source_target_pairs={{0,16},{2,18},{4,20},{6,22},{8,24},{10,26},{12,28},{14,30},{16,0},... | collective-permute-start | bytes 393224 | tf_op jit(solution)/shard_map/ppermute | solution.py:381
  0.7 12.2 %collective-permute-start = (bf16[64,1024]{1,0:T(8,128)(2,1)}, bf16[64,1024]{1,0:T(8,128)(2,1)S(1)}, u32[]{:S(2)}, u32[]{:S(2)}) collective-permute-start(bf16[64,1024]{1,0:T(8,128)(2,1)} %refs_3_), channel_id=1, source_target_pairs={{0,8},{2,10},{4,12},{6,14},{8,0},{10,2},{12,4},{14,6},{16,24},{18,... | collective-permute-start | bytes 393224 | tf_op jit(solution)/shard_map/ppermute | solution.py:381
  2.1 13.6 %collective-permute-start.2 = (bf16[64,1024]{1,0:T(8,128)(2,1)}, bf16[64,1024]{1,0:T(8,128)(2,1)S(1)}, u32[]{:S(2)}, u32[]{:S(2)}) collective-permute-start(bf16[64,1024]{1,0:T(8,128)(2,1)} %refs_3_), channel_id=1, source_target_pairs={{0,24},{2,26},{4,28},{6,30},{8,16},{10,18},{12,20},{14,22},{16,8},... | collective-permute-start | bytes 393224 | tf_op jit(solution)/shard_map/ppermute | solution.py:381
  3.3 12.3 %copy-start.2 = (f32[2,111,1024]{2,0,1:T(2,128)S(1)}, f32[2,111,1024]{2,0,1:T(2,128)}, u32[]{:S(2)}) copy-start(f32[2,111,1024]{2,0,1:T(2,128)} %param.9) | copy-start | bytes 2727940
  3.3 12.3 %copy-start.3 = (bf16[64,1024]{1,0:T(8,128)(2,1)S(1)}, bf16[64,1024]{1,0:T(8,128)(2,1)}, u32[]{:S(2)}) copy-start(bf16[64,1024]{1,0:T(8,128)(2,1)} %refs_3_) | copy-start | bytes 393220
  22.5 3.6 %collective-permute-start.3 = (bf16[256,1024]{1,0:T(8,128)(2,1)S(1)}, bf16[256,1024]{1,0:T(8,128)(2,1)S(1)}, u32[]{:S(2)}, u32[]{:S(2)}) collective-permute-start(bf16[256,1024]{1,0:T(8,128)(2,1)S(1)} %get-tuple-element.70), channel_id=1, source_target_pairs={{0,2},{2,0},{4,6},{6,4},{8,10},{10,8},{12,14},{14,12},{16,18},{18,... | collective-permute-start | bytes 1572872 | tf_op jit(solution)/shard_map/ppermute | solution.py:381
  23.0 14.5 %collective-permute-start.6 = (bf16[256,1024]{1,0:T(8,128)(2,1)S(1)}, bf16[256,1024]{1,0:T(8,128)(2,1)S(1)}, u32[]{:S(2)}, u32[]{:S(2)}) collective-permute-start(bf16[256,1024]{1,0:T(8,128)(2,1)S(1)} %get-tuple-element.70), channel_id=1, source_target_pairs={{0,6},{2,4},{4,2},{6,0},{8,14},{10,12},{12,10},{14,8},{16,22},{18,... | collective-permute-start | bytes 1572872 | tf_op jit(solution)/shard_map/ppermute | solution.py:381
  24.1 23.4 %collective-permute-start.5 = (bf16[256,1024]{1,0:T(8,128)(2,1)S(1)}, bf16[256,1024]{1,0:T(8,128)(2,1)S(1)}, u32[]{:S(2)}, u32[]{:S(2)}) collective-permute-start(bf16[256,1024]{1,0:T(8,128)(2,1)S(1)} %get-tuple-element.70), channel_id=1, source_target_pairs={{0,4},{2,6},{4,0},{6,2},{8,12},{10,14},{12,8},{14,10},{16,20},{18,... | collective-permute-start | bytes 1572872 | tf_op jit(solution)/shard_map/ppermute | solution.py:381
  24.4 35.3 %collective-permute-start.4 = (bf16[111,16,128]{2,1,0:T(8,128)(2,1)}, bf16[111,16,128]{2,1,0:T(8,128)(2,1)S(1)}, u32[]{:S(2)}, u32[]{:S(2)}) collective-permute-start(bf16[111,16,128]{2,1,0:T(8,128)(2,1)} %get-tuple-element.73.refs_0_), channel_id=1, source_target_pairs={{0,16},{2,18},{4,20},{6,22},{8,24},{10,26},{12,28},{14,30},{16,0},... | collective-permute-start | bytes 1363976 | tf_op jit(solution)/shard_map/ppermute | solution.py:381
  24.4 41.5 %collective-permute-start.8 = (bf16[111,16,128]{2,1,0:T(8,128)(2,1)}, bf16[111,16,128]{2,1,0:T(8,128)(2,1)S(1)}, u32[]{:S(2)}, u32[]{:S(2)}) collective-permute-start(bf16[111,16,128]{2,1,0:T(8,128)(2,1)} %get-tuple-element.85.refs_1_), channel_id=1, source_target_pairs={{0,24},{2,26},{4,28},{6,30},{8,16},{10,18},{12,20},{14,22},{16,8},... | collective-permute-start | bytes 1363976 | tf_op jit(solution)/shard_map/ppermute | solution.py:381
  26.1 1.9 copy-start.7
  26.1 30.5 %collective-permute-start.14 = (bf16[111,16,128]{2,1,0:T(8,128)(2,1)}, bf16[111,16,128]{2,1,0:T(8,128)(2,1)S(1)}, u32[]{:S(2)}, u32[]{:S(2)}) collective-permute-start(bf16[111,16,128]{2,1,0:T(8,128)(2,1)} %get-tuple-element.95.refs_2_), channel_id=1, source_target_pairs={{0,8},{2,10},{4,12},{6,14},{8,0},{10,2},{12,4},{14,6},{16,24},{18,... | collective-permute-start | bytes 1363976 | tf_op jit(solution)/shard_map/ppermute | solution.py:381
  37.5 10.1 %copy-start.5 = (bf16[256,1024]{1,0:T(8,128)(2,1)}, bf16[256,1024]{1,0:T(8,128)(2,1)S(1)}, u32[]{:S(2)}) copy-start(bf16[256,1024]{1,0:T(8,128)(2,1)S(1)} %collective-permute-done.6.refs_1_) | copy-start | bytes 1572868
  48.3 8.2 %copy-start.11 = (bf16[111,16,128]{2,1,0:T(8,128)(2,1)S(1)}, bf16[111,16,128]{2,1,0:T(8,128)(2,1)}, u32[]{:S(2)}) copy-start(bf16[111,16,128]{2,1,0:T(8,128)(2,1)} %get-tuple-element.111.refs_7_) | copy-start | bytes 1363972
  48.3 9.3 %copy-start.10 = (bf16[111,16,128]{2,1,0:T(8,128)(2,1)S(1)}, bf16[111,16,128]{2,1,0:T(8,128)(2,1)}, u32[]{:S(2)}) copy-start(bf16[111,16,128]{2,1,0:T(8,128)(2,1)} %get-tuple-element.117.refs_6_) | copy-start | bytes 1363972
  48.4 17.5 %copy-start.9 = (bf16[111,16,128]{2,1,0:T(8,128)(2,1)S(1)}, bf16[111,16,128]{2,1,0:T(8,128)(2,1)}, u32[]{:S(2)}) copy-start(bf16[111,16,128]{2,1,0:T(8,128)(2,1)} %get-tuple-element.90.refs_5_) | copy-start | bytes 1363972
  56.6 9.3 %copy-start.8 = (bf16[111,16,128]{2,1,0:T(8,128)(2,1)}, bf16[111,16,128]{2,1,0:T(8,128)(2,1)S(1)}, u32[]{:S(2)}) copy-start(bf16[111,16,128]{2,1,0:T(8,128)(2,1)S(1)} %collective-permute-done.14.refs_4_) | copy-start | bytes 1363972
  56.6 14.0 %collective-permute-start.15 = (bf16[111,16,128]{2,1,0:T(8,128)(2,1)S(1)}, bf16[111,16,128]{2,1,0:T(8,128)(2,1)}, u32[]{:S(2)}, u32[]{:S(2)}) collective-permute-start(bf16[111,16,128]{2,1,0:T(8,128)(2,1)S(1)} %copy-done.11), channel_id=1, source_target_pairs={{0,2},{2,0},{4,6},{6,4},{8,10},{10,8},{12,14},{14,12},{16,18},{18,... | collective-permute-start | bytes 1363976 | tf_op jit(solution)/shard_map/ppermute | solution.py:381
  57.7 14.8 %collective-permute-start.18 = (bf16[111,16,128]{2,1,0:T(8,128)(2,1)S(1)}, bf16[111,16,128]{2,1,0:T(8,128)(2,1)}, u32[]{:S(2)}, u32[]{:S(2)}) collective-permute-start(bf16[111,16,128]{2,1,0:T(8,128)(2,1)S(1)} %copy-done.10), channel_id=1, source_target_pairs={{0,10},{2,8},{4,14},{6,12},{8,2},{10,0},{12,6},{14,4},{16,26},{18,... | collective-permute-start | bytes 1363976 | tf_op jit(solution)/shard_map/ppermute | solution.py:381
  65.9 53.0 %collective-permute-start.9 = (bf16[111,16,128]{2,1,0:T(8,128)(2,1)}, bf16[111,16,128]{2,1,0:T(8,128)(2,1)S(1)}, u32[]{:S(2)}, u32[]{:S(2)}) collective-permute-start(bf16[111,16,128]{2,1,0:T(8,128)(2,1)} %get-tuple-element.87.refs_8_), channel_id=1, source_target_pairs={{0,20},{2,22},{4,16},{6,18},{8,28},{10,30},{12,24},{14,26},{16,4},... | collective-permute-start | bytes 1363976 | tf_op jit(solution)/shard_map/ppermute | solution.py:381
  65.9 54.5 %collective-permute-start.10 = (bf16[111,16,128]{2,1,0:T(8,128)(2,1)S(1)}, bf16[111,16,128]{2,1,0:T(8,128)(2,1)S(1)}, u32[]{:S(2)}, u32[]{:S(2)}) collective-permute-start(bf16[111,16,128]{2,1,0:T(8,128)(2,1)S(1)} %copy-done.9), channel_id=1, source_target_pairs={{0,26},{2,24},{4,30},{6,28},{8,18},{10,16},{12,22},{14,20},{16,10}... | collective-permute-start | bytes 1363976 | tf_op jit(solution)/shard_map/ppermute | solution.py:381
  66.7 59.4 %collective-permute-start.7 = (bf16[111,16,128]{2,1,0:T(8,128)(2,1)}, bf16[111,16,128]{2,1,0:T(8,128)(2,1)S(1)}, u32[]{:S(2)}, u32[]{:S(2)}) collective-permute-start(bf16[111,16,128]{2,1,0:T(8,128)(2,1)} %get-tuple-element.80.refs_4_), channel_id=1, source_target_pairs={{0,18},{2,16},{4,22},{6,20},{8,26},{10,24},{12,30},{14,28},{16,2},... | collective-permute-start | bytes 1363976 | tf_op jit(solution)/shard_map/ppermute | solution.py:381
  70.6 34.8 %collective-permute-start.16 = (bf16[111,16,128]{2,1,0:T(8,128)(2,1)}, bf16[111,16,128]{2,1,0:T(8,128)(2,1)}, u32[]{:S(2)}, u32[]{:S(2)}) collective-permute-start(bf16[111,16,128]{2,1,0:T(8,128)(2,1)} %get-tuple-element.113.refs_11_), channel_id=1, source_target_pairs={{0,4},{2,6},{4,0},{6,2},{8,12},{10,14},{12,8},{14,10},{16,20},{18,... | collective-permute-start | bytes 1363976 | tf_op jit(solution)/shard_map/ppermute | solution.py:381
  72.5 38.1 %collective-permute-start.19 = (bf16[111,16,128]{2,1,0:T(8,128)(2,1)}, bf16[111,16,128]{2,1,0:T(8,128)(2,1)}, u32[]{:S(2)}, u32[]{:S(2)}) collective-permute-start(bf16[111,16,128]{2,1,0:T(8,128)(2,1)} %get-tuple-element.119.refs_10_), channel_id=1, source_target_pairs={{0,12},{2,14},{4,8},{6,10},{8,4},{10,6},{12,0},{14,2},{16,28},{18,... | collective-permute-start | bytes 1363976 | tf_op jit(solution)/shard_map/ppermute | solution.py:381
  105.3 50.0 %collective-permute-start.17 = (bf16[111,16,128]{2,1,0:T(8,128)(2,1)}, bf16[111,16,128]{2,1,0:T(8,128)(2,1)}, u32[]{:S(2)}, u32[]{:S(2)}) collective-permute-start(bf16[111,16,128]{2,1,0:T(8,128)(2,1)} %get-tuple-element.115.refs_15_), channel_id=1, source_target_pairs={{0,6},{2,4},{4,2},{6,0},{8,14},{10,12},{12,10},{14,8},{16,22},{18,... | collective-permute-start | bytes 1363976 | tf_op jit(solution)/shard_map/ppermute | solution.py:381
  110.6 44.7 %collective-permute-start.20 = (bf16[111,16,128]{2,1,0:T(8,128)(2,1)}, bf16[111,16,128]{2,1,0:T(8,128)(2,1)}, u32[]{:S(2)}, u32[]{:S(2)}) collective-permute-start(bf16[111,16,128]{2,1,0:T(8,128)(2,1)} %get-tuple-element.121.refs_14_), channel_id=1, source_target_pairs={{0,14},{2,12},{4,10},{6,8},{8,6},{10,4},{12,2},{14,0},{16,30},{18,... | collective-permute-start | bytes 1363976 | tf_op jit(solution)/shard_map/ppermute | solution.py:381
  112.2 38.3 %all-to-all-start = ((f32[16,17,128]{2,1,0:T(8,128)}), f32[16,17,128]{2,1,0:T(8,128)S(1)}, u32[]{:S(2)}, u32[]{:S(2)}) async-start(f32[16,17,128]{2,1,0:T(8,128)} %pad_maximum_fusion), calls=%async_computation | async-start | bytes 393216 | tf_op jit(solution)/shard_map/all_to_all | solution.py:362
  118.9 51.9 %collective-permute-start.13 = (bf16[111,16,128]{2,1,0:T(8,128)(2,1)}, bf16[111,16,128]{2,1,0:T(8,128)(2,1)S(1)}, u32[]{:S(2)}, u32[]{:S(2)}) collective-permute-start(bf16[111,16,128]{2,1,0:T(8,128)(2,1)} %get-tuple-element.109.refs_13_), channel_id=1, source_target_pairs={{0,30},{2,28},{4,26},{6,24},{8,22},{10,20},{12,18},{14,16},{16,14}... | collective-permute-start | bytes 1363976 | tf_op jit(solution)/shard_map/ppermute | solution.py:381
  120.4 56.7 %collective-permute-start.11 = (bf16[111,16,128]{2,1,0:T(8,128)(2,1)}, bf16[111,16,128]{2,1,0:T(8,128)(2,1)S(1)}, u32[]{:S(2)}, u32[]{:S(2)}) collective-permute-start(bf16[111,16,128]{2,1,0:T(8,128)(2,1)} %get-tuple-element.91.refs_12_), channel_id=1, source_target_pairs={{0,22},{2,20},{4,18},{6,16},{8,30},{10,28},{12,26},{14,24},{16,6},... | collective-permute-start | bytes 1363976 | tf_op jit(solution)/shard_map/ppermute | solution.py:381
  152.2 36.8 %copy-start = (f32[256,128]{0,1:T(8,128)}, f32[256,128]{0,1:T(8,128)S(1)}, u32[]{:S(2)}) copy-start(f32[256,128]{0,1:T(8,128)S(1)} %copy.15) | copy-start | bytes 393220
  152.4 36.5 %copy-start.1 = (f32[2,4,256]{2,1,0:T(4,128)}, f32[2,4,256]{2,1,0:T(4,128)S(1)}, u32[]{:S(2)}) copy-start(f32[2,4,256]{2,1,0:T(4,128)S(1)} %reshape.37.refs_10_) | copy-start | bytes 24580
  152.4 36.5 %collective-permute-start.12 = (bf16[111,16,128]{2,1,0:T(8,128)(2,1)}, bf16[111,16,128]{2,1,0:T(8,128)(2,1)S(1)}, u32[]{:S(2)}, u32[]{:S(2)}) collective-permute-start(bf16[111,16,128]{2,1,0:T(8,128)(2,1)} %get-tuple-element.108.refs_9_), channel_id=1, source_target_pairs={{0,28},{2,30},{4,24},{6,26},{8,20},{10,22},{12,16},{14,18},{16,12}... | collective-permute-start | bytes 1363976 | tf_op jit(solution)/shard_map/ppermute | solution.py:381
  (2 other events, 1.5 us)
